TPU v7x, 32 devices: a whole 2x2x4 slice. The times are simulated.
32 devices in a mesh: row: 8 (over y, x, core), col: 4 (over z).
Axes of the slice: x: 2, y: 2, z: 4, core: 2. Of those that a mesh axis runs over, the one named last changes fastest.
Arguments:
- tokens: bfloat16 [8192, 2048], P('row', 'col'), may hold values from -6 to 6
- norm_attn: bfloat16 [2048], P('col'), may hold values from 0.099609375 to 1.8984375
- norm_query: bfloat16 [2048], P('col'), may hold values from 0.099609375 to 1.8984375
- norm_key: bfloat16 [2048], P('col'), may hold values from 0.099609375 to 1.8984375
- norm_moe: bfloat16 [2048], P('col'), may hold values from 0.099609375 to 1.8984375
- w_query: bfloat16 [2048, 2048], P('row', 'col'), may hold values from -0.125 to 0.125
- w_key: bfloat16 [2048, 2048], P('row', 'col'), may hold values from -0.125 to 0.125
- w_value: bfloat16 [2048, 2048], P('row', 'col'), may hold values from -0.125 to 0.125
- w_out: bfloat16 [2048, 2048], P('row', 'col'), may hold values from -1.5 to 1.5
- w_router: bfloat16 [2048, 16], P('row', 'col'), may hold values from -0.0625 to 0.0625
- w_gate: bfloat16 [2048, 16, 1024], P('row', None, 'col'), may hold values from -0.125 to 0.125
- w_up: bfloat16 [2048, 16, 1024], P('row', None, 'col'), may hold values from -0.125 to 0.125
- w_down: bfloat16 [2048, 16, 1024], P('row', None, 'col'), may hold values from -0.5 to 0.5
- routes: int32 [8192, 8], P('row'), may hold values from 0 to 15, all different within a row; in each aligned block of 1024 rows (0 to 1023, 1024 to 2047, ...) at most 640 rows name the same one
- span_starts: int32 [8, 2], P('row'), may hold values from 0 to 768, as said below
- cotangent: bfloat16 [8192, 2048], P('row', 'col'), may hold values from -6 to 6
Outputs:
- output: bfloat16 [8192, 2048], P('row', 'col')
- d_tokens: float32 [8192, 2048], P('row', 'col')
- d_norm_attn: float32 [2048], P('col')
- d_norm_query: float32 [2048], P('col')
- d_norm_key: float32 [2048], P('col')
- d_norm_moe: float32 [2048], P('col')
- d_w_query: float32 [2048, 2048], P('row', 'col')
- d_w_key: float32 [2048, 2048], P('row', 'col')
- d_w_value: float32 [2048, 2048], P('row', 'col')
- d_w_out: float32 [2048, 2048], P('row', 'col')
- d_w_router: float32 [2048, 16], P('row', 'col')
- d_w_gate: float32 [2048, 16, 1024], P('row', None, 'col')
- d_w_up: float32 [2048, 16, 1024], P('row', None, 'col')
- d_w_down: float32 [2048, 16, 1024], P('row', None, 'col')
Inputs may be any that keep to these rules, and one draw needn't show every extreme that they name: `routes`: each row names 8 different experts; among the 1024 rows of one sequence no expert is named more than 640 times. `span_starts`: span k of a sequence (k from 0) starts between k * 2 * 256 and k * 2 * 256 + 256; the spans of a sequence are disjoint and lie within it.
All inputs are finite; a program needn't handle non-finite values.
Results may differ from a plain program's by a relative error of at most 0.014.
The roundings to bfloat16 on the way count: a program that leaves them out, or rounds other values in their place, can miss the bound.
Values may be sent and summed in bfloat16 or wider, within the bound.
A program may use at most 384 MiB of HBM per device.

v0:
```python
import math

import jax
import jax.numpy as jnp
from jax import lax
from jax.sharding import PartitionSpec as P

HD = 128
IMG = 256
CAP = 640


EPSILON = 1e-05
ROPE_BASE = 10000.0
MASKED = -1e30


def rope_tables(length, head_size):
    half_size = head_size // 2
    places = jnp.arange(length, dtype=jnp.float32)
    rates = jnp.exp(-math.log(ROPE_BASE) * jnp.arange(half_size, dtype=jnp.float32) / half_size)
    angles = places[:, None] * rates[None, :]
    return (jnp.cos(angles), jnp.sin(angles))


def rotate(values, cosine, sine, direction):
    half_size = values.shape[-1] // 2
    first_half = values[..., :half_size]
    second_half = values[..., half_size:]
    cos_part = cosine[:, None, :]
    sin_part = direction * sine[:, None, :]
    return jnp.concatenate(
        [
            first_half * cos_part - second_half * sin_part,
            second_half * cos_part + first_half * sin_part,
        ],
        axis=-1,
    )


def span_ids(starts, length):
    places = jnp.arange(length, dtype=jnp.int32)
    inside = (places[None, :] >= starts[:, None]) & (places[None, :] < starts[:, None] + IMG)
    numbers = jnp.arange(1, starts.shape[0] + 1, dtype=jnp.int32)
    return jnp.sum(jnp.where(inside, numbers[:, None], 0), axis=0)


def masked_scores(query_block, key_heads, first_row, span_of, scale):
    scores = (
        jnp.einsum("bhd,khd->hbk", query_block, key_heads, preferred_element_type=jnp.float32)
        * scale
    )
    block_rows = query_block.shape[0]
    row_places = first_row + jnp.arange(block_rows, dtype=jnp.int32)
    key_places = jnp.arange(key_heads.shape[0], dtype=jnp.int32)
    row_spans = lax.dynamic_slice_in_dim(span_of, first_row, block_rows)
    allowed = (key_places[None, :] <= row_places[:, None]) | (
        row_spans[:, None] == span_of[None, :]
    ) & (row_spans[:, None] > 0)
    return jnp.where(allowed[None], scores, MASKED)


def sum_features(terms):
    return lax.psum_scatter(terms, "col", scatter_dimension=1, tiled=True)


def spread_grad(values):
    return lax.all_gather(values, "col", axis=1, tiled=True)


def sum_with_stat(terms, local_stat):
    copies = jnp.broadcast_to(local_stat[:, None], (local_stat.shape[0], lax.axis_size("col")))
    return (
        lax.psum_scatter(terms, "col", scatter_dimension=1, tiled=True),
        lax.psum_scatter(copies, "col", scatter_dimension=1, tiled=True),
    )


def shards(
    tokens,
    norm_attn,
    norm_query,
    norm_key,
    norm_moe,
    w_query,
    w_key,
    w_value,
    w_out,
    w_router,
    w_gate,
    w_up,
    w_down,
    routes,
    span_starts,
    cotangent,
):
    rows_here, feature_part = tokens.shape
    width = feature_part * lax.axis_size("col")
    heads_here = feature_part // HD
    experts = w_gate.shape[1]
    scale = 1.0 / math.sqrt(HD)
    whole_tokens, whole_attn_gain, whole_moe_gain = (
        lax.all_gather(tokens, "col", axis=1, tiled=True),
        lax.all_gather(norm_attn.reshape(1, feature_part), "col", axis=1, tiled=True),
        lax.all_gather(norm_moe.reshape(1, feature_part), "col", axis=1, tiled=True),
    )
    full_query, full_key, full_value, full_out, full_router, full_gate, full_up, full_down = (
        lax.all_gather(w_query, "row", axis=0, tiled=True),
        lax.all_gather(w_key, "row", axis=0, tiled=True),
        lax.all_gather(w_value, "row", axis=0, tiled=True),
        lax.all_gather(w_out, "row", axis=0, tiled=True),
        lax.all_gather(w_router, "row", axis=0, tiled=True),
        lax.all_gather(w_gate, "row", axis=0, tiled=True),
        lax.all_gather(w_up, "row", axis=0, tiled=True),
        lax.all_gather(w_down, "row", axis=0, tiled=True),
    )
    token_values = whole_tokens.astype(jnp.float32)
    attn_gain = whole_attn_gain.astype(jnp.float32)
    inv_first = lax.rsqrt(jnp.mean(token_values * token_values, axis=1, keepdims=True) + EPSILON)
    normed_attn = (token_values * inv_first * attn_gain).astype(jnp.bfloat16)
    query_raw = jnp.dot(normed_attn, full_query, preferred_element_type=jnp.float32)
    key_raw = jnp.dot(normed_attn, full_key, preferred_element_type=jnp.float32)
    value_low = jnp.dot(normed_attn, full_value, preferred_element_type=jnp.float32).astype(
        jnp.bfloat16
    )
    query_square, key_square = lax.psum(
        (jnp.sum(query_raw * query_raw, axis=1), jnp.sum(key_raw * key_raw, axis=1)), "col"
    )
    query_inv = lax.rsqrt(query_square[:, None] / width + EPSILON)
    key_inv = lax.rsqrt(key_square[:, None] / width + EPSILON)
    query_gain = norm_query.astype(jnp.float32)
    key_gain = norm_key.astype(jnp.float32)
    cosine, sine = rope_tables(rows_here, HD)
    query_heads = rotate(
        (query_raw * query_inv * query_gain).reshape(rows_here, heads_here, HD), cosine, sine, 1.0
    ).astype(jnp.bfloat16)
    key_heads = rotate(
        (key_raw * key_inv * key_gain).reshape(rows_here, heads_here, HD), cosine, sine, 1.0
    ).astype(jnp.bfloat16)
    value_heads = value_low.reshape(rows_here, heads_here, HD)
    span_of = span_ids(span_starts[0], rows_here)
    block_rows = min(512, rows_here)
    block_count = rows_here // block_rows
    first_rows = jnp.arange(block_count, dtype=jnp.int32) * block_rows
    query_blocks = query_heads.reshape(block_count, block_rows, heads_here, HD)

    def attend_block(packed):
        query_block, first_row = packed
        scores = masked_scores(query_block, key_heads, first_row, span_of, scale)
        top_score = jnp.max(scores, axis=2, keepdims=True)
        raised = jnp.exp(scores - top_score)
        totals = jnp.sum(raised, axis=2, keepdims=True)
        probs = (raised / totals).astype(jnp.bfloat16)
        mixed_block = jnp.einsum(
            "hbk,khd->bhd", probs, value_heads, preferred_element_type=jnp.float32
        )
        return (mixed_block.astype(jnp.bfloat16), (top_score + jnp.log(totals))[..., 0])

    mixed_blocks, log_totals = lax.map(attend_block, (query_blocks, first_rows))
    mixed = mixed_blocks.reshape(rows_here, feature_part)
    attn = sum_features(
        jnp.einsum("tj,dj->td", mixed, full_out, preferred_element_type=jnp.float32)
    )
    local_tokens = tokens.astype(jnp.float32)
    hidden_state = local_tokens + attn
    hidden_full = lax.all_gather(hidden_state, "col", axis=1, tiled=True)
    moe_gain = whole_moe_gain.astype(jnp.float32)
    inv_second = lax.rsqrt(jnp.mean(hidden_full * hidden_full, axis=1, keepdims=True) + EPSILON)
    normed_moe = (hidden_full * inv_second * moe_gain).astype(jnp.bfloat16)
    logit_part = jnp.dot(normed_moe, full_router, preferred_element_type=jnp.float32)
    logits = lax.all_gather(logit_part, "col", axis=1, tiled=True)
    router_probs = jax.nn.softmax(logits, axis=1)
    expert_ids = jnp.arange(experts, dtype=jnp.int32)
    routed = jnp.any(routes[:, :, None] == expert_ids[None, None, :], axis=1)
    gate_table = jnp.where(routed, router_probs, 0.0)
    slots = jnp.cumsum(routed.astype(jnp.int32), axis=0) - 1
    slots = jnp.where(routed, slots, CAP)
    token_ids = jnp.broadcast_to(
        jnp.arange(rows_here, dtype=jnp.int32)[:, None], (rows_here, experts)
    )
    expert_grid = jnp.broadcast_to(expert_ids[None, :], (rows_here, experts))
    table = (
        jnp.full((experts, CAP + 1), rows_here, jnp.int32)
        .at[expert_grid, slots]
        .set(token_ids)[:, :CAP]
    )
    padded_rows = jnp.concatenate([normed_moe, jnp.zeros((1, width), jnp.bfloat16)], axis=0)
    padded_gates = jnp.concatenate([gate_table, jnp.zeros((1, experts), jnp.float32)], axis=0)

    def expert_forward(total, expert):
        slot_tokens = lax.dynamic_index_in_dim(table, expert, 0, keepdims=False)
        chosen = padded_rows[slot_tokens]
        weight_column = lax.dynamic_index_in_dim(padded_gates, expert, 1, keepdims=False)[
            slot_tokens
        ]
        gate_pre = jnp.dot(
            chosen,
            lax.dynamic_index_in_dim(full_gate, expert, 1, keepdims=False),
            preferred_element_type=jnp.float32,
        )
        up_pre = jnp.dot(
            chosen,
            lax.dynamic_index_in_dim(full_up, expert, 1, keepdims=False),
            preferred_element_type=jnp.float32,
        )
        hidden = (weight_column[:, None] * jax.nn.silu(gate_pre) * up_pre).astype(jnp.bfloat16)
        expert_out = jnp.einsum(
            "cf,df->cd",
            hidden,
            lax.dynamic_index_in_dim(full_down, expert, 1, keepdims=False),
            preferred_element_type=jnp.float32,
        )
        return (total.at[slot_tokens].add(expert_out), (gate_pre, up_pre, hidden))

    moe_totals, kept = lax.scan(
        expert_forward, jnp.zeros((rows_here + 1, width), jnp.float32), expert_ids
    )
    moe = sum_features(moe_totals[:rows_here])
    output = (hidden_state + moe).astype(jnp.bfloat16)
    full_query, full_key, full_value, full_out, full_router, full_gate, full_up, full_down = (
        lax.all_gather(w_query, "row", axis=0, tiled=True),
        lax.all_gather(w_key, "row", axis=0, tiled=True),
        lax.all_gather(w_value, "row", axis=0, tiled=True),
        lax.all_gather(w_out, "row", axis=0, tiled=True),
        lax.all_gather(w_router, "row", axis=0, tiled=True),
        lax.all_gather(w_gate, "row", axis=0, tiled=True),
        lax.all_gather(w_up, "row", axis=0, tiled=True),
        lax.all_gather(w_down, "row", axis=0, tiled=True),
    )
    grad_full = spread_grad(cotangent)
    padded_grad = jnp.concatenate([grad_full, jnp.zeros((1, width), jnp.bfloat16)], axis=0)
    kept_gate, kept_up, kept_hidden = kept

    def expert_backward(input_acc, packed):
        expert, gate_pre, up_pre = packed
        slot_tokens = lax.dynamic_index_in_dim(table, expert, 0, keepdims=False)
        grad_rows = padded_grad[slot_tokens]
        weight_column = lax.dynamic_index_in_dim(padded_gates, expert, 1, keepdims=False)[
            slot_tokens
        ]
        gate_mat = lax.dynamic_index_in_dim(full_gate, expert, 1, keepdims=False)
        up_mat = lax.dynamic_index_in_dim(full_up, expert, 1, keepdims=False)
        down_mat = lax.dynamic_index_in_dim(full_down, expert, 1, keepdims=False)
        hidden_grad = jnp.dot(grad_rows, down_mat, preferred_element_type=jnp.float32)
        sigmoid_gate = jax.nn.sigmoid(gate_pre)
        silu_gate = gate_pre * sigmoid_gate
        weight_grad = jnp.sum(hidden_grad * silu_gate * up_pre, axis=1)
        act_grad = hidden_grad * weight_column[:, None]
        gate_grad = (
            act_grad * up_pre * (sigmoid_gate * (1.0 + gate_pre * (1.0 - sigmoid_gate)))
        ).astype(jnp.bfloat16)
        up_grad = (act_grad * silu_gate).astype(jnp.bfloat16)
        input_rows = jnp.einsum(
            "cf,df->cd", gate_grad, gate_mat, preferred_element_type=jnp.float32
        ) + jnp.einsum("cf,df->cd", up_grad, up_mat, preferred_element_type=jnp.float32)
        input_acc = input_acc.at[slot_tokens].add(input_rows)
        return (input_acc, (weight_grad, gate_grad, up_grad))

    input_acc, stacked = lax.scan(
        expert_backward,
        jnp.zeros((rows_here + 1, width), jnp.float32),
        (expert_ids, kept_gate, kept_up),
    )
    slot_weight_grads, stacked_gate_grad, stacked_up_grad = stacked
    gate_acc = (
        jnp.zeros((rows_here + 1, experts), jnp.float32)
        .at[table, expert_ids[:, None]]
        .add(slot_weight_grads)
    )
    chosen_all = padded_rows[table]
    grad_all = padded_grad[table]
    d_gate_w = jnp.einsum(
        "ecd,ecf->def", chosen_all, stacked_gate_grad, preferred_element_type=jnp.float32
    )
    d_up_w = jnp.einsum(
        "ecd,ecf->def", chosen_all, stacked_up_grad, preferred_element_type=jnp.float32
    )
    d_down_w = jnp.einsum("ecd,ecf->def", grad_all, kept_hidden, preferred_element_type=jnp.float32)
    gate_table_grad = lax.psum(gate_acc[:rows_here], "col")
    logit_grad = router_probs * (
        gate_table_grad - jnp.sum(router_probs * gate_table_grad, axis=1, keepdims=True)
    )
    logit_low = logit_grad.astype(jnp.bfloat16)
    router_cols = full_router.shape[1]
    logit_local = lax.dynamic_slice_in_dim(
        logit_low, lax.axis_index("col") * router_cols, router_cols, 1
    )
    normed_moe_grad = input_acc[:rows_here] + jnp.einsum(
        "te,de->td", logit_local, full_router, preferred_element_type=jnp.float32
    )
    d_router_w = jnp.einsum(
        "td,te->de", normed_moe, logit_local, preferred_element_type=jnp.float32
    )
    moe_stat = jnp.sum(normed_moe_grad * moe_gain * hidden_full, axis=1)
    moe_in_grad, moe_stat_total = sum_with_stat(normed_moe_grad, moe_stat)
    local_moe_gain = norm_moe.astype(jnp.float32)
    d_moe_gain = jnp.sum(moe_in_grad * hidden_state * inv_second, axis=0)
    hidden_grad_total = (
        cotangent.astype(jnp.float32)
        + inv_second * local_moe_gain * moe_in_grad
        - inv_second**3 * hidden_state * moe_stat_total / width
    )
    attn_grad_full = spread_grad(hidden_grad_total.astype(jnp.bfloat16))
    mixed_grad = jnp.dot(attn_grad_full, full_out, preferred_element_type=jnp.float32).astype(
        jnp.bfloat16
    )
    d_out_w = jnp.einsum("td,tj->dj", attn_grad_full, mixed, preferred_element_type=jnp.float32)
    mixed_grad_blocks = mixed_grad.reshape(block_count, block_rows, heads_here, HD)

    def attend_back(carry, packed):
        key_grad, value_grad = carry
        query_block, grad_block, log_total, first_row = packed
        scores = masked_scores(query_block, key_heads, first_row, span_of, scale)
        probs = jnp.exp(scores - log_total[..., None])
        prob_grad = jnp.einsum(
            "bhd,khd->hbk", grad_block, value_heads, preferred_element_type=jnp.float32
        )
        score_grad = (
            probs * (prob_grad - jnp.sum(probs * prob_grad, axis=2, keepdims=True))
        ).astype(jnp.bfloat16)
        query_grad = (
            jnp.einsum("hbk,khd->bhd", score_grad, key_heads, preferred_element_type=jnp.float32)
            * scale
        )
        key_grad = (
            key_grad
            + jnp.einsum(
                "hbk,bhd->khd", score_grad, query_block, preferred_element_type=jnp.float32
            )
            * scale
        )
        value_grad = value_grad + jnp.einsum(
            "hbk,bhd->khd",
            probs.astype(jnp.bfloat16),
            grad_block,
            preferred_element_type=jnp.float32,
        )
        return ((key_grad, value_grad), query_grad)

    head_zeros = jnp.zeros((rows_here, heads_here, HD), jnp.float32)
    (key_grad_sum, value_grad_sum), query_grad_blocks = lax.scan(
        attend_back,
        (head_zeros, head_zeros),
        (query_blocks, mixed_grad_blocks, log_totals, first_rows),
    )
    query_turned = rotate(
        query_grad_blocks.reshape(rows_here, heads_here, HD), cosine, sine, -1.0
    ).reshape(rows_here, feature_part)
    key_turned = rotate(key_grad_sum, cosine, sine, -1.0).reshape(rows_here, feature_part)
    query_scaled = query_turned * query_gain
    key_scaled = key_turned * key_gain
    query_stat, key_stat = lax.psum(
        (jnp.sum(query_scaled * query_raw, axis=1), jnp.sum(key_scaled * key_raw, axis=1)), "col"
    )
    d_query_gain = jnp.sum(query_turned * query_raw * query_inv, axis=0)
    d_key_gain = jnp.sum(key_turned * key_raw * key_inv, axis=0)
    query_raw_grad = (
        query_inv * query_scaled - query_inv**3 * query_raw * query_stat[:, None] / width
    ).astype(jnp.bfloat16)
    key_raw_grad = (
        key_inv * key_scaled - key_inv**3 * key_raw * key_stat[:, None] / width
    ).astype(jnp.bfloat16)
    value_raw_grad = value_grad_sum.reshape(rows_here, feature_part).astype(jnp.bfloat16)
    d_query_w = jnp.einsum(
        "td,tj->dj", normed_attn, query_raw_grad, preferred_element_type=jnp.float32
    )
    d_key_w = jnp.einsum("td,tj->dj", normed_attn, key_raw_grad, preferred_element_type=jnp.float32)
    d_value_w = jnp.einsum(
        "td,tj->dj", normed_attn, value_raw_grad, preferred_element_type=jnp.float32
    )
    attn_in_terms = (
        jnp.einsum("tj,dj->td", query_raw_grad, full_query, preferred_element_type=jnp.float32)
        + jnp.einsum("tj,dj->td", key_raw_grad, full_key, preferred_element_type=jnp.float32)
        + jnp.einsum("tj,dj->td", value_raw_grad, full_value, preferred_element_type=jnp.float32)
    )
    attn_stat = jnp.sum(attn_in_terms * attn_gain * token_values, axis=1)
    attn_in_grad, attn_stat_total = sum_with_stat(attn_in_terms, attn_stat)
    local_attn_gain = norm_attn.astype(jnp.float32)
    d_attn_gain = jnp.sum(attn_in_grad * local_tokens * inv_first, axis=0)
    d_tokens = (
        hidden_grad_total
        + inv_first * local_attn_gain * attn_in_grad
        - inv_first**3 * local_tokens * attn_stat_total / width
    )
    gain_grads = lax.psum((d_attn_gain, d_query_gain, d_key_gain, d_moe_gain), "row")
    (
        summed_query_w,
        summed_key_w,
        summed_value_w,
        summed_out_w,
        summed_router_w,
        summed_gate_w,
        summed_up_w,
        summed_down_w,
    ) = (
        lax.psum_scatter(d_query_w, "row", scatter_dimension=0, tiled=True),
        lax.psum_scatter(d_key_w, "row", scatter_dimension=0, tiled=True),
        lax.psum_scatter(d_value_w, "row", scatter_dimension=0, tiled=True),
        lax.psum_scatter(d_out_w, "row", scatter_dimension=0, tiled=True),
        lax.psum_scatter(d_router_w, "row", scatter_dimension=0, tiled=True),
        lax.psum_scatter(d_gate_w, "row", scatter_dimension=0, tiled=True),
        lax.psum_scatter(d_up_w, "row", scatter_dimension=0, tiled=True),
        lax.psum_scatter(d_down_w, "row", scatter_dimension=0, tiled=True),
    )
    return (
        output,
        d_tokens,
        gain_grads[0],
        gain_grads[1],
        gain_grads[2],
        gain_grads[3],
        summed_query_w,
        summed_key_w,
        summed_value_w,
        summed_out_w,
        summed_router_w,
        summed_gate_w,
        summed_up_w,
        summed_down_w,
    )


def solution(mesh):
    in_specs = (
        P("row", "col"),
        P("col"),
        P("col"),
        P("col"),
        P("col"),
        P("row", "col"),
        P("row", "col"),
        P("row", "col"),
        P("row", "col"),
        P("row", "col"),
        P("row", None, "col"),
        P("row", None, "col"),
        P("row", None, "col"),
        P("row", None),
        P("row", None),
        P("row", "col"),
    )
    out_specs = (
        P("row", "col"),
        P("row", "col"),
        P("col"),
        P("col"),
        P("col"),
        P("col"),
        P("row", "col"),
        P("row", "col"),
        P("row", "col"),
        P("row", "col"),
        P("row", "col"),
        P("row", None, "col"),
        P("row", None, "col"),
        P("row", None, "col"),
    )
    return jax.shard_map(shards, mesh=mesh, in_specs=in_specs, out_specs=out_specs, check_vma=False)
```

profile of v0, /device:TPU:0, one launch (start us, length us, event | category | flops | bytes accessed | tf_op | source)
XLA Modules:
  0.0 4125.3 jit_solution(1129559334412963518)
XLA Ops:
  29.0 64.2 %all-gather.17.cloned.1.call-done = bf16[1024,2048]{0,1:T(8,128)(2,1)} async-done(((bf16[1024,512]{0,1:T(8,128)(2,1)}), bf16[1024,2048]{0,1:T(8,128)(2,1)}) %all-gather.17.cloned.1.call-update) | async-done | bytes 4194320 | tf_op jit(solution)/shard_map/all_gather | solution.py:103
  96.9 24.5 all-gather.19.cloned.1.call-done
  126.7 24.4 all-gather.21.cloned.1.call-done
  201.3 24.9 while.59
  235.8 141.2 %reduce-scatter.15.cloned.1.call-done = f32[1024,512]{0,1:T(8,128)} async-done(((f32[1024,2048]{0,1:T(8,128)}), f32[1024,512]{0,1:T(8,128)}) %reduce-scatter.15.cloned.1.call-update) | async-done | bytes 2097168 | tf_op jit(solution)/shard_map/reduce_scatter | solution.py:64
  420.6 60.4 %scatter_custom_fusion.2 = s32[10256]{0:T(1024)S(1)} fusion(s32[16384]{0:T(1024)S(1)} %reshape.511, s32[16384]{0:T(1024)S(1)} %reshape.513, s32[]{:T(128)} %constant.174.clone.1), kind=kCustom, calls=%fused_computation.207 | custom fusion | bytes 41028
  496.3 114.1 %all-gather.27.cloned.1.call-done = f32[1024,2048]{0,1:T(8,128)} async-done(((f32[1024,512]{0,1:T(8,128)}), f32[1024,2048]{0,1:T(8,128)}) %all-gather.27.cloned.1.call-update) | async-done | bytes 8388624 | tf_op jit(solution)/shard_map/all_gather | solution.py:166
  644.9 55.3 %all-gather.29.cloned.1.call-done = bf16[2048,16,256]{2,0,1:T(8,128)(2,1)} async-done(((bf16[256,16,256]{2,0,1:T(8,128)(2,1)}), bf16[2048,16,256]{2,0,1:T(8,128)(2,1)}) %all-gather.29.cloned.1.call-update) | async-done | bytes 16777232 | tf_op jit(solution)/shard_map/all_gather | solution.py:113
  700.2 91.5 %all-gather.31.cloned.1.call-done = bf16[2048,16,256]{2,0,1:T(8,128)(2,1)} async-done(((bf16[256,16,256]{2,0,1:T(8,128)(2,1)}), bf16[2048,16,256]{2,0,1:T(8,128)(2,1)}) %all-gather.31.cloned.1.call-update) | async-done | bytes 16777232 | tf_op jit(solution)/shard_map/all_gather | solution.py:114
  791.7 91.7 %all-gather.33.cloned.1.call-done = bf16[2048,16,256]{2,0,1:T(8,128)(2,1)} async-done(((bf16[256,16,256]{2,0,1:T(8,128)(2,1)}), bf16[2048,16,256]{2,0,1:T(8,128)(2,1)}) %all-gather.33.cloned.1.call-update) | async-done | bytes 16777232 | tf_op jit(solution)/shard_map/all_gather | solution.py:115
  887.8 772.9 %while.60 = (s32[]{:T(128)}, f32[1025,2048]{1,0:T(8,128)}, f32[16,640,256]{2,1,0:T(8,128)}, f32[16,640,256]{2,1,0:T(8,128)}, bf16[16,640,256]{2,1,0:T(8,128)(2,1...) while((s32[]{:T(128)}, f32[1025,2048]{1,0:T(8,128)}, ...), condition=%wide.region_20.21_spmd, body=%wide.region_18.20_spmd.sunk | while | flops 2015726464 | bytes 42176756 | solution.py:215
  962.1 21.4 scatter_fusion
  1107.0 21.4 scatter_fusion
  1155.3 21.4 scatter_fusion
  1665.0 925.4 %while.61 = (s32[]{:T(128)}, f32[1025,2048]{1,0:T(8,128)}, f32[16,640]{1,0:T(8,128)S(1)}, bf16[16,640,256]{1,2,0:T(8,128)(2,1)}, bf16[16,640,256]{1,2,0:T(8,128)...) while((s32[]{:T(128)}, f32[1025,2048]{1,0:T(8,128)}, ...), condition=%wide.region_25.26_spmd, body=%wide.region_22.25_spmd.sunk | while | flops 2019330304 | bytes 56808740 | solution.py:259
  1699.4 23.5 scatter_custom_fusion.12
  1757.2 23.5 scatter_custom_fusion.12
  1815.0 23.5 scatter_custom_fusion.12
  1872.8 23.5 scatter_custom_fusion.12
  1930.6 23.5 scatter_custom_fusion.12
  1988.4 23.5 scatter_custom_fusion.12
  2046.2 23.5 scatter_custom_fusion.12
  2104.0 23.5 scatter_custom_fusion.12
  2161.8 23.5 scatter_custom_fusion.12
  2219.6 23.5 scatter_custom_fusion.12
  2277.4 23.5 scatter_custom_fusion.12
  2335.2 23.5 scatter_custom_fusion.12
  2393.0 23.5 scatter_custom_fusion.12
  2450.9 23.5 scatter_custom_fusion.12
  2508.6 23.5 scatter_custom_fusion.12
  2566.5 23.5 scatter_custom_fusion.12
  2590.5 71.3 %scatter_custom_fusion.3 = f32[16400]{0:T(1024)S(1)} fusion(s32[10240]{0:T(1024)} %reshape.517, f32[10240]{0:T(1024)S(1)} %reshape.519, f32[]{:T(128)} %constant.116.clone.1), kind=kCustom, calls=%fused_computation.203 | custom fusion | flops 10240 | bytes 66112
  2671.7 25.2 all-reduce.10.cloned.1.call-done
  2730.2 123.0 %reduce-scatter.19.cloned.1.call-done = f32[1024,512]{0,1:T(8,128)} async-done(((f32[1024,2048]{0,1:T(8,128)}), f32[1024,512]{0,1:T(8,128)}) %reduce-scatter.19.cloned.1.call-update) | async-done | bytes 2097168 | tf_op jit(solution)/shard_map/reduce_scatter | solution.py:74
  2878.8 59.3 %all-gather.37.cloned.1.call-done = bf16[1024,2048]{0,1:T(8,128)(2,1)} async-done(((bf16[1024,512]{0,1:T(8,128)(2,1)}), bf16[1024,2048]{0,1:T(8,128)(2,1)}) %all-gather.37.cloned.1.call-update) | async-done | bytes 4194320 | tf_op jit(solution)/shard_map/all_gather | solution.py:68
  2946.7 50.5 %while.62 = (s32[]{:T(128)}, f32[1024,4,128]{0,2,1:T(8,128)S(1)}, f32[1024,4,128]{0,2,1:T(8,128)}, f32[2,512,4,128]{3,1,0,2:T(8,128)}, bf16[2,512,4,128]{3,1,2,0...) while((s32[]{:T(128)}, f32[1024,4,128]{0,2,1:T(8,128)S(1)}, ...), condition=%wide.region_34.35_spmd.clone, body=%wide.region_32.34_spmd.clone.sunk | while | flops 2720791552 | bytes 181478368 | solution.py:341
  3054.2 79.6 %gather_fusion.4 = bf16[10240,2048]{1,0:T(8,128)(2,1)} fusion(bf16[1025,2048]{1,0:T(8,128)(2,1)} %get-tuple-element.1223, s32[10240]{0:T(1024)S(1)} %broadcast_clamp_fusion), kind=kCustom, calls=%fused_computation.4 | custom fusion | bytes 83927040 | tf_op jit(solution)/shard_map/gather | solution.py:270
  3133.8 29.2 convolution_bitcast_fusion.2
  3163.1 29.3 convolution_bitcast_fusion.1
  3192.5 79.1 %gather_fusion.5 = bf16[10240,2048]{1,0:T(8,128)(2,1)} fusion(bf16[1025,2048]{1,0:T(8,128)(2,1)} %get-tuple-element.1222, s32[10240]{0:T(1024)S(1)} %broadcast_clamp_fusion), kind=kCustom, calls=%fused_computation.5 | custom fusion | bytes 83927040 | tf_op jit(solution)/shard_map/gather | solution.py:271
  3271.5 34.0 convolution_bitcast_fusion
  3382.6 97.9 %reduce-scatter.31.cloned.1.call-done = f32[256,16,256]{0,2,1:T(8,128)} async-done(((f32[2048,16,256]{0,2,1:T(8,128)}), f32[256,16,256]{0,2,1:T(8,128)}) %reduce-scatter.31.cloned.1.call-update) | async-done | bytes 4194320 | tf_op jit(solution)/shard_map/reduce_scatter | solution.py:401
  3485.9 203.4 %reduce-scatter.33.cloned.1.call-done = f32[256,16,256]{0,2,1:T(8,128)} async-done(((f32[2048,16,256]{0,2,1:T(8,128)}), f32[256,16,256]{0,2,1:T(8,128)}) %reduce-scatter.33.cloned.1.call-update) | async-done | bytes 4194320 | tf_op jit(solution)/shard_map/reduce_scatter | solution.py:402
  3694.7 203.3 %reduce-scatter.35.cloned.1.call-done = f32[256,16,256]{0,2,1:T(8,128)} async-done(((f32[2048,16,256]{0,2,1:T(8,128)}), f32[256,16,256]{0,2,1:T(8,128)}) %reduce-scatter.35.cloned.1.call-update) | async-done | bytes 4194320 | tf_op jit(solution)/shard_map/reduce_scatter | solution.py:403
  3903.4 49.7 %reduce-scatter.25.cloned.1.call-done = f32[256,512]{1,0:T(8,128)} async-done(((f32[2048,512]{1,0:T(8,128)}), f32[256,512]{1,0:T(8,128)}) %reduce-scatter.25.cloned.1.call-update) | async-done | bytes 524304 | tf_op jit(solution)/shard_map/reduce_scatter | solution.py:397
  3953.1 55.1 %reduce-scatter.29.cloned.1.call-done = f32[256,512]{1,0:T(8,128)} async-done(((f32[2048,512]{1,0:T(8,128)}), f32[256,512]{1,0:T(8,128)}) %reduce-scatter.29.cloned.1.call-update) | async-done | bytes 524304 | tf_op jit(solution)/shard_map/reduce_scatter | solution.py:399
  4008.2 55.1 %reduce-scatter.23.cloned.1.call-done = f32[256,512]{1,0:T(8,128)} async-done(((f32[2048,512]{1,0:T(8,128)}), f32[256,512]{1,0:T(8,128)}) %reduce-scatter.23.cloned.1.call-update) | async-done | bytes 524304 | tf_op jit(solution)/shard_map/reduce_scatter | solution.py:396
  4063.3 55.0 %reduce-scatter.27.cloned.1.call-done = f32[256,512]{1,0:T(8,128)} async-done(((f32[2048,512]{1,0:T(8,128)}), f32[256,512]{1,0:T(8,128)}) %reduce-scatter.27.cloned.1.call-update) | async-done | bytes 524304 | tf_op jit(solution)/shard_map/reduce_scatter | solution.py:398
  (961 shorter events, 1679.3 us)
Async XLA Ops:
  7.2 86.0 %all-gather.17.cloned.1.call-start = ((), (), s32[]{:S(2)}) async-start(), calls=%async_computation.12 | async-start | bytes 5242880 | tf_op jit(solution)/shard_map/all_gather | solution.py:103
  9.6 111.8 %all-gather.19.cloned.1.call-start = ((), (), s32[]{:S(2)}) async-start(), calls=%async_computation.13 | async-start | bytes 2359296 | tf_op jit(solution)/shard_map/all_gather | solution.py:108
  10.3 140.8 %all-gather.21.cloned.1.call-start = ((), (), s32[]{:S(2)}) async-start(), calls=%async_computation.14 | async-start | bytes 2359296 | tf_op jit(solution)/shard_map/all_gather | solution.py:109
  11.1 181.8 %all-gather.23.cloned.1.call-start = ((), (), s32[]{:S(2)}) async-start(), calls=%async_computation.15 | async-start | bytes 2359296 | tf_op jit(solution)/shard_map/all_gather | solution.py:110
  11.6 214.6 %all-gather.25.cloned.1.call-start = ((), (), s32[]{:S(2)}) async-start(), calls=%async_computation.16 | async-start | bytes 2359296 | tf_op jit(solution)/shard_map/all_gather | solution.py:111
  12.2 364.8 %reduce-scatter.15.cloned.1.call-start = ((), (), s32[]{:S(2)}) async-start(), calls=%async_computation.17 | async-start | bytes 10485760 | tf_op jit(solution)/shard_map/reduce_scatter | solution.py:64
  26.1 166.7 %copy-start.68 = (f32[4,1,512]{2,1,0:T(1,128)}, f32[4,1,512]{2,1,0:T(1,128)S(1)}, u32[]{:S(2)}) copy-start(f32[4,1,512]{2,1,0:T(1,128)S(1)} %mul.713) | copy-start | bytes 24580
  26.1 144.2 %copy-start.64 = (f32[512]{0:T(512)}, f32[512]{0:T(512)S(1)}, u32[]{:S(2)}) copy-start(f32[512]{0:T(512)S(1)} %convert_element_type.91) | copy-start | bytes 6148
  26.2 152.4 %copy-start.66 = (f32[512]{0:T(512)}, f32[512]{0:T(512)S(1)}, u32[]{:S(2)}) copy-start(f32[512]{0:T(512)S(1)} %convert_element_type.92) | copy-start | bytes 6148
  28.9 157.9 %copy-start.30 = (f32[1024,64]{1,0:T(8,128)}, f32[1024,64]{1,0:T(8,128)S(1)}, u32[]{:S(2)}) copy-start(f32[1024,64]{1,0:T(8,128)S(1)} %get-tuple-element.700) | copy-start | bytes 786436
  96.9 95.9 %copy-start.75 = (f32[1024]{0:T(1024)}, f32[1024]{0:T(1024)S(1)}, u32[]{:S(2)}) copy-start(f32[1024]{0:T(1024)S(1)} %get-tuple-element.691) | copy-start | bytes 12292
  126.7 43.7 %copy-start.17 = (f32[1024,512]{0,1:T(8,128)}, f32[1024,512]{0,1:T(8,128)S(1)}, u32[]{:S(2)}) copy-start(f32[1024,512]{0,1:T(8,128)S(1)} %get-tuple-element.702) | copy-start | bytes 6291460
  235.0 142.0 %copy-start.23 = (bf16[1024,512]{0,1:T(8,128)(2,1)S(1)}, bf16[1024,512]{0,1:T(8,128)(2,1)}, u32[]{:S(2)}) copy-start(bf16[1024,512]{0,1:T(8,128)(2,1)} %copy.154) | copy-start | bytes 3145732
  235.0 145.4 %copy-start.36 = (bf16[256,16,256]{2,1,0:T(8,128)(2,1)S(1)}, bf16[256,16,256]{2,1,0:T(8,128)(2,1)}, u32[]{:S(2)}) copy-start(bf16[256,16,256]{2,1,0:T(8,128)(2,1)} %param.34) | copy-start | bytes 6291460
  235.0 256.4 %all-gather.35.cloned.1.call-start = ((), (), s32[]{:S(2)}) async-start(), calls=%async_computation.23 | async-start | bytes 5242880 | tf_op jit(solution)/shard_map/all_gather | solution.py:68
  235.8 374.6 %all-gather.27.cloned.1.call-start = ((), (), s32[]{:S(2)}) async-start(), calls=%async_computation.18 | async-start | bytes 10485760 | tf_op jit(solution)/shard_map/all_gather | solution.py:166
  380.4 319.9 %all-gather.29.cloned.1.call-start = ((), (), s32[]{:S(2)}) async-start(), calls=%async_computation.19 | async-start | bytes 18874368 | tf_op jit(solution)/shard_map/all_gather | solution.py:113
  382.5 409.3 %all-gather.31.cloned.1.call-start = ((), (), s32[]{:S(2)}) async-start(), calls=%async_computation.20 | async-start | bytes 18874368 | tf_op jit(solution)/shard_map/all_gather | solution.py:114
  386.3 95.4 %copy-start.90 = (s32[2]{0:T(128)S(1)}, s32[2]{0:T(128)}, u32[]{:S(2)}) copy-start(s32[2]{0:T(128)} %constant.198) | copy-start | bytes 28
  386.3 497.1 %all-gather.33.cloned.1.call-start = ((), (), s32[]{:S(2)}) async-start(), calls=%async_computation.21 | async-start | bytes 18874368 | tf_op jit(solution)/shard_map/all_gather | solution.py:115
  388.4 93.4 %copy-start.89 = (s32[2]{0:T(128)S(1)}, s32[2]{0:T(128)}, u32[]{:S(2)}) copy-start(s32[2]{0:T(128)} %constant.201) | copy-start | bytes 28
  388.4 94.1 %copy-start.86 = (bf16[256,4]{0,1:T(4,128)(2,1)S(1)}, bf16[256,4]{0,1:T(4,128)(2,1)}, u32[]{:S(2)}) copy-start(bf16[256,4]{0,1:T(4,128)(2,1)} %param.33) | copy-start | bytes 6148
  388.4 2308.5 %all-reduce.10.cloned.1.call-start = ((), (), s32[]{:S(2)}) async-start(), calls=%async_computation.24 | async-start | bytes 131072 | tf_op jit(solution)/shard_map/psum | solution.py:279
  401.8 213.4 %copy-start.50 = (f32[4,1,512]{2,1,0:T(1,128)}, f32[4,1,512]{2,1,0:T(1,128)S(1)}, u32[]{:S(2)}) copy-start(f32[4,1,512]{2,1,0:T(1,128)S(1)} %mul.714) | copy-start | bytes 24580
  491.4 138.9 %copy-start.46 = (bf16[2048,4]{0,1:T(4,128)(2,1)}, bf16[2048,4]{0,1:T(4,128)(2,1)S(1)}, u32[]{:S(2)}) copy-start(bf16[2048,4]{0,1:T(4,128)(2,1)S(1)} %all_gather.61) | copy-start | bytes 49156
  2662.5 190.7 %reduce-scatter.19.cloned.1.call-start = ((), (), s32[]{:S(2)}) async-start(), calls=%async_computation.25 | async-start | bytes 10485760 | tf_op jit(solution)/shard_map/reduce_scatter | solution.py:74
  2662.6 36.0 copy-start.47
  2708.6 144.7 %copy-start.15 = (f32[1024,512]{0,1:T(8,128)S(1)}, f32[1024,512]{0,1:T(8,128)}, u32[]{:S(2)}) copy-start(f32[1024,512]{0,1:T(8,128)} %convert_add_fusion) | copy-start | bytes 6291460
  2708.6 144.7 %copy-start.53 = (f32[1024]{0:T(1024)S(1)}, f32[1024]{0:T(1024)}, u32[]{:S(2)}) copy-start(f32[1024]{0:T(1024)} %copy-done.52) | copy-start | bytes 12292
  2708.6 144.6 %copy-start.60 = (f32[1024]{0:T(1024)S(1)}, f32[1024]{0:T(1024)}, u32[]{:S(2)}) copy-start(f32[1024]{0:T(1024)} %get-tuple-element.696) | copy-start | bytes 12292
  2708.7 229.5 %all-gather.37.cloned.1.call-start = ((), (), s32[]{:S(2)}) async-start(), calls=%async_computation.26 | async-start | bytes 5242880 | tf_op jit(solution)/shard_map/all_gather | solution.py:68
  2710.4 150.6 %copy-start.28 = (bf16[1024,512]{0,1:T(8,128)(2,1)}, bf16[1024,512]{0,1:T(8,128)(2,1)S(1)}, u32[]{:S(2)}) copy-start(bf16[1024,512]{0,1:T(8,128)(2,1)S(1)} %copy.174) | copy-start | bytes 3145732
  2710.4 150.6 %copy-start.72 = (f32[512]{0:T(512)}, f32[512]{0:T(512)S(1)}, u32[]{:S(2)}) copy-start(f32[512]{0:T(512)S(1)} %convert_element_type.98) | copy-start | bytes 6148
  2730.2 130.8 %copy-start.62 = (f32[1024,1]{0,1:T(1,128)}, f32[1024,1]{0,1:T(1,128)S(1)}, u32[]{:S(2)}) copy-start(f32[1024,1]{0,1:T(1,128)S(1)} %constant_dynamic-slice_fusion.4) | copy-start | bytes 12292
  2856.5 483.2 %reduce-scatter.37.cloned.1.call-start = ((), (), s32[]{:S(2)}) async-start(), calls=%async_computation.35 | async-start | bytes 1179648
  2861.0 497.7 %reduce-scatter.17.cloned.1.call-start = ((), (), s32[]{:S(2)}) async-start(), calls=%async_computation.22 | async-start | bytes 10485760 | tf_op jit(solution)/shard_map/reduce_scatter | solution.py:64
  2878.7 480.1 %reduce-scatter.21.cloned.1.call-start = ((), (), s32[]{:S(2)}) async-start(), calls=%async_computation.27 | async-start | bytes 10485760 | tf_op jit(solution)/shard_map/reduce_scatter | solution.py:74
  2878.8 67.9 %copy-start.4 = (bf16[1024,4,128]{2,0,1:T(8,128)(2,1)S(1)}, bf16[1024,4,128]{2,0,1:T(8,128)(2,1)}, u32[]{:S(2)}) copy-start(bf16[1024,4,128]{2,0,1:T(8,128)(2,1)} %copy-done.3) | copy-start | bytes 3145732
  2878.8 67.9 %copy-start.39 = (s32[1024]{0:T(1024)S(1)}, s32[1024]{0:T(1024)}, u32[]{:S(2)}) copy-start(s32[1024]{0:T(1024)} %copy-done.38) | copy-start | bytes 12292
  2878.8 67.9 %copy-start.49 = (f32[2,4,512]{2,1,0:T(4,128)S(1)}, f32[2,4,512]{2,1,0:T(4,128)}, u32[]{:S(2)}) copy-start(f32[2,4,512]{2,1,0:T(4,128)} %copy-done.48) | copy-start | bytes 49156
  2878.8 67.9 %copy-start.97 = (s32[2]{0:T(128)S(1)}, s32[2]{0:T(128)}, u32[]{:S(2)}) copy-start(s32[2]{0:T(128)} %copy-done.96) | copy-start | bytes 28
  3053.5 427.0 %reduce-scatter.31.cloned.1.call-start = ((), (), s32[]{:S(2)}) async-start(), calls=%async_computation.32 | async-start | bytes 37748736 | tf_op jit(solution)/shard_map/reduce_scatter | solution.py:401
  3163.1 526.2 %reduce-scatter.33.cloned.1.call-start = ((), (), s32[]{:S(2)}) async-start(), calls=%async_computation.33 | async-start | bytes 37748736 | tf_op jit(solution)/shard_map/reduce_scatter | solution.py:402
  3192.4 705.6 %reduce-scatter.35.cloned.1.call-start = ((), (), s32[]{:S(2)}) async-start(), calls=%async_computation.34 | async-start | bytes 37748736 | tf_op jit(solution)/shard_map/reduce_scatter | solution.py:403
  3305.6 647.5 %reduce-scatter.25.cloned.1.call-start = ((), (), s32[]{:S(2)}) async-start(), calls=%async_computation.29 | async-start | bytes 4718592 | tf_op jit(solution)/shard_map/reduce_scatter | solution.py:397
  3314.7 693.5 %reduce-scatter.29.cloned.1.call-start = ((), (), s32[]{:S(2)}) async-start(), calls=%async_computation.31 | async-start | bytes 4718592 | tf_op jit(solution)/shard_map/reduce_scatter | solution.py:399
  3322.6 740.7 %reduce-scatter.23.cloned.1.call-start = ((), (), s32[]{:S(2)}) async-start(), calls=%async_computation.28 | async-start | bytes 4718592 | tf_op jit(solution)/shard_map/reduce_scatter | solution.py:396
  3330.6 787.7 %reduce-scatter.27.cloned.1.call-start = ((), (), s32[]{:S(2)}) async-start(), calls=%async_computation.30 | async-start | bytes 4718592 | tf_op jit(solution)/shard_map/reduce_scatter | solution.py:398
  (129 other events, 1762.1 us)
Sparse Core Ops, SparseCore 0:
  9.7 83.4 all-gather.16
  95.1 26.2 all-gather.18
  123.3 27.7 all-gather.20
  152.8 27.7 all-gather.22
  182.4 27.7 all-gather.24
  235.1 141.8 reduce-scatter.14
  378.6 81.4 all-gather.34
  462.2 148.0 all-gather.26
  612.3 87.9 all-gather.28
  702.0 89.7 all-gather.30
  793.6 89.7 all-gather.32
  2662.7 34.2 all-reduce.9
  2708.8 144.4 reduce-scatter.18
  2856.6 81.4 all-gather.36
  2941.2 34.4 reduce-scatter.36
  2977.9 145.0 reduce-scatter.16
  3125.2 145.2 reduce-scatter.20
  3273.9 206.4 reduce-scatter.30
  3484.0 205.2 reduce-scatter.32
  3692.7 205.2 reduce-scatter.34
  3901.9 51.1 reduce-scatter.24
  3957.0 51.1 reduce-scatter.28
  4012.1 51.1 reduce-scatter.22
  4067.1 51.1 reduce-scatter.26
where the time goes:
time: 4140 us; the launch traced here: 4130 us
  waiting for transfers between devices  1540 us (37%)
  local copies, waits for them, and re-layouts  894 us (22%)
  other arithmetic  891 us (22%)
  matrix products  592 us (14%)
  blocking collectives  122 us (3%)
  loops' own time  72.8 us (2%)
    scatter-add x16, other arithmetic, expert_backward(): input_acc = input_acc.at[slot_tokens].add(input_rows)  376 us
    scatter-add x16, other arithmetic, expert_forward(): return (total.at[slot_tokens].add(expert_out), (gate_pre, up_pre, hidden))  343 us
    reduce_scatter x1, waiting for transfers between devices, shards(): lax.psum_scatter(d_up_w, 'row', scatter_dimension=0, tiled=True)  203 us
    reduce_scatter x1, waiting for transfers between devices, shards(): lax.psum_scatter(d_down_w, 'row', scatter_dimension=0, tiled=True)  203 us
    gather x16, local copies, waits for them, and re-layouts, expert_forward(): chosen = padded_rows[slot_tokens]  145 us
    gather x16, local copies, waits for them, and re-layouts, expert_backward(): grad_rows = padded_grad[slot_tokens]  145 us
    reduce_scatter x2, waiting for transfers between devices, sum_features(): return lax.psum_scatter(terms, 'col', scatter_dimension=1, tiled=True)  141 us
    unnamed x202, local copies, waits for them, and re-layouts  124 us
  transfers between devices with their start and end apart: 24, of which 18 were waited for; matrix products, arithmetic and copies ran while one was open for 15% of the time, Pallas kernels for 0%

commit v1 on v0

v1 whole, which is shorter than its diff:
```python
import functools
import math

import jax
import jax.numpy as jnp
from jax import lax
from jax.experimental import pallas as pl
from jax.experimental.layout import Layout, with_layout_constraint
from jax.experimental.pallas import tpu as pltpu
from jax.sharding import PartitionSpec as P

HD = 128
IMG = 256

EPSILON = 1e-05
ROPE_BASE = 10000.0
MASKED = -1e30
VMEM_LIMIT = 66_000_000
BF = jnp.bfloat16
F32 = jnp.float32


def dot_nn(a, b):
    return lax.dot_general(a, b, (((1,), (0,)), ((), ())), preferred_element_type=F32)


def dot_nt(a, b):
    return lax.dot_general(a, b, (((1,), (1,)), ((), ())), preferred_element_type=F32)


def dot_tn(a, b):
    return lax.dot_general(a, b, (((0,), (0,)), ((), ())), preferred_element_type=F32)


def row_major(values):
    return with_layout_constraint(values, Layout(major_to_minor=tuple(range(values.ndim))))


def after(values, *others):
    return lax.optimization_barrier((values, *others))[0]


def line_pairs():
    n = lax.axis_size("col")
    return n, [(i, i + 1) for i in range(n - 1)], [(i + 1, i) for i in range(n - 1)]


def gather_line(block):
    n, to_right, to_left = line_pairs()
    me = lax.axis_index("col")
    from_left, from_right = [block], [block]
    for _ in range(n - 1):
        from_left.append(lax.ppermute(from_left[-1], "col", to_right))
        from_right.append(lax.ppermute(from_right[-1], "col", to_left))
    out = jnp.zeros((n, *block.shape), block.dtype)
    out = lax.dynamic_update_index_in_dim(out, block, me, 0)
    for r in range(1, n):
        piece = from_left[r] + from_right[n - r]
        out = lax.dynamic_update_index_in_dim(out, piece, lax.rem(me - r + n, n), 0)
    return out


def scatter_line(part):
    n, to_right, to_left = line_pairs()
    me = lax.axis_index("col")
    right = left = None
    for r in range(1, n):
        k = n - r
        go_right = part(jnp.minimum(me + k, n - 1))
        go_left = part(jnp.maximum(me - k, 0))
        if right is not None:
            go_right = go_right + right.astype(F32)
            go_left = go_left + left.astype(F32)
        right = lax.ppermute(go_right.astype(BF), "col", to_right)
        left = lax.ppermute(go_left.astype(BF), "col", to_left)
    return part(me) + right.astype(F32) + left.astype(F32)


def sum_small(values):
    n = lax.axis_size("col")
    total = values
    for k in range(1, n):
        total = total + lax.ppermute(values, "col", [(i, (i + k) % n) for i in range(n)])
    return total


def gather_small(values):
    n = lax.axis_size("col")
    me = lax.axis_index("col")
    out = jnp.zeros((n, *values.shape), values.dtype)
    out = lax.dynamic_update_index_in_dim(out, values, me, 0)
    for k in range(1, n):
        piece = lax.ppermute(values, "col", [(i, (i + k) % n) for i in range(n)])
        out = lax.dynamic_update_index_in_dim(out, piece, lax.rem(me - k + n, n), 0)
    return out


def rope_tables(length):
    half_size = HD // 2
    places = jnp.arange(length, dtype=F32)
    rates = jnp.exp(-math.log(ROPE_BASE) * jnp.arange(half_size, dtype=F32) / half_size)
    angles = places[:, None] * rates[None, :]
    cosine, sine = jnp.cos(angles), jnp.sin(angles)
    return jnp.concatenate([cosine, cosine], 1), jnp.concatenate([-sine, sine], 1)


def span_ids(starts, length):
    places = jnp.arange(length, dtype=jnp.int32)
    inside = (places[None, :] >= starts[:, None]) & (places[None, :] < starts[:, None] + IMG)
    numbers = jnp.arange(1, starts.shape[0] + 1, dtype=jnp.int32)
    return jnp.sum(jnp.where(inside, numbers[:, None], 0), axis=0)


def attend_kernel(
    scale, block, q_ref, k_ref, v_ref, iq_ref, ik_ref, gq_ref, gk_ref, cos_ref, sin_ref,
    srow_ref, scol_ref, qo_ref, ko_ref, vo_ref, mixed_ref
):
    rows = q_ref.shape[0]
    cosine, sine = cos_ref[...], sin_ref[...]

    def turned(raw_ref, inv_ref, gain_ref):
        normed = raw_ref[...] * inv_ref[...] * gain_ref[...].astype(F32)
        return (normed * cosine + pltpu.roll(normed, HD // 2, 1) * sine).astype(BF)

    qo_ref[...] = turned(q_ref, iq_ref, gq_ref)
    ko_ref[...] = turned(k_ref, ik_ref, gk_ref)
    vo_ref[...] = v_ref[...].astype(BF)
    for first in range(0, rows, block):
        last = min(rows, first + block + IMG)
        scores = dot_nt(qo_ref[first : first + block, :], ko_ref[:last, :]) * scale
        q_at = first + lax.broadcasted_iota(jnp.int32, scores.shape, 0)
        k_at = lax.broadcasted_iota(jnp.int32, scores.shape, 1)
        q_span = scol_ref[first : first + block, :]
        seen = (k_at <= q_at) | ((q_span == srow_ref[:, :last]) & (q_span > 0))
        scores = jnp.where(seen, scores, MASKED)
        raised = jnp.exp(scores - jnp.max(scores, axis=1, keepdims=True))
        probs = (raised / jnp.sum(raised, axis=1, keepdims=True)).astype(BF)
        mixed_ref[first : first + block, :] = dot_nn(probs, vo_ref[:last, :]).astype(BF)


def attend(qkv, inv_q, inv_k, gain_q, gain_k, cosine, sine, span_row, span_col):
    rows = qkv.shape[0]
    width = qkv.shape[1] // 3
    heads = width // HD
    head = lambda shift: pl.BlockSpec((rows, HD), lambda h: (0, h + shift * heads))
    whole = lambda shape: pl.BlockSpec(shape, lambda h: (0, 0))
    out = jax.ShapeDtypeStruct((rows, width), BF)
    return pl.pallas_call(
        functools.partial(attend_kernel, 1.0 / math.sqrt(HD), min(256, rows)),
        grid=(heads,),
        in_specs=[
            head(0), head(1), head(2), whole((rows, 1)), whole((rows, 1)),
            pl.BlockSpec((1, HD), lambda h: (0, h)), pl.BlockSpec((1, HD), lambda h: (0, h)),
            whole((rows, HD)), whole((rows, HD)), whole((1, rows)), whole((rows, 1)),
        ],
        out_specs=[head(0)] * 4,
        out_shape=[out] * 4,
        compiler_params=pltpu.CompilerParams(vmem_limit_bytes=VMEM_LIMIT),
        cost_estimate=pl.CostEstimate(
            flops=4 * rows * rows * width, bytes_accessed=20 * rows * width,
            transcendentals=rows * rows * heads,
        ),
        name="attend",
    )(qkv, qkv, qkv, inv_q, inv_k, gain_q, gain_k, cosine, sine, span_row, span_col)


def attend_back_kernel(
    scale, block, q_ref, k_ref, v_ref, d_ref, cos_ref, sin_ref, srow_ref, scol_ref,
    dq_ref, dk_ref, dv_ref, dk_sum, dv_sum
):
    rows = q_ref.shape[0]
    dk_sum[...] = jnp.zeros_like(dk_sum)
    dv_sum[...] = jnp.zeros_like(dv_sum)

    def turned(values, at):
        return values * cos_ref[at, :] - pltpu.roll(values, HD // 2, 1) * sin_ref[at, :]

    for first in range(0, rows, block):
        here = slice(first, first + block)
        last = min(rows, first + block + IMG)
        queries, keys, grads = q_ref[here, :], k_ref[:last, :], d_ref[here, :]
        scores = dot_nt(keys, queries) * scale
        k_at = lax.broadcasted_iota(jnp.int32, scores.shape, 0)
        q_at = first + lax.broadcasted_iota(jnp.int32, scores.shape, 1)
        q_span = srow_ref[:, here]
        seen = (k_at <= q_at) | ((q_span == scol_ref[:last, :]) & (q_span > 0))
        scores = jnp.where(seen, scores, MASKED)
        raised = jnp.exp(scores - jnp.max(scores, axis=0, keepdims=True))
        probs = raised / jnp.sum(raised, axis=0, keepdims=True)
        d_probs = dot_nt(v_ref[:last, :], grads)
        d_scores = (probs * (d_probs - jnp.sum(probs * d_probs, axis=0, keepdims=True))).astype(BF)
        dq_ref[here, :] = turned(dot_tn(d_scores, keys) * scale, here)
        dk_sum[:last, :] += dot_nn(d_scores, queries)
        dv_sum[:last, :] += dot_nn(probs.astype(BF), grads)
    dk_ref[...] = turned(dk_sum[...] * scale, slice(0, rows))
    dv_ref[...] = dv_sum[...].astype(BF)


def attend_back(queries, keys, values, grads, cosine, sine, span_row, span_col):
    rows, width = queries.shape
    heads = width // HD
    head = pl.BlockSpec((rows, HD), lambda h: (0, h))
    whole = lambda shape: pl.BlockSpec(shape, lambda h: (0, 0))
    return pl.pallas_call(
        functools.partial(attend_back_kernel, 1.0 / math.sqrt(HD), min(256, rows)),
        grid=(heads,),
        in_specs=[head] * 4
        + [whole((rows, HD)), whole((rows, HD)), whole((1, rows)), whole((rows, 1))],
        out_specs=[head] * 3,
        out_shape=[
            jax.ShapeDtypeStruct((rows, width), F32),
            jax.ShapeDtypeStruct((rows, width), F32),
            jax.ShapeDtypeStruct((rows, width), BF),
        ],
        scratch_shapes=[pltpu.VMEM((rows, HD), F32)] * 2,
        compiler_params=pltpu.CompilerParams(vmem_limit_bytes=VMEM_LIMIT),
        cost_estimate=pl.CostEstimate(
            flops=10 * rows * rows * width, bytes_accessed=20 * rows * width,
            transcendentals=rows * rows * heads,
        ),
        name="attend_back",
    )(queries, keys, values, grads, cosine, sine, span_row, span_col)


def moe_kernel(
    first, n_col, closing, x_ref, xt_ref, y_ref, yt_ref, gates_ref, w_ref, *rest
):
    if closing:
        probs_ref, before_ref, router_ref, *rest = rest
    dx_ref, dw_ref, hid_ref, dg_ref, acc, pre, up, grad, d_pre, d_up = rest
    step = pl.program_id(0)
    expert = step + first
    rows, width = x_ref.shape
    n_row, _, _, depth, units = w_ref.shape
    experts = gates_ref.shape[1]

    @pl.when(step == 0)
    def _():
        acc[...] = jnp.zeros_like(acc)
        dg_ref[...] = before_ref[...] if closing else jnp.zeros_like(dg_ref)

    w_gate = w_ref[:, 0, 0].reshape(width, units)
    w_up = w_ref[:, 0, 1].reshape(width, units)
    w_down = w_ref[:, 0, 2].reshape(width, units)
    pre[...] = dot_nn(x_ref[...], w_gate)
    up[...] = dot_nn(x_ref[...], w_up)
    grad[...] = dot_nn(y_ref[...], w_down)

    span = 32

    def activate(i, carry):
        at = pl.ds(pl.multiple_of(i * span, span), span)
        g, u, dh = pre[at, :], up[at, :], grad[at, :]
        mine = lax.broadcasted_iota(jnp.int32, (span, experts), 1) == expert
        gate = jnp.sum(jnp.where(mine, gates_ref[at, :], 0.0), axis=1, keepdims=True)
        s = 1.0 / (1.0 + jnp.exp(-g))
        silu = g * s
        both = silu * u
        hid_ref[0, at, :] = (gate * both).astype(BF)
        d_gate = jnp.sum(dh * both, axis=1, keepdims=True)
        dg_ref[at, :] += jnp.where(mine, d_gate, 0.0)
        act = dh * gate
        d_pre[at, :] = (act * u * (s * (1.0 + g * (1.0 - s)))).astype(BF)
        d_up[at, :] = (act * silu).astype(BF)
        return carry

    lax.fori_loop(0, rows // span, activate, 0)

    dw_ref[:, 0, 0] = dot_nn(xt_ref[...], d_pre[...]).astype(BF).reshape(n_row, depth, units)
    dw_ref[:, 0, 1] = dot_nn(xt_ref[...], d_up[...]).astype(BF).reshape(n_row, depth, units)
    dw_ref[:, 0, 2] = dot_nn(yt_ref[...], hid_ref[0]).astype(BF).reshape(n_row, depth, units)
    part = width // n_col
    for s in range(n_col):
        cols = slice(s * part, (s + 1) * part)
        acc[:, cols] += dot_nt(d_pre[...], w_gate[cols, :]) + dot_nt(d_up[...], w_up[cols, :])

    @pl.when(step == pl.num_programs(0) - 1)
    def _():
        if closing:
            probs = probs_ref[...]
            g = jnp.where(gates_ref[...] > 0.0, dg_ref[...], 0.0)
            low = (probs * (g - jnp.sum(probs * g, axis=1, keepdims=True))).astype(BF)
        for s in range(n_col):
            cols = slice(s * part, (s + 1) * part)
            total = acc[:, cols]
            if closing:
                total = total + dot_nn(low, router_ref[:, cols])
            dx_ref[s] = total.astype(BF)


def moe_half(first, x, xt, y, yt, gates, weights, closing):
    rows, width = x.shape
    n_row, here, _, depth, units = weights.shape
    experts = gates.shape[1]
    n_col = lax.axis_size("col")
    once = lambda shape: pl.BlockSpec(
        shape, lambda e: (0,) * len(shape), pipeline_mode=pl.Buffered(1)
    )
    block = pl.BlockSpec((n_row, 1, 3, depth, units), lambda e: (0, e, 0, 0, 0))
    operands = [x, xt, y, yt, gates, weights]
    in_specs = [
        once((rows, width)), once((width, rows)), once((rows, width)), once((width, rows)),
        once((rows, experts)), block,
    ]
    if closing is not None:
        operands += list(closing)
        in_specs += [once(a.shape) for a in closing]
    return pl.pallas_call(
        functools.partial(moe_kernel, first, n_col, closing is not None),
        grid=(here,),
        in_specs=in_specs,
        out_specs=[
            once((n_col, rows, width // n_col)), block,
            pl.BlockSpec((1, rows, units), lambda e: (e, 0, 0)), once((rows, experts)),
        ],
        out_shape=[
            jax.ShapeDtypeStruct((n_col, rows, width // n_col), BF),
            jax.ShapeDtypeStruct(weights.shape, BF),
            jax.ShapeDtypeStruct((here, rows, units), BF),
            jax.ShapeDtypeStruct((rows, experts), F32),
        ],
        scratch_shapes=[pltpu.VMEM((rows, width), F32)]
        + [pltpu.VMEM((rows, units), F32)] * 3
        + [pltpu.VMEM((rows, units), BF)] * 2,
        compiler_params=pltpu.CompilerParams(vmem_limit_bytes=VMEM_LIMIT),
        cost_estimate=pl.CostEstimate(
            flops=16 * here * rows * width * units,
            bytes_accessed=12 * here * n_row * depth * units + 12 * rows * width,
            transcendentals=here * rows * units,
        ),
        name="experts",
    )(*operands)


def down_kernel(n_col, hid_a, hid_b, w_a, w_b, out_ref, acc):
    step = pl.program_id(0)
    half = pl.num_programs(0) // 2
    rows, width = acc.shape
    part = width // n_col

    @pl.when(step == 0)
    def _():
        acc[...] = jnp.zeros_like(acc)

    def add(hid, weight):
        w_down = weight[:, 0, 0].reshape(width, weight.shape[-1])
        for s in range(n_col):
            cols = slice(s * part, (s + 1) * part)
            acc[:, cols] += dot_nt(hid[0], w_down[cols, :])

    pl.when(step < half)(lambda: add(hid_a, w_a))
    pl.when(step >= half)(lambda: add(hid_b, w_b))

    @pl.when(step == 2 * half - 1)
    def _():
        for s in range(n_col):
            out_ref[s] = acc[:, s * part : (s + 1) * part].astype(BF)


def down(hid_a, hid_b, weights_a, weights_b):
    half, rows, units = hid_a.shape
    n_row, _, _, depth, _ = weights_a.shape
    width = n_row * depth
    n_col = lax.axis_size("col")
    low = lambda e: jnp.minimum(e, half - 1)
    high = lambda e: jnp.maximum(e - half, 0)
    return pl.pallas_call(
        functools.partial(down_kernel, n_col),
        grid=(2 * half,),
        in_specs=[
            pl.BlockSpec((1, rows, units), lambda e: (low(e), 0, 0)),
            pl.BlockSpec((1, rows, units), lambda e: (high(e), 0, 0)),
            pl.BlockSpec((n_row, 1, 1, depth, units), lambda e: (0, low(e), 2, 0, 0)),
            pl.BlockSpec((n_row, 1, 1, depth, units), lambda e: (0, high(e), 2, 0, 0)),
        ],
        out_specs=pl.BlockSpec((n_col, rows, width // n_col), lambda e: (0, 0, 0)),
        out_shape=jax.ShapeDtypeStruct((n_col, rows, width // n_col), BF),
        scratch_shapes=[pltpu.VMEM((rows, width), F32)],
        compiler_params=pltpu.CompilerParams(vmem_limit_bytes=VMEM_LIMIT),
        cost_estimate=pl.CostEstimate(
            flops=4 * half * rows * width * units,
            bytes_accessed=4 * half * (width + rows) * units + 2 * rows * width,
            transcendentals=0,
        ),
        name="down",
    )(hid_a, hid_b, weights_a, weights_b)


def pack_experts(w_gate, w_up, w_down, first, last):
    pick = lambda w: jnp.transpose(w[:, first:last], (1, 0, 2))
    return row_major(jnp.stack([pick(w_gate), pick(w_up), pick(w_down)], axis=1))


def shards(
    tokens, norm_attn, norm_query, norm_key, norm_moe, w_query, w_key, w_value, w_out, w_router,
    w_gate, w_up, w_down, routes, span_starts, cotangent,
):
    rows, part = tokens.shape
    n_col = lax.axis_size("col")
    me = lax.axis_index("col")
    width = part * n_col
    experts = w_gate.shape[1]
    half = experts // 2
    cols = w_router.shape[1]

    pad = (-(4 * part + cols)) % 128
    mats = jnp.concatenate(
        [w_query, w_key, w_value, w_out, w_router, jnp.zeros((w_router.shape[0], pad), BF)], axis=1
    )
    mats = lax.all_gather(mats, "row", axis=0, tiled=True)
    full_qkv = mats[:, : 3 * part]
    full_out = mats[:, 3 * part : 4 * part]
    first_half = lax.all_gather(pack_experts(w_gate, w_up, w_down, 0, half), "row", axis=0)
    second_half = lax.all_gather(pack_experts(w_gate, w_up, w_down, half, experts), "row", axis=0)

    below = jnp.broadcast_to(norm_attn.reshape(1, part), (16, part))
    spread = gather_line(jnp.concatenate([tokens, below], axis=0))
    token_values = jnp.transpose(spread[:, :rows], (1, 0, 2)).reshape(rows, width).astype(F32)
    attn_gain = spread[:, rows].reshape(1, width).astype(F32)
    inv_first = lax.rsqrt(jnp.mean(token_values * token_values, axis=1, keepdims=True) + EPSILON)
    normed_attn = (token_values * inv_first * attn_gain).astype(BF)
    grad_blocks = gather_line(after(cotangent, spread))
    qkv = dot_nn(normed_attn, full_qkv)
    query_raw, key_raw = qkv[:, :part], qkv[:, part : 2 * part]

    squares = sum_small(
        jnp.stack([jnp.sum(query_raw * query_raw, axis=1), jnp.sum(key_raw * key_raw, axis=1)])
    )
    inv_qk = lax.rsqrt(squares / width + EPSILON)
    query_inv, key_inv = inv_qk[0][:, None], inv_qk[1][:, None]
    query_gain, key_gain = norm_query.reshape(1, part), norm_key.reshape(1, part)
    cosine, sine = rope_tables(rows)
    span_of = span_ids(span_starts[0], rows)
    span_row, span_col = span_of[None, :], span_of[:, None]
    queries, keys, values, mixed = attend(
        qkv, query_inv, key_inv, query_gain, key_gain, cosine, sine, span_row, span_col
    )

    attn_parts = dot_nt(mixed, full_out)
    attn = scatter_line(
        lambda s: lax.dynamic_slice_in_dim(attn_parts, s * part, part, 1)
    )
    local_tokens = tokens.astype(F32)
    hidden_state = local_tokens + after(attn, grad_blocks)
    moe_gain = norm_moe.astype(F32).reshape(1, part)
    hidden_square = sum_small(jnp.sum(hidden_state * hidden_state, axis=1)[None])
    inv_second = lax.rsqrt(hidden_square[0][:, None] / width + EPSILON)
    flat = lambda blocks: jnp.transpose(blocks, (1, 0, 2)).reshape(rows, width)
    turn = lambda blocks: jnp.transpose(blocks, (0, 2, 1)).reshape(width, rows)
    moe_blocks = gather_line((hidden_state * inv_second * moe_gain).astype(BF))
    normed_moe, normed_moe_t = flat(moe_blocks), turn(moe_blocks)
    grad_full, grad_full_t = flat(grad_blocks), turn(grad_blocks)

    router_t = gather_small(mats[:, 4 * part : 4 * part + cols].T).reshape(experts, width)
    router_probs = jax.nn.softmax(dot_nt(normed_moe, router_t), axis=1)
    expert_ids = jnp.arange(experts, dtype=jnp.int32)
    routed = jnp.any(routes[:, :, None] == expert_ids[None, None, :], axis=1)
    gate_table = jnp.where(routed, router_probs, 0.0)

    dx_a, dw_a, hid_a, dg_a = moe_half(
        0, normed_moe, normed_moe_t, grad_full, grad_full_t, gate_table, first_half, None
    )
    dx_b, dw_b, hid_b, dg_b = moe_half(
        half, normed_moe, normed_moe_t, grad_full, grad_full_t, gate_table, second_half,
        (router_probs, dg_a, router_t),
    )
    summed_a = lax.psum_scatter(dw_a, "row", scatter_dimension=0)
    summed_b = lax.psum_scatter(dw_b, "row", scatter_dimension=0)

    pick = lambda blocks, s: lax.dynamic_index_in_dim(blocks, s, 0, keepdims=False).astype(F32)
    dx_b = after(dx_b, summed_a)
    moe_in_grad = scatter_line(lambda s: pick(dx_a, s) + pick(dx_b, s))
    moe_stat = sum_small(jnp.sum(moe_in_grad * moe_gain * hidden_state, axis=1)[None])[0][:, None]
    d_moe_gain = jnp.sum(moe_in_grad * hidden_state * inv_second, axis=0)
    hidden_grad = (
        cotangent.astype(F32)
        + inv_second * moe_gain * moe_in_grad
        - inv_second**3 * hidden_state * moe_stat / width
    )
    attn_grad = flat(gather_line(hidden_grad.astype(BF)))
    mixed_grad = dot_nn(attn_grad, full_out).astype(BF)
    d_out_w = dot_tn(attn_grad, mixed)

    query_turned, key_turned, value_grad = attend_back(
        queries, keys, values, after(mixed_grad, summed_b), cosine, sine, span_row, span_col
    )
    query_scaled = query_turned * query_gain.astype(F32)
    key_scaled = key_turned * key_gain.astype(F32)
    stats = sum_small(
        jnp.stack(
            [jnp.sum(query_scaled * query_raw, axis=1), jnp.sum(key_scaled * key_raw, axis=1)]
        )
    )
    d_query_gain = jnp.sum(query_turned * query_raw * query_inv, axis=0)
    d_key_gain = jnp.sum(key_turned * key_raw * key_inv, axis=0)
    query_raw_grad = (
        query_inv * query_scaled - query_inv**3 * query_raw * stats[0][:, None] / width
    ).astype(BF)
    key_raw_grad = (
        key_inv * key_scaled - key_inv**3 * key_raw * stats[1][:, None] / width
    ).astype(BF)
    qkv_grad = jnp.concatenate([query_raw_grad, key_raw_grad, value_grad], axis=1)
    attn_in_terms = dot_nt(qkv_grad, full_qkv)
    d_qkv_w = dot_tn(normed_attn, qkv_grad)

    gate_grad = jnp.where(routed, sum_small(dg_b.T).T, 0.0)
    logit_low = (
        router_probs * (gate_grad - jnp.sum(router_probs * gate_grad, axis=1, keepdims=True))
    ).astype(BF)
    d_router_w = dot_tn(normed_moe, lax.dynamic_slice_in_dim(logit_low, me * cols, cols, 1))

    d_out_mats = jnp.concatenate(
        [d_out_w.astype(BF), d_router_w.astype(BF), jnp.zeros((width, -cols % 128), BF)], axis=1
    )
    summed_out = lax.psum_scatter(
        after(row_major(d_out_mats), summed_b), "row", scatter_dimension=0, tiled=True
    ).astype(F32)
    summed_qkv = lax.psum_scatter(
        after(row_major(d_qkv_w.astype(BF)), summed_out), "row", scatter_dimension=0, tiled=True
    ).astype(F32)

    attn_in_grad = scatter_line(
        lambda s: lax.dynamic_slice_in_dim(attn_in_terms, s * part, part, 1)
    )
    local_gain = norm_attn.astype(F32).reshape(1, part)
    attn_stat = sum_small(jnp.sum(attn_in_grad * local_gain * local_tokens, axis=1)[None])
    d_attn_gain = jnp.sum(attn_in_grad * local_tokens * inv_first, axis=0)
    d_tokens = (
        hidden_grad
        + inv_first * local_gain * attn_in_grad
        - inv_first**3 * local_tokens * attn_stat[0][:, None] / width
    )

    moe_parts = down(hid_a, hid_b, first_half, second_half)
    output = (hidden_state + scatter_line(lambda s: pick(moe_parts, s))).astype(BF)

    gains = lax.psum(jnp.stack([d_attn_gain, d_query_gain, d_key_gain, d_moe_gain]), "row")
    expert_grads = jnp.concatenate([summed_a, summed_b], axis=0)
    unpack = lambda i: jnp.transpose(expert_grads[:, i], (1, 0, 2)).astype(F32)
    cut = lambda i: summed_qkv[:, i * part : (i + 1) * part]
    return (
        output, d_tokens, gains[0], gains[1], gains[2], gains[3],
        cut(0), cut(1), cut(2), summed_out[:, :part], summed_out[:, part : part + cols],
        unpack(0), unpack(1), unpack(2),
    )


def solution(mesh):
    grid = P("row", "col")
    cube = P("row", None, "col")
    rows = P("row", None)
    line = P("col")
    in_specs = (
        grid, line, line, line, line, grid, grid, grid, grid, grid,
        cube, cube, cube, rows, rows, grid,
    )
    out_specs = (
        grid, grid, line, line, line, line, grid, grid, grid, grid, grid, cube, cube, cube,
    )
    return jax.shard_map(shards, mesh=mesh, in_specs=in_specs, out_specs=out_specs, check_vma=False)
```

time: 4140 us -> 1260 us (0.30)
  waiting for transfers between devices: 1540 us -> 466 us
  local copies, waits for them, and re-layouts: 894 us -> 97.3 us
  other arithmetic: 891 us -> 101 us
  matrix products: 592 us -> 49.6 us
  Pallas kernels: 0 us -> 326 us
  starting transfers between devices: 1.19 us -> 187 us
  blocking collectives: 122 us -> 12.1 us
  loops' own time: 72.8 us -> 0 us
    reduce_scatter x11 -> x4, waiting for transfers between devices: 984 us -> 24.2 us  [the longest x1 24.2 us: shards(): summed_a = lax.psum_scatter(dw_a, 'row', scatter_dimension=0)]
    scatter-add x32 -> x0, other arithmetic: 720 us -> none  [the longest x16 376 us: expert_backward(): input_acc = input_acc.at[slot_tokens].add(input_rows)]
    gather x66 -> x0, local copies, waits for them, and re-layouts: 573 us -> none  [the longest x16 145 us: expert_forward(): chosen = padded_rows[slot_tokens]]
    dot_general x127 -> x8, matrix products: 587 us -> 49.6 us  [the longest x3 17.1 us: dot_tn(): lax.dot_general(a, b, (((0,), (0,)), ((), ())), preferred_element_type=F32)]
    all_gather x11 -> x3, waiting for transfers between devices: 525 us -> 0.02 us  [the longest x1 0.02 us: shards(): lax.all_gather(pack_experts(w_gate, w_up, w_down, half, experts), 'row',...]
    ppermute x0 -> x69, waiting for transfers between devices: none -> 442 us  [the longest x12 116 us: gather_line(): from_right.append(lax.ppermute(from_right[-1], 'col', to_left))]
    pallas_call x0 -> x5, Pallas kernels: none -> 326 us  [the longest x2 258 us: moe_half(): pl.pallas_call(functools.partial(moe_kernel, first, n_col, closing is not...]
    ppermute x0 -> x69, starting transfers between devices: none -> 186 us  [the longest x12 69.6 us: gather_line(): from_left.append(lax.ppermute(from_left[-1], 'col', to_right))]
  transfers between devices with their start and end apart: 24 -> 76, of which waited for: 18 -> 42; matrix products, arithmetic and copies ran while one was open for 15% -> 18% of each run, Pallas kernels for 0% -> 26%
where the time goes in v1:
time: 1260 us
  waiting for transfers between devices  466 us (37%)
  Pallas kernels  326 us (26%)
  starting transfers between devices  187 us (15%)
  other arithmetic  101 us (8%)
  local copies, waits for them, and re-layouts  97.3 us (8%)
  matrix products  49.6 us (4%)
  between operations  15.9 us (1%)
    pallas_call x2, Pallas kernels, moe_half(): pl.pallas_call(functools.partial(moe_kernel, first, n_col, closing is not...  258 us
    ppermute x12, waiting for transfers between devices, gather_line(): from_right.append(lax.ppermute(from_right[-1], 'col', to_left))  116 us
    ppermute x12, waiting for transfers between devices, scatter_line(): right = lax.ppermute(go_right.astype(BF), 'col', to_right)  107 us
    ppermute x12, starting transfers between devices, gather_line(): from_left.append(lax.ppermute(from_left[-1], 'col', to_right))  69.6 us
    ppermute x12, waiting for transfers between devices, scatter_line(): left = lax.ppermute(go_left.astype(BF), 'col', to_left)  65.5 us
    ppermute x18, waiting for transfers between devices, sum_small(): lax.ppermute(values, 'col', [(i, (i + k) % n) for i in range(n)])  59.1 us
    ppermute x12, starting transfers between devices, scatter_line(): right = lax.ppermute(go_right.astype(BF), 'col', to_right)  50.5 us
    ppermute x12, waiting for transfers between devices, gather_line(): from_left.append(lax.ppermute(from_left[-1], 'col', to_right))  48.5 us
  transfers between devices with their start and end apart: 76, of which 42 were waited for; matrix products, arithmetic and copies ran while one was open for 18% of the time, Pallas kernels for 26%

profile of v1, /device:TPU:0, one launch (start us, length us, event | category | flops | bytes accessed | tf_op | source)
XLA Modules:
  0.0 1255.7 jit_solution(14891918423695477656)
XLA Ops:
  25.0 6.7 collective-permute-start
  31.6 20.7 %collective-permute-done.1 = bf16[1040,512]{1,0:T(8,128)(2,1)S(1)} collective-permute-done((bf16[1040,512]{1,0:T(8,128)(2,1)}, bf16[1040,512]{1,0:T(8,128)(2,1)S(1)}, u32[]{:S(2)}, u32[]{:S(2)}) %collective-permute-start.1) | collective-permute-done | bytes 1064992 | tf_op jit(solution)/shard_map/ppermute | solution.py:54
  53.7 5.6 collective-permute-start.4
  61.2 17.9 %collective-permute-done.2 = bf16[1040,512]{1,0:T(8,128)(2,1)} collective-permute-done((bf16[1040,512]{1,0:T(8,128)(2,1)S(1)}, bf16[1040,512]{1,0:T(8,128)(2,1)}, u32[]{:S(2)}, u32[]{:S(2)}) %collective-permute-start.2) | collective-permute-done | bytes 1064992 | tf_op jit(solution)/shard_map/ppermute | solution.py:54
  85.4 6.0 collective-permute-start.5
  93.7 11.5 collective-permute-done.3
  131.7 10.5 fusion.4.q_ref.k_ref.v_ref
  158.8 16.7 %attend.1 = (bf16[1024,512]{1,0:T(8,128)(2,1)}, bf16[1024,512]{1,0:T(8,128)(2,1)}, bf16[1024,512]{1,0:T(8,128)(2,1)}, bf16[1024,512]{1,0:T(8,128)(2,1)}) custom-call(f32[1024,1536]{1,0:T(8,128)} %copy-done, f32[1024,1536]{1,0:T(8,128)} %copy-done, f32[1024,1536]{1,0:T(8,128)} %copy-done, f32[1024,1]{1,0:T(8,128)} %copy.225.iq_ref, f32[1024,1]{1,0:T(8,128)} %copy.226.ik_ref, ...), custom_call_target="tpu_custom_call" | custom-call | flops 2147483648 | bytes 10485760 | tf_op jit(solution)/shard_map/attend/pallas_call | solution.py:148
  188.5 5.5 collective-permute-start.15
  195.3 14.2 %collective-permute-done.9 = bf16[1024,512]{1,0:T(8,128)(2,1)} collective-permute-done((bf16[1024,512]{1,0:T(8,128)(2,1)}, bf16[1024,512]{1,0:T(8,128)(2,1)}, u32[]{:S(2)}, u32[]{:S(2)}) %collective-permute-start.9) | collective-permute-done | bytes 1048608 | tf_op jit(solution)/shard_map/ppermute | solution.py:74
  219.7 12.2 collective-permute-done.15
  231.9 5.5 collective-permute-start.19
  238.6 15.9 %collective-permute-done.10 = bf16[1024,512]{1,0:T(8,128)(2,1)} collective-permute-done((bf16[1024,512]{1,0:T(8,128)(2,1)}, bf16[1024,512]{1,0:T(8,128)(2,1)}, u32[]{:S(2)}, u32[]{:S(2)}) %collective-permute-start.10) | collective-permute-done | bytes 1048608 | tf_op jit(solution)/shard_map/ppermute | solution.py:74
  262.0 10.5 collective-permute-done.19
  279.8 7.6 collective-permute-done.13
  291.6 18.3 %collective-permute-done.18 = bf16[1024,512]{0,1:T(8,128)(2,1)} collective-permute-done((bf16[1024,512]{0,1:T(8,128)(2,1)}, bf16[1024,512]{0,1:T(8,128)(2,1)}, u32[]{:S(2)}, u32[]{:S(2)}) %collective-permute-start.18) | collective-permute-done | bytes 1048608 | tf_op jit(solution)/shard_map/ppermute | solution.py:54
  337.2 15.6 %collective-permute-done.24 = bf16[1024,512]{1,0:T(8,128)(2,1)} collective-permute-done((bf16[1024,512]{1,0:T(8,128)(2,1)S(1)}, bf16[1024,512]{1,0:T(8,128)(2,1)}, u32[]{:S(2)}, u32[]{:S(2)}) %collective-permute-start.24) | collective-permute-done | bytes 1048608 | tf_op jit(solution)/shard_map/ppermute | solution.py:53
  352.8 5.6 collective-permute-start.28
  358.8 6.6 copy.263.y_ref
  374.2 45.9 %collective-permute-done.31 = bf16[4,2048]{0,1:T(8,128)(2,1)} collective-permute-done((bf16[4,2048]{0,1:T(8,128)(2,1)S(1)}, bf16[4,2048]{0,1:T(8,128)(2,1)}, u32[]{:S(2)}, u32[]{:S(2)}) %collective-permute-start.31) | collective-permute-done | bytes 16416 | tf_op jit(solution)/shard_map/ppermute | solution.py:93
  438.8 8.8 collective-permute-done.27
  454.9 6.4 copy.262.x_ref
  466.1 127.3 %experts.2 = (bf16[4,1024,512]{2,1,0:T(8,128)(2,1)}, bf16[8,8,3,256,256]{4,3,2,1,0:T(8,128)(2,1)}, bf16[8,1024,256]{2,1,0:T(8,128)(2,1)}, f32[1024,16]{1,0:T(8,128)}) custom-call(bf16[1024,2048]{1,0:T(8,128)(2,1)} %copy.262.x_ref, bf16[2048,1024]{1,0:T(8,128)(2,1)} %bitcast.26.xt_ref, bf16[1024,2048]{1,0:T(8,128)(2,1)} %copy.263.y_ref, ...), custom_call_target="tpu_custom_call" | custom-call | flops 68719476736 | bytes 75497472 | tf_op jit(solution)/shard_map/experts/pallas_call | solution.py:308
  593.5 131.0 %experts.3 = (bf16[4,1024,512]{2,1,0:T(8,128)(2,1)}, bf16[8,8,3,256,256]{4,3,2,1,0:T(8,128)(2,1)}, bf16[8,1024,256]{2,1,0:T(8,128)(2,1)}, f32[1024,16]{1,0:T(8,128)}) custom-call(bf16[1024,2048]{1,0:T(8,128)(2,1)} %copy.262.x_ref, bf16[2048,1024]{1,0:T(8,128)(2,1)} %bitcast.26.xt_ref, bf16[1024,2048]{1,0:T(8,128)(2,1)} %copy.263.y_ref, ...), custom_call_target="tpu_custom_call" | custom-call | flops 68719476736 | bytes 75497472 | tf_op jit(solution)/shard_map/experts/pallas_call | solution.py:308
  724.6 24.2 %reduce-scatter.5.cloned.1.call-done = bf16[1,8,3,256,256]{4,3,2,1,0:T(8,128)(2,1)} async-done(((bf16[8,8,3,256,256]{4,3,2,1,0:T(8,128)(2,1)}), bf16[1,8,3,256,256]{4,3,2,1,0:T(8,128)(2,1)}) %reduce-scatter.5.cloned.1.call-update) | async-done | bytes 3145744 | tf_op jit(solution)/shard_map/reduce_scatter | solution.py:467
  757.2 29.9 %down.1 = bf16[4,1024,512]{2,1,0:T(8,128)(2,1)} custom-call(bf16[8,1024,256]{2,1,0:T(8,128)(2,1)} %get-tuple-element.38.hid_a, bf16[8,1024,256]{2,1,0:T(8,128)(2,1)} %get-tuple-element.40.hid_b, bf16[8,8,3,256,256]{4,3,2,1,0:T(8,128)(2,1)} %bitcast.267, bf16[8,8,3,256,256]{4,3,2,1,0:T(8,128)(2,1)} %bitcast.269), custom_call_target="tpu_custom_call" | custom-call | flops 17179869184 | bytes 29360128 | tf_op jit(solution)/shard_map/down/pallas_call | solution.py:367
  803.8 12.4 collective-permute-done.33
  819.0 5.4 collective-permute-start.34
  824.3 14.3 %collective-permute-done.40 = bf16[1024,512]{1,0:T(8,128)(2,1)S(1)} collective-permute-done((bf16[1024,512]{1,0:T(8,128)(2,1)}, bf16[1024,512]{1,0:T(8,128)(2,1)S(1)}, u32[]{:S(2)}, u32[]{:S(2)}) %collective-permute-start.40) | collective-permute-done | bytes 1048608 | tf_op jit(solution)/shard_map/ppermute | solution.py:74
  843.6 15.5 %collective-permute-done.34 = bf16[1024,512]{1,0:T(8,128)(2,1)} collective-permute-done((bf16[1024,512]{1,0:T(8,128)(2,1)}, bf16[1024,512]{1,0:T(8,128)(2,1)}, u32[]{:S(2)}, u32[]{:S(2)}) %collective-permute-start.34) | collective-permute-done | bytes 1048608 | tf_op jit(solution)/shard_map/ppermute | solution.py:74
  874.2 15.9 %collective-permute-done.37 = bf16[1024,512]{1,0:T(8,128)(2,1)S(1)} collective-permute-done((bf16[1024,512]{1,0:T(8,128)(2,1)S(1)}, bf16[1024,512]{1,0:T(8,128)(2,1)S(1)}, u32[]{:S(2)}, u32[]{:S(2)}) %collective-permute-start.37) | collective-permute-done | bytes 1048608 | tf_op jit(solution)/shard_map/ppermute | solution.py:75
  891.8 20.7 %collective-permute-done.44 = bf16[1024,512]{1,0:T(8,128)(2,1)S(1)} collective-permute-done((bf16[1024,512]{1,0:T(8,128)(2,1)S(1)}, bf16[1024,512]{1,0:T(8,128)(2,1)S(1)}, u32[]{:S(2)}, u32[]{:S(2)}) %collective-permute-start.44) | collective-permute-done | bytes 1048608 | tf_op jit(solution)/shard_map/ppermute | solution.py:75
  918.1 15.5 %collective-permute-done.47 = f32[1,1024]{1,0:T(1,128)S(1)} collective-permute-done((f32[1,1024]{1,0:T(1,128)S(1)}, f32[1,1024]{1,0:T(1,128)S(1)}, u32[]{:S(2)}, u32[]{:S(2)}) %collective-permute-start.47) | collective-permute-done | bytes 4128 | tf_op jit(solution)/shard_map/ppermute | solution.py:83
  939.5 5.5 collective-permute-start.48
  945.1 18.5 %collective-permute-done.49 = bf16[1024,512]{1,0:T(8,128)(2,1)S(1)} collective-permute-done((bf16[1024,512]{1,0:T(8,128)(2,1)S(1)}, bf16[1024,512]{1,0:T(8,128)(2,1)S(1)}, u32[]{:S(2)}, u32[]{:S(2)}) %collective-permute-start.49) | collective-permute-done | bytes 1048608 | tf_op jit(solution)/shard_map/ppermute | solution.py:54
  964.8 5.6 collective-permute-start.52
  973.2 20.3 %collective-permute-done.50 = bf16[1024,512]{1,0:T(8,128)(2,1)} collective-permute-done((bf16[1024,512]{1,0:T(8,128)(2,1)S(1)}, bf16[1024,512]{1,0:T(8,128)(2,1)}, u32[]{:S(2)}, u32[]{:S(2)}) %collective-permute-start.50) | collective-permute-done | bytes 1048608 | tf_op jit(solution)/shard_map/ppermute | solution.py:54
  994.8 30.1 %collective-permute-done.67 = f32[16,1024]{0,1:T(8,128)} collective-permute-done((f32[16,1024]{0,1:T(8,128)S(1)}, f32[16,1024]{0,1:T(8,128)}, u32[]{:S(2)}, u32[]{:S(2)}) %collective-permute-start.67) | collective-permute-done | bytes 65568 | tf_op jit(solution)/shard_map/ppermute | solution.py:83
  1027.1 14.7 %collective-permute-start.53 = (bf16[1024,512]{1,0:T(8,128)(2,1)}, bf16[1024,512]{1,0:T(8,128)(2,1)}, u32[]{:S(2)}, u32[]{:S(2)}) collective-permute-start(bf16[1024,512]{1,0:T(8,128)(2,1)} %collective-permute-done.52), channel_id=1, source_target_pairs={{0,1},{1,2},{2,3},{4,5},{5,6},{6,7},{8,9},{9,10},{10,11},{12,13},{... | collective-permute-start | bytes 3145736 | tf_op jit(solution)/shard_map/ppermute | solution.py:53
  1070.6 6.2 fusion.33.d_ref
  1076.8 21.5 %attend_back.1 = (f32[1024,512]{1,0:T(8,128)}, f32[1024,512]{1,0:T(8,128)}, bf16[1024,512]{1,0:T(8,128)(2,1)}) custom-call(bf16[1024,512]{1,0:T(8,128)(2,1)} %get-tuple-element.45.q_ref, bf16[1024,512]{1,0:T(8,128)(2,1)} %get-tuple-element.46.k_ref, bf16[1024,512]{1,0:T(8,128)(2,1)} %get-tuple-element.47.v_ref, bf16[1024,512]{1,0:T(8,128)(2,1)} %fusion.33.d_ref, ...), custom_call_target="tpu_custom_call" | custom-call | flops 5368709120 | bytes 10485760 | tf_op jit(solution)/shard_map/attend_back/pallas_call | solution.py:204
  1117.3 8.9 convolution_convert_fusion
  1127.4 8.8 fusion.2
  1139.7 17.2 %collective-permute-done.57 = bf16[1024,512]{1,0:T(8,128)(2,1)S(1)} collective-permute-done((bf16[1024,512]{1,0:T(8,128)(2,1)S(1)}, bf16[1024,512]{1,0:T(8,128)(2,1)S(1)}, u32[]{:S(2)}, u32[]{:S(2)}) %collective-permute-start.57) | collective-permute-done | bytes 1048608 | tf_op jit(solution)/shard_map/ppermute | solution.py:74
  1161.8 15.2 %collective-permute-done.58 = bf16[1024,512]{1,0:T(8,128)(2,1)S(1)} collective-permute-done((bf16[1024,512]{1,0:T(8,128)(2,1)S(1)}, bf16[1024,512]{1,0:T(8,128)(2,1)S(1)}, u32[]{:S(2)}, u32[]{:S(2)}) %collective-permute-start.58) | collective-permute-done | bytes 1048608 | tf_op jit(solution)/shard_map/ppermute | solution.py:74
  1180.0 6.3 collective-permute-start.59
  1186.3 14.7 %collective-permute-done.61 = bf16[1024,512]{1,0:T(8,128)(2,1)S(1)} collective-permute-done((bf16[1024,512]{1,0:T(8,128)(2,1)S(1)}, bf16[1024,512]{1,0:T(8,128)(2,1)S(1)}, u32[]{:S(2)}, u32[]{:S(2)}) %collective-permute-start.61) | collective-permute-done | bytes 1048608 | tf_op jit(solution)/shard_map/ppermute | solution.py:75
  1230.0 12.1 psum.7
  (387 shorter events, 348.1 us)
Async XLA Ops:
  7.2 124.5 %all-gather.6.cloned.1.call-start = ((), (), s32[]{:S(2)}) async-start(), calls=%async_computation.4 | async-start | bytes 10027008 | tf_op jit(solution)/shard_map/all_gather | solution.py:410
  11.5 454.7 %all-gather.8.cloned.1.call-start = ((), (), s32[]{:S(2)}) async-start(), calls=%async_computation.9 | async-start | bytes 28311552 | tf_op jit(solution)/shard_map/all_gather | solution.py:413
  17.4 576.1 %all-gather.10.cloned.1.call-start = ((), (), s32[]{:S(2)}) async-start(), calls=%async_computation.10 | async-start | bytes 28311552 | tf_op jit(solution)/shard_map/all_gather | solution.py:414
  20.2 728.5 %reduce-scatter.5.cloned.1.call-start = ((), (), s32[]{:S(2)}) async-start(), calls=%async_computation.5 | async-start | bytes 28311552 | tf_op jit(solution)/shard_map/reduce_scatter | solution.py:467
  23.7 28.7 %collective-permute-start.1 = (bf16[1040,512]{1,0:T(8,128)(2,1)}, bf16[1040,512]{1,0:T(8,128)(2,1)S(1)}, u32[]{:S(2)}, u32[]{:S(2)}) collective-permute-start(bf16[1040,512]{1,0:T(8,128)(2,1)} %copy.219), channel_id=1, source_target_pairs={{1,0},{2,1},{3,2},{5,4},{6,5},{7,6},{9,8},{10,9},{11,10},{13,12},{... | collective-permute-start | bytes 3194888 | tf_op jit(solution)/shard_map/ppermute | solution.py:54
  25.0 28.7 %collective-permute-start = (bf16[1040,512]{1,0:T(8,128)(2,1)}, bf16[1040,512]{1,0:T(8,128)(2,1)}, u32[]{:S(2)}, u32[]{:S(2)}) collective-permute-start(bf16[1040,512]{1,0:T(8,128)(2,1)} %copy.219), channel_id=1, source_target_pairs={{0,1},{1,2},{2,3},{4,5},{5,6},{6,7},{8,9},{9,10},{10,11},{12,13},{... | collective-permute-start | bytes 3194888 | tf_op jit(solution)/shard_map/ppermute | solution.py:53
  52.4 26.8 %collective-permute-start.2 = (bf16[1040,512]{1,0:T(8,128)(2,1)S(1)}, bf16[1040,512]{1,0:T(8,128)(2,1)}, u32[]{:S(2)}, u32[]{:S(2)}) collective-permute-start(bf16[1040,512]{1,0:T(8,128)(2,1)S(1)} %collective-permute-done.1), channel_id=1, source_target_pairs={{1,0},{2,1},{3,2},{5,4},{6,5},{7,6},{9,8},{10,9},{11,10},{13,12},{... | collective-permute-start | bytes 3194888 | tf_op jit(solution)/shard_map/ppermute | solution.py:54
  53.7 31.7 %collective-permute-start.4 = (bf16[1040,512]{1,0:T(8,128)(2,1)}, bf16[1040,512]{1,0:T(8,128)(2,1)}, u32[]{:S(2)}, u32[]{:S(2)}) collective-permute-start(bf16[1040,512]{1,0:T(8,128)(2,1)} %collective-permute-done), channel_id=1, source_target_pairs={{0,1},{1,2},{2,3},{4,5},{5,6},{6,7},{8,9},{9,10},{10,11},{12,13},{... | collective-permute-start | bytes 3194888 | tf_op jit(solution)/shard_map/ppermute | solution.py:53
  85.4 26.3 %collective-permute-start.5 = (bf16[1040,512]{1,0:T(8,128)(2,1)}, bf16[1040,512]{1,0:T(8,128)(2,1)}, u32[]{:S(2)}, u32[]{:S(2)}) collective-permute-start(bf16[1040,512]{1,0:T(8,128)(2,1)} %collective-permute-done.4), channel_id=1, source_target_pairs={{0,1},{1,2},{2,3},{4,5},{5,6},{6,7},{8,9},{9,10},{10,11},{12,13},{... | collective-permute-start | bytes 3194888 | tf_op jit(solution)/shard_map/ppermute | solution.py:53
  187.2 31.2 %collective-permute-start.16 = (bf16[1024,512]{0,1:T(8,128)(2,1)S(1)}, bf16[1024,512]{0,1:T(8,128)(2,1)}, u32[]{:S(2)}, u32[]{:S(2)}) collective-permute-start(bf16[1024,512]{0,1:T(8,128)(2,1)S(1)} %copy.228), channel_id=1, source_target_pairs={{1,0},{2,1},{3,2},{5,4},{6,5},{7,6},{9,8},{10,9},{11,10},{13,12},{... | collective-permute-start | bytes 3145736 | tf_op jit(solution)/shard_map/ppermute | solution.py:54
  188.5 43.4 %collective-permute-start.15 = (bf16[1024,512]{0,1:T(8,128)(2,1)S(1)}, bf16[1024,512]{0,1:T(8,128)(2,1)}, u32[]{:S(2)}, u32[]{:S(2)}) collective-permute-start(bf16[1024,512]{0,1:T(8,128)(2,1)S(1)} %copy.228), channel_id=1, source_target_pairs={{0,1},{1,2},{2,3},{4,5},{5,6},{6,7},{8,9},{9,10},{10,11},{12,13},{... | collective-permute-start | bytes 3145736 | tf_op jit(solution)/shard_map/ppermute | solution.py:53
  194.0 43.6 %collective-permute-start.12 = (bf16[1024,512]{1,0:T(8,128)(2,1)S(1)}, bf16[1024,512]{1,0:T(8,128)(2,1)S(1)}, u32[]{:S(2)}, u32[]{:S(2)}) collective-permute-start(bf16[1024,512]{1,0:T(8,128)(2,1)S(1)} %get-tuple-element.175), channel_id=1, source_target_pairs={{1,0},{2,1},{3,2},{5,4},{6,5},{7,6},{9,8},{10,9},{11,10},{13,12},{... | collective-permute-start | bytes 3145736 | tf_op jit(solution)/shard_map/ppermute | solution.py:75
  213.2 41.3 %collective-permute-start.10 = (bf16[1024,512]{1,0:T(8,128)(2,1)}, bf16[1024,512]{1,0:T(8,128)(2,1)}, u32[]{:S(2)}, u32[]{:S(2)}) collective-permute-start(bf16[1024,512]{1,0:T(8,128)(2,1)} %add_convert_fusion.9), channel_id=1, source_target_pairs={{0,1},{1,2},{2,3},{4,5},{5,6},{6,7},{8,9},{9,10},{10,11},{12,13},{... | collective-permute-start | bytes 3145736 | tf_op jit(solution)/shard_map/ppermute | solution.py:74
  218.4 42.2 %collective-permute-start.17 = (bf16[1024,512]{0,1:T(8,128)(2,1)}, bf16[1024,512]{0,1:T(8,128)(2,1)}, u32[]{:S(2)}, u32[]{:S(2)}) collective-permute-start(bf16[1024,512]{0,1:T(8,128)(2,1)} %collective-permute-done.16), channel_id=1, source_target_pairs={{1,0},{2,1},{3,2},{5,4},{6,5},{7,6},{9,8},{10,9},{11,10},{13,12},{... | collective-permute-start | bytes 3145736 | tf_op jit(solution)/shard_map/ppermute | solution.py:54
  231.9 40.5 %collective-permute-start.19 = (bf16[1024,512]{0,1:T(8,128)(2,1)}, bf16[1024,512]{0,1:T(8,128)(2,1)}, u32[]{:S(2)}, u32[]{:S(2)}) collective-permute-start(bf16[1024,512]{0,1:T(8,128)(2,1)} %collective-permute-done.15), channel_id=1, source_target_pairs={{0,1},{1,2},{2,3},{4,5},{5,6},{6,7},{8,9},{9,10},{10,11},{12,13},{... | collective-permute-start | bytes 3145736 | tf_op jit(solution)/shard_map/ppermute | solution.py:53
  259.4 28.0 %collective-permute-start.13 = (bf16[1024,512]{1,0:T(8,128)(2,1)S(1)}, bf16[1024,512]{1,0:T(8,128)(2,1)}, u32[]{:S(2)}, u32[]{:S(2)}) collective-permute-start(bf16[1024,512]{1,0:T(8,128)(2,1)S(1)} %get-tuple-element.173), channel_id=1, source_target_pairs={{1,0},{2,1},{3,2},{5,4},{6,5},{7,6},{9,8},{10,9},{11,10},{13,12},{... | collective-permute-start | bytes 3145736 | tf_op jit(solution)/shard_map/ppermute | solution.py:75
  260.7 49.2 %collective-permute-start.18 = (bf16[1024,512]{0,1:T(8,128)(2,1)}, bf16[1024,512]{0,1:T(8,128)(2,1)}, u32[]{:S(2)}, u32[]{:S(2)}) collective-permute-start(bf16[1024,512]{0,1:T(8,128)(2,1)} %collective-permute-done.17), channel_id=1, source_target_pairs={{1,0},{2,1},{3,2},{5,4},{6,5},{7,6},{9,8},{10,9},{11,10},{13,12},{... | collective-permute-start | bytes 3145736 | tf_op jit(solution)/shard_map/ppermute | solution.py:54
  272.4 41.3 %collective-permute-start.20 = (bf16[1024,512]{0,1:T(8,128)(2,1)}, bf16[1024,512]{0,1:T(8,128)(2,1)S(1)}, u32[]{:S(2)}, u32[]{:S(2)}) collective-permute-start(bf16[1024,512]{0,1:T(8,128)(2,1)} %collective-permute-done.19), channel_id=1, source_target_pairs={{0,1},{1,2},{2,3},{4,5},{5,6},{6,7},{8,9},{9,10},{10,11},{12,13},{... | collective-permute-start | bytes 3145736 | tf_op jit(solution)/shard_map/ppermute | solution.py:53
  276.9 40.8 %collective-permute-start.11 = (bf16[1024,512]{1,0:T(8,128)(2,1)S(1)}, bf16[1024,512]{1,0:T(8,128)(2,1)S(1)}, u32[]{:S(2)}, u32[]{:S(2)}) collective-permute-start(bf16[1024,512]{1,0:T(8,128)(2,1)S(1)} %get-tuple-element.172), channel_id=1, source_target_pairs={{0,1},{1,2},{2,3},{4,5},{5,6},{6,7},{8,9},{9,10},{10,11},{12,13},{... | collective-permute-start | bytes 3145736 | tf_op jit(solution)/shard_map/ppermute | solution.py:74
  289.7 33.1 %collective-permute-start.14 = (bf16[1024,512]{1,0:T(8,128)(2,1)S(1)}, bf16[1024,512]{1,0:T(8,128)(2,1)S(1)}, u32[]{:S(2)}, u32[]{:S(2)}) collective-permute-start(bf16[1024,512]{1,0:T(8,128)(2,1)S(1)} %add_convert_fusion.6), channel_id=1, source_target_pairs={{1,0},{2,1},{3,2},{5,4},{6,5},{7,6},{9,8},{10,9},{11,10},{13,12},{... | collective-permute-start | bytes 3145736 | tf_op jit(solution)/shard_map/ppermute | solution.py:75
  335.9 29.5 %collective-permute-start.25 = (bf16[1024,512]{1,0:T(8,128)(2,1)S(1)}, bf16[1024,512]{1,0:T(8,128)(2,1)}, u32[]{:S(2)}, u32[]{:S(2)}) collective-permute-start(bf16[1024,512]{1,0:T(8,128)(2,1)S(1)} %multiply_convert_fusion), channel_id=1, source_target_pairs={{1,0},{2,1},{3,2},{5,4},{6,5},{7,6},{9,8},{10,9},{11,10},{13,12},{... | collective-permute-start | bytes 3145736 | tf_op jit(solution)/shard_map/ppermute | solution.py:54
  352.8 69.8 %collective-permute-start.28 = (bf16[1024,512]{1,0:T(8,128)(2,1)}, bf16[1024,512]{1,0:T(8,128)(2,1)}, u32[]{:S(2)}, u32[]{:S(2)}) collective-permute-start(bf16[1024,512]{1,0:T(8,128)(2,1)} %collective-permute-done.24), channel_id=1, source_target_pairs={{0,1},{1,2},{2,3},{4,5},{5,6},{6,7},{8,9},{9,10},{10,11},{12,13},{... | collective-permute-start | bytes 3145736 | tf_op jit(solution)/shard_map/ppermute | solution.py:53
  365.4 60.9 %collective-permute-start.26 = (bf16[1024,512]{1,0:T(8,128)(2,1)}, bf16[1024,512]{1,0:T(8,128)(2,1)}, u32[]{:S(2)}, u32[]{:S(2)}) collective-permute-start(bf16[1024,512]{1,0:T(8,128)(2,1)} %collective-permute-done.25), channel_id=1, source_target_pairs={{1,0},{2,1},{3,2},{5,4},{6,5},{7,6},{9,8},{10,9},{11,10},{13,12},{... | collective-permute-start | bytes 3145736 | tf_op jit(solution)/shard_map/ppermute | solution.py:54
  367.9 52.2 %collective-permute-start.31 = (bf16[4,2048]{0,1:T(8,128)(2,1)S(1)}, bf16[4,2048]{0,1:T(8,128)(2,1)}, u32[]{:S(2)}, u32[]{:S(2)}) collective-permute-start(bf16[4,2048]{0,1:T(8,128)(2,1)S(1)} %get-tuple-element.162), channel_id=1, source_target_pairs={{0,2},{1,3},{2,0},{3,1},{4,6},{5,7},{6,4},{7,5},{8,10},{9,11},{10,... | collective-permute-start | bytes 49160 | tf_op jit(solution)/shard_map/ppermute | solution.py:93
  370.1 51.3 %collective-permute-start.30 = (bf16[4,2048]{0,1:T(8,128)(2,1)S(1)}, bf16[4,2048]{0,1:T(8,128)(2,1)}, u32[]{:S(2)}, u32[]{:S(2)}) collective-permute-start(bf16[4,2048]{0,1:T(8,128)(2,1)S(1)} %get-tuple-element.162), channel_id=1, source_target_pairs={{0,1},{1,2},{2,3},{3,0},{4,5},{5,6},{6,7},{7,4},{8,9},{9,10},{10,1... | collective-permute-start | bytes 49160 | tf_op jit(solution)/shard_map/ppermute | solution.py:93
  372.0 53.0 %collective-permute-start.32 = (bf16[4,2048]{0,1:T(8,128)(2,1)S(1)}, bf16[4,2048]{0,1:T(8,128)(2,1)}, u32[]{:S(2)}, u32[]{:S(2)}) collective-permute-start(bf16[4,2048]{0,1:T(8,128)(2,1)S(1)} %get-tuple-element.162), channel_id=1, source_target_pairs={{0,3},{1,0},{2,1},{3,2},{4,7},{5,4},{6,5},{7,6},{8,11},{9,8},{10,9... | collective-permute-start | bytes 49160 | tf_op jit(solution)/shard_map/ppermute | solution.py:93
  593.4 477.1 %reduce-scatter.7.cloned.1.call-start = ((), (), s32[]{:S(2)}) async-start(), calls=%async_computation.6 | async-start | bytes 28311552 | tf_op jit(solution)/shard_map/reduce_scatter | solution.py:468
  724.5 401.7 %reduce-scatter.9.cloned.1.call-start = ((), (), s32[]{:S(2)}) async-start(), calls=%async_computation.7 | async-start | bytes 2949120 | tf_op jit(solution)/shard_map/reduce_scatter | solution.py:515
  752.9 41.7 %collective-permute-start.39 = (bf16[1024,512]{1,0:T(8,128)(2,1)}, bf16[1024,512]{1,0:T(8,128)(2,1)}, u32[]{:S(2)}, u32[]{:S(2)}) collective-permute-start(bf16[1024,512]{1,0:T(8,128)(2,1)} %get-tuple-element.170), channel_id=1, source_target_pairs={{0,1},{1,2},{2,3},{4,5},{5,6},{6,7},{8,9},{9,10},{10,11},{12,13},{... | collective-permute-start | bytes 3145736 | tf_op jit(solution)/shard_map/ppermute | solution.py:74
  789.8 26.4 %collective-permute-start.33 = (bf16[1024,512]{1,0:T(8,128)(2,1)}, bf16[1024,512]{1,0:T(8,128)(2,1)}, u32[]{:S(2)}, u32[]{:S(2)}) collective-permute-start(bf16[1024,512]{1,0:T(8,128)(2,1)} %get-tuple-element.183), channel_id=1, source_target_pairs={{0,1},{1,2},{2,3},{4,5},{5,6},{6,7},{8,9},{9,10},{10,11},{12,13},{... | collective-permute-start | bytes 3145736 | tf_op jit(solution)/shard_map/ppermute | solution.py:74
  793.3 31.0 %collective-permute-start.42 = (bf16[1024,512]{1,0:T(8,128)(2,1)}, bf16[1024,512]{1,0:T(8,128)(2,1)S(1)}, u32[]{:S(2)}, u32[]{:S(2)}) collective-permute-start(bf16[1024,512]{1,0:T(8,128)(2,1)} %get-tuple-element.171), channel_id=1, source_target_pairs={{1,0},{2,1},{3,2},{5,4},{6,5},{7,6},{9,8},{10,9},{11,10},{13,12},{... | collective-permute-start | bytes 3145736 | tf_op jit(solution)/shard_map/ppermute | solution.py:75
  798.1 40.6 %collective-permute-start.40 = (bf16[1024,512]{1,0:T(8,128)(2,1)}, bf16[1024,512]{1,0:T(8,128)(2,1)S(1)}, u32[]{:S(2)}, u32[]{:S(2)}) collective-permute-start(bf16[1024,512]{1,0:T(8,128)(2,1)} %fusion.26), channel_id=1, source_target_pairs={{0,1},{1,2},{2,3},{4,5},{5,6},{6,7},{8,9},{9,10},{10,11},{12,13},{... | collective-permute-start | bytes 3145736 | tf_op jit(solution)/shard_map/ppermute | solution.py:74
  802.5 41.2 %collective-permute-start.36 = (bf16[1024,512]{1,0:T(8,128)(2,1)S(1)}, bf16[1024,512]{1,0:T(8,128)(2,1)}, u32[]{:S(2)}, u32[]{:S(2)}) collective-permute-start(bf16[1024,512]{1,0:T(8,128)(2,1)S(1)} %get-tuple-element.184), channel_id=1, source_target_pairs={{1,0},{2,1},{3,2},{5,4},{6,5},{7,6},{9,8},{10,9},{11,10},{13,12},{... | collective-permute-start | bytes 3145736 | tf_op jit(solution)/shard_map/ppermute | solution.py:75
  819.0 40.1 %collective-permute-start.34 = (bf16[1024,512]{1,0:T(8,128)(2,1)}, bf16[1024,512]{1,0:T(8,128)(2,1)}, u32[]{:S(2)}, u32[]{:S(2)}) collective-permute-start(bf16[1024,512]{1,0:T(8,128)(2,1)} %fusion.19), channel_id=1, source_target_pairs={{0,1},{1,2},{2,3},{4,5},{5,6},{6,7},{8,9},{9,10},{10,11},{12,13},{... | collective-permute-start | bytes 3145736 | tf_op jit(solution)/shard_map/ppermute | solution.py:74
  861.2 28.8 %collective-permute-start.37 = (bf16[1024,512]{1,0:T(8,128)(2,1)S(1)}, bf16[1024,512]{1,0:T(8,128)(2,1)S(1)}, u32[]{:S(2)}, u32[]{:S(2)}) collective-permute-start(bf16[1024,512]{1,0:T(8,128)(2,1)S(1)} %get-tuple-element.182), channel_id=1, source_target_pairs={{1,0},{2,1},{3,2},{5,4},{6,5},{7,6},{9,8},{10,9},{11,10},{13,12},{... | collective-permute-start | bytes 3145736 | tf_op jit(solution)/shard_map/ppermute | solution.py:75
  862.5 29.3 %collective-permute-start.41 = (bf16[1024,512]{1,0:T(8,128)(2,1)S(1)}, bf16[1024,512]{1,0:T(8,128)(2,1)S(1)}, u32[]{:S(2)}, u32[]{:S(2)}) collective-permute-start(bf16[1024,512]{1,0:T(8,128)(2,1)S(1)} %get-tuple-element.168), channel_id=1, source_target_pairs={{0,1},{1,2},{2,3},{4,5},{5,6},{6,7},{8,9},{9,10},{10,11},{12,13},{... | collective-permute-start | bytes 3145736 | tf_op jit(solution)/shard_map/ppermute | solution.py:74
  868.1 44.4 %collective-permute-start.44 = (bf16[1024,512]{1,0:T(8,128)(2,1)S(1)}, bf16[1024,512]{1,0:T(8,128)(2,1)S(1)}, u32[]{:S(2)}, u32[]{:S(2)}) collective-permute-start(bf16[1024,512]{1,0:T(8,128)(2,1)S(1)} %fusion.25), channel_id=1, source_target_pairs={{1,0},{2,1},{3,2},{5,4},{6,5},{7,6},{9,8},{10,9},{11,10},{13,12},{... | collective-permute-start | bytes 3145736 | tf_op jit(solution)/shard_map/ppermute | solution.py:75
  869.6 66.2 %collective-permute-start.35 = (bf16[1024,512]{1,0:T(8,128)(2,1)S(1)}, bf16[1024,512]{1,0:T(8,128)(2,1)S(1)}, u32[]{:S(2)}, u32[]{:S(2)}) collective-permute-start(bf16[1024,512]{1,0:T(8,128)(2,1)S(1)} %get-tuple-element.181), channel_id=1, source_target_pairs={{0,1},{1,2},{2,3},{4,5},{5,6},{6,7},{8,9},{9,10},{10,11},{12,13},{... | collective-permute-start | bytes 3145736 | tf_op jit(solution)/shard_map/ppermute | solution.py:74
  890.4 45.4 %collective-permute-start.38 = (bf16[1024,512]{1,0:T(8,128)(2,1)S(1)}, bf16[1024,512]{1,0:T(8,128)(2,1)S(1)}, u32[]{:S(2)}, u32[]{:S(2)}) collective-permute-start(bf16[1024,512]{1,0:T(8,128)(2,1)S(1)} %fusion.18), channel_id=1, source_target_pairs={{1,0},{2,1},{3,2},{5,4},{6,5},{7,6},{9,8},{10,9},{11,10},{13,12},{... | collective-permute-start | bytes 3145736 | tf_op jit(solution)/shard_map/ppermute | solution.py:75
  963.5 30.0 %collective-permute-start.50 = (bf16[1024,512]{1,0:T(8,128)(2,1)S(1)}, bf16[1024,512]{1,0:T(8,128)(2,1)}, u32[]{:S(2)}, u32[]{:S(2)}) collective-permute-start(bf16[1024,512]{1,0:T(8,128)(2,1)S(1)} %collective-permute-done.49), channel_id=1, source_target_pairs={{1,0},{2,1},{3,2},{5,4},{6,5},{7,6},{9,8},{10,9},{11,10},{13,12},{... | collective-permute-start | bytes 3145736 | tf_op jit(solution)/shard_map/ppermute | solution.py:54
  964.8 62.2 %collective-permute-start.52 = (bf16[1024,512]{1,0:T(8,128)(2,1)}, bf16[1024,512]{1,0:T(8,128)(2,1)}, u32[]{:S(2)}, u32[]{:S(2)}) collective-permute-start(bf16[1024,512]{1,0:T(8,128)(2,1)} %collective-permute-done.48), channel_id=1, source_target_pairs={{0,1},{1,2},{2,3},{4,5},{5,6},{6,7},{8,9},{9,10},{10,11},{12,13},{... | collective-permute-start | bytes 3145736 | tf_op jit(solution)/shard_map/ppermute | solution.py:53
  970.4 54.6 %collective-permute-start.67 = (f32[16,1024]{0,1:T(8,128)S(1)}, f32[16,1024]{0,1:T(8,128)}, u32[]{:S(2)}, u32[]{:S(2)}) collective-permute-start(f32[16,1024]{0,1:T(8,128)S(1)} %bitcast.214), channel_id=1, source_target_pairs={{0,2},{1,3},{2,0},{3,1},{4,6},{5,7},{6,4},{7,5},{8,10},{9,11},{10,... | collective-permute-start | bytes 196616 | tf_op jit(solution)/shard_map/ppermute | solution.py:83
  971.1 53.9 %collective-permute-start.68 = (f32[16,1024]{0,1:T(8,128)S(1)}, f32[16,1024]{0,1:T(8,128)}, u32[]{:S(2)}, u32[]{:S(2)}) collective-permute-start(f32[16,1024]{0,1:T(8,128)S(1)} %bitcast.215), channel_id=1, source_target_pairs={{0,3},{1,0},{2,1},{3,2},{4,7},{5,4},{6,5},{7,6},{8,11},{9,8},{10,9... | collective-permute-start | bytes 196616 | tf_op jit(solution)/shard_map/ppermute | solution.py:83
  972.3 53.2 %collective-permute-start.66 = (f32[16,1024]{0,1:T(8,128)S(1)}, f32[16,1024]{0,1:T(8,128)}, u32[]{:S(2)}, u32[]{:S(2)}) collective-permute-start(f32[16,1024]{0,1:T(8,128)S(1)} %bitcast.216), channel_id=1, source_target_pairs={{0,1},{1,2},{2,3},{3,0},{4,5},{5,6},{6,7},{7,4},{8,9},{9,10},{10,1... | collective-permute-start | bytes 196616 | tf_op jit(solution)/shard_map/ppermute | solution.py:83
  993.5 58.2 %collective-permute-start.51 = (bf16[1024,512]{1,0:T(8,128)(2,1)}, bf16[1024,512]{1,0:T(8,128)(2,1)}, u32[]{:S(2)}, u32[]{:S(2)}) collective-permute-start(bf16[1024,512]{1,0:T(8,128)(2,1)} %collective-permute-done.50), channel_id=1, source_target_pairs={{1,0},{2,1},{3,2},{5,4},{6,5},{7,6},{9,8},{10,9},{11,10},{13,12},{... | collective-permute-start | bytes 3145736 | tf_op jit(solution)/shard_map/ppermute | solution.py:54
  1027.1 30.6 %collective-permute-start.53 = (bf16[1024,512]{1,0:T(8,128)(2,1)}, bf16[1024,512]{1,0:T(8,128)(2,1)}, u32[]{:S(2)}, u32[]{:S(2)}) collective-permute-start(bf16[1024,512]{1,0:T(8,128)(2,1)} %collective-permute-done.52), channel_id=1, source_target_pairs={{0,1},{1,2},{2,3},{4,5},{5,6},{6,7},{8,9},{9,10},{10,11},{12,13},{... | collective-permute-start | bytes 3145736 | tf_op jit(solution)/shard_map/ppermute | solution.py:53
  1070.5 175.8 %reduce-scatter.11.cloned.1.call-start = ((), (), s32[]{:S(2)}) async-start(), calls=%async_computation.8 | async-start | bytes 7077888 | tf_op jit(solution)/shard_map/reduce_scatter | solution.py:518
  1180.0 39.6 %collective-permute-start.59 = (bf16[1024,512]{1,0:T(8,128)(2,1)}, bf16[1024,512]{1,0:T(8,128)(2,1)}, u32[]{:S(2)}, u32[]{:S(2)}) collective-permute-start(bf16[1024,512]{1,0:T(8,128)(2,1)} %get-tuple-element.164), channel_id=1, source_target_pairs={{0,1},{1,2},{2,3},{4,5},{5,6},{6,7},{8,9},{9,10},{10,11},{12,13},{... | collective-permute-start | bytes 3145736 | tf_op jit(solution)/shard_map/ppermute | solution.py:74
  (85 other events, 1975.5 us)
Sparse Core Ops, SparseCore 0:
  11.6 59.1 all-gather.5
  72.7 125.1 all-gather.7
  199.8 125.1 all-gather.9
  593.6 155.1 reduce-scatter.4
  752.2 156.2 reduce-scatter.6
  1070.7 45.3 reduce-scatter.8
  1126.3 59.6 reduce-scatter.10

commit v2 on v1

--- a/solution.py
+++ b/solution.py
@@ -36,44 +36,29 @@
     return with_layout_constraint(values, Layout(major_to_minor=tuple(range(values.ndim))))
 
 
-def after(values, *others):
-    return lax.optimization_barrier((values, *others))[0]
-
-
-def line_pairs():
+def zero_of(values):
+    return jnp.minimum(jnp.abs(values[(0,) * values.ndim].astype(F32)), 0.0).astype(BF)
+
+
+def shift(values, k):
     n = lax.axis_size("col")
-    return n, [(i, i + 1) for i in range(n - 1)], [(i + 1, i) for i in range(n - 1)]
-
-
-def gather_line(block):
-    n, to_right, to_left = line_pairs()
+    return lax.ppermute(values, "col", [(i, (i + k) % n) for i in range(n)])
+
+
+def pieces_line(block):
+    n = lax.axis_size("col")
+    far = {k: shift(block, k) for k in (*range(2, n), 1)}
+    return [far[k] for k in range(1, n)]
+
+
+def scatter_line(part):
+    n = lax.axis_size("col")
     me = lax.axis_index("col")
-    from_left, from_right = [block], [block]
-    for _ in range(n - 1):
-        from_left.append(lax.ppermute(from_left[-1], "col", to_right))
-        from_right.append(lax.ppermute(from_right[-1], "col", to_left))
-    out = jnp.zeros((n, *block.shape), block.dtype)
-    out = lax.dynamic_update_index_in_dim(out, block, me, 0)
-    for r in range(1, n):
-        piece = from_left[r] + from_right[n - r]
-        out = lax.dynamic_update_index_in_dim(out, piece, lax.rem(me - r + n, n), 0)
-    return out
-
-
-def scatter_line(part):
-    n, to_right, to_left = line_pairs()
-    me = lax.axis_index("col")
-    right = left = None
-    for r in range(1, n):
-        k = n - r
-        go_right = part(jnp.minimum(me + k, n - 1))
-        go_left = part(jnp.maximum(me - k, 0))
-        if right is not None:
-            go_right = go_right + right.astype(F32)
-            go_left = go_left + left.astype(F32)
-        right = lax.ppermute(go_right.astype(BF), "col", to_right)
-        left = lax.ppermute(go_left.astype(BF), "col", to_left)
-    return part(me) + right.astype(F32) + left.astype(F32)
+    others = [
+        shift(part(lax.rem(me + k, n)).astype(BF), k) for k in (*range(2, n), 1)
+    ]
+    total = part(me).astype(F32)
+    return total, others
 
 
 def sum_small(values):
@@ -93,6 +78,332 @@
         piece = lax.ppermute(values, "col", [(i, (i + k) % n) for i in range(n)])
         out = lax.dynamic_update_index_in_dim(out, piece, lax.rem(me - k + n, n), 0)
     return out
+
+
+CHUNK = 128
+
+
+def line_kernel(n, make, n_in, n_out, *refs):
+    plan = make(refs[:n_in], refs[n_in : n_in + n_out])
+    term, first, second, out = plan
+    stat_out, stat_in, stat_sem, *rest = refs[n_in + n_out :]
+    if term is not None:
+        sums, held, sum_sem, *rest = rest
+    if out is not None:
+        (gather_sem,) = rest
+    chunks = stat_out.shape[0]
+    me = lax.axis_index("col")
+    ways = ((1, me > 0, me < n - 1), (-1, me < n - 1, me > 0))
+
+    barrier = pltpu.get_barrier_semaphore()
+    for k in range(1, n):
+        pl.semaphore_signal(
+            barrier, inc=1, device_id={"col": lax.rem(me + k, n)},
+            device_id_type=pl.DeviceIdType.MESH,
+        )
+    pl.semaphore_wait(barrier, n - 1)
+
+    def at(c):
+        return pl.ds(pl.multiple_of(c * CHUNK, CHUNK), CHUNK)
+
+    def remote(ref, sems, index, other):
+        return pltpu.make_async_remote_copy(
+            src_ref=ref, dst_ref=ref, send_sem=sems.at[(0, *index)], recv_sem=sems.at[(1, *index)],
+            device_id={"col": other}, device_id_type=pl.DeviceIdType.MESH,
+        )
+
+    def sum_copy(way, s, c, other):
+        return remote(sums.at[way, s, at(c)], sum_sem, (way, s, c), other)
+
+    def gather_copy(way, s, c, other):
+        part = out.shape[1] // n
+        block = out.at[at(c), pl.ds(pl.multiple_of(s * part, part), part)]
+        return remote(block, gather_sem, (way, s, c), other)
+
+    def stat_copy(k, c):
+        return pltpu.make_async_remote_copy(
+            src_ref=stat_out.at[c], dst_ref=stat_in.at[k, c], send_sem=stat_sem.at[0, k, c],
+            recv_sem=stat_sem.at[1, k, c], device_id={"col": lax.rem(me + k, n)},
+            device_id_type=pl.DeviceIdType.MESH,
+        )
+
+    def arrived(way, s, c):
+        step, has_source, _ = ways[way]
+
+        @pl.when(has_source)
+        def _():
+            sum_copy(way, s, c, me - step).wait_recv()
+
+        @pl.when(jnp.logical_not(has_source))
+        def _():
+            sums[way, s, at(c)] = jnp.zeros_like(sums[way, s, at(c)])
+
+    depths = (me, n - 1 - me)
+    hops = []
+    for j in range(n - 1):
+        hops += [(0, n - 1 - j, n - 1 - j > me), (1, j, j < me)]
+
+    def on_turn(t, hop, action):
+        way, s, mine = hop
+        c = t - depths[way]
+        pl.when(mine & (c >= 0) & (c < chunks))(lambda: action(way, s, c))
+
+    def ready(way, s, c):
+        held[way] = term(at(c), s)
+
+    def add(way, s, c):
+        arrived(way, s, c)
+        sums[way, s, at(c)] = (held[way] + sums[way, s, at(c)].astype(F32)).astype(BF)
+
+    def send(way, s, c):
+        sum_copy(way, s, c, me + ways[way][0]).start()
+
+    def finish(c):
+        total = None
+        if term is not None:
+            arrived(0, me, c)
+            arrived(1, me, c)
+            total = (
+                term(at(c), me) + sums[0, me, at(c)].astype(F32) + sums[1, me, at(c)].astype(F32)
+            )
+        stat = jnp.broadcast_to(first(at(c), total), (CHUNK, 128))
+        stat_out[c] = stat.T[:8]
+
+    def apply(c):
+        row = stat_out[c]
+        for k in range(1, n):
+            stat_copy(k, c).wait_recv()
+            row = row + stat_in[k, c]
+        stat = jnp.broadcast_to(row[:1], (128, CHUNK)).T[:, :1]
+        block = second(at(c), stat)
+        if out is not None:
+            part = out.shape[1] // n
+            out[at(c), pl.ds(pl.multiple_of(me * part, part), part)] = block
+
+    def pass_on(c, r):
+        for way, (step, _, has_target) in enumerate(ways):
+            s = me - step * r
+            there = jnp.logical_and(s >= 0, s < n)
+            if r > 0:
+                @pl.when(there)
+                def _():
+                    gather_copy(way, s, c, me - step).wait_recv()
+
+            @pl.when(jnp.logical_and(there, has_target))
+            def _():
+                gather_copy(way, s, c, me + step).start()
+
+    lag = 0 if term is None else n - 1
+    last = lag + 1 + (0 if out is None else n)
+
+    def body(t, carry):
+        def stage(delay, action):
+            c = t - delay
+            pl.when(jnp.logical_and(c >= 0, c < chunks))(lambda: action(c))
+
+        if out is not None:
+            for r in range(n - 1, -1, -1):
+                stage(lag + 2 + r, lambda c: pass_on(c, r))
+        if term is not None:
+            on_turn(t, hops[0], ready)
+            for hop, later in zip(hops, hops[1:]):
+                on_turn(t, hop, add)
+                on_turn(t, later, ready)
+                on_turn(t, hop, send)
+            on_turn(t, hops[-1], add)
+        stage(lag, finish)
+        if term is not None:
+            on_turn(t, hops[-1], send)
+        stage(lag + 1, apply)
+
+        def tell(c):
+            for k in range(1, n):
+                stat_copy(k, c).start()
+
+        stage(lag, tell)
+        return carry
+
+    lax.fori_loop(0, chunks + last + 1, body, 0)
+
+    def drain(c, carry):
+        for k in range(1, n):
+            stat_copy(k, c).wait_send()
+        if term is not None:
+            for way, s, mine in hops:
+                @pl.when(mine)
+                def _():
+                    sum_copy(way, s, c, me + ways[way][0]).wait_send()
+        if out is not None:
+            for r in range(n):
+                for way, (step, _, has_target) in enumerate(ways):
+                    s = me - step * r
+                    there = jnp.logical_and(s >= 0, s < n)
+
+                    @pl.when(jnp.logical_and(there, has_target))
+                    def _():
+                        gather_copy(way, s, c, me + step).wait_send()
+        return carry
+
+    lax.fori_loop(0, chunks, drain, 0)
+
+
+def along_line(make, operands, out_shape, rows, part, sums, gathers, number, name, others=()):
+    n = lax.axis_size("col")
+    chunks = rows // CHUNK
+    vmem = pl.BlockSpec(memory_space=pltpu.VMEM)
+    scratch = [
+        pltpu.VMEM((chunks, 8, 128), F32), pltpu.VMEM((n, chunks, 8, 128), F32),
+        pltpu.SemaphoreType.DMA((2, n, chunks)),
+    ]
+    if sums:
+        scratch += [
+            pltpu.VMEM((2, n, rows, part), BF), pltpu.VMEM((2, CHUNK, part), F32),
+            pltpu.SemaphoreType.DMA((2, 2, n, chunks)),
+        ]
+    if gathers:
+        scratch += [pltpu.SemaphoreType.DMA((2, 2, n, chunks))]
+    return pl.pallas_call(
+        functools.partial(line_kernel, n, make, len(operands), len(out_shape)),
+        in_specs=[vmem] * (len(operands) - len(others)) + list(others),
+        out_specs=[vmem] * len(out_shape),
+        out_shape=out_shape,
+        scratch_shapes=scratch,
+        compiler_params=pltpu.CompilerParams(
+            vmem_limit_bytes=VMEM_LIMIT, collective_id=number, has_side_effects=True
+        ),
+        cost_estimate=pl.CostEstimate(
+            flops=1_000_000, bytes_accessed=rows * part, transcendentals=0
+        ),
+        name=name,
+    )(*operands)
+
+
+def norm_line(tokens, gain, width):
+    rows, part = tokens.shape
+
+    def make(ins, outs):
+        x_ref, gain_ref = ins
+        out_ref, inv_ref = outs
+
+        def first(at, total):
+            x = x_ref[at, :].astype(F32)
+            return jnp.sum(x * x, axis=1, keepdims=True)
+
+        def second(at, stat):
+            inv = lax.rsqrt(stat / width + EPSILON)
+            inv_ref[at, :] = inv
+            return (x_ref[at, :].astype(F32) * inv * gain_ref[...].astype(F32)).astype(BF)
+
+        return None, first, second, out_ref
+
+    out_shape = [
+        jax.ShapeDtypeStruct((rows, width), BF), jax.ShapeDtypeStruct((rows, 1), F32)
+    ]
+    return along_line(make, [tokens, gain], out_shape, rows, part, False, True, 1, "norm_line")
+
+
+def attn_line(mixed, w_out, tokens, gain, width):
+    rows, part = tokens.shape
+
+    def make(ins, outs):
+        m_ref, w_ref, x_ref, gain_ref = ins
+        out_ref, hidden_ref, inv_ref = outs
+
+        def term(at, s):
+            return dot_nt(m_ref[at, :], w_ref[pl.ds(s * part, part), :])
+
+        def first(at, total):
+            hidden = x_ref[at, :].astype(F32) + total
+            hidden_ref[at, :] = hidden
+            return jnp.sum(hidden * hidden, axis=1, keepdims=True)
+
+        def second(at, stat):
+            inv = lax.rsqrt(stat / width + EPSILON)
+            inv_ref[at, :] = inv
+            return (hidden_ref[at, :] * inv * gain_ref[...].astype(F32)).astype(BF)
+
+        return term, first, second, out_ref
+
+    out_shape = [
+        jax.ShapeDtypeStruct((rows, width), BF), jax.ShapeDtypeStruct((rows, part), F32),
+        jax.ShapeDtypeStruct((rows, 1), F32),
+    ]
+    return along_line(
+        make, [mixed, w_out, tokens, gain], out_shape, rows, part, True, True, 2, "attn_line"
+    )
+
+
+def moe_line(terms, hidden, inv, gain, grads, earlier, width):
+    rows, part = hidden.shape
+
+    def make(ins, outs):
+        t_ref, hidden_ref, inv_ref, gain_ref, y_ref, _ = ins
+        out_ref, grad_ref, d_gain_ref = outs
+        d_gain_ref[...] = jnp.zeros_like(d_gain_ref)
+
+        def term(at, s):
+            return t_ref[s, at, :].astype(F32)
+
+        def first(at, total):
+            grad_ref[at, :] = total
+            product = total * hidden_ref[at, :]
+            d_gain_ref[...] += jnp.sum(product * inv_ref[at, :], axis=0, keepdims=True)
+            return jnp.sum(product * gain_ref[...].astype(F32), axis=1, keepdims=True)
+
+        def second(at, stat):
+            factor = inv_ref[at, :]
+            grad = (
+                y_ref[at, :].astype(F32)
+                + factor * gain_ref[...].astype(F32) * grad_ref[at, :]
+                - factor * factor * factor * (stat / width) * hidden_ref[at, :]
+            )
+            grad_ref[at, :] = grad
+            return grad.astype(BF)
+
+        return term, first, second, out_ref
+
+    out_shape = [
+        jax.ShapeDtypeStruct((rows, width), BF), jax.ShapeDtypeStruct((rows, part), F32),
+        jax.ShapeDtypeStruct((1, part), F32),
+    ]
+    return along_line(
+        make, [terms, hidden, inv, gain, grads, earlier], out_shape, rows, part, True, True, 3,
+        "moe_line", [pl.BlockSpec(memory_space=pl.ANY)],
+    )
+
+
+def input_line(qkv_grad, w_qkv, tokens, inv, gain, grads, width):
+    rows, part = tokens.shape
+
+    def make(ins, outs):
+        q_ref, w_ref, x_ref, inv_ref, gain_ref, y_ref = ins
+        grad_ref, d_gain_ref = outs
+        d_gain_ref[...] = jnp.zeros_like(d_gain_ref)
+
+        def term(at, s):
+            return dot_nt(q_ref[at, :], w_ref[pl.ds(s * part, part), :])
+
+        def first(at, total):
+            grad_ref[at, :] = total
+            product = total * x_ref[at, :].astype(F32)
+            d_gain_ref[...] += jnp.sum(product * inv_ref[at, :], axis=0, keepdims=True)
+            return jnp.sum(product * gain_ref[...].astype(F32), axis=1, keepdims=True)
+
+        def second(at, stat):
+            factor = inv_ref[at, :]
+            grad_ref[at, :] = (
+                y_ref[at, :]
+                + factor * gain_ref[...].astype(F32) * grad_ref[at, :]
+                - factor * factor * factor * (stat / width) * x_ref[at, :].astype(F32)
+            )
+
+        return term, first, second, None
+
+    out_shape = [jax.ShapeDtypeStruct((rows, part), F32), jax.ShapeDtypeStruct((1, part), F32)]
+    return along_line(
+        make, [qkv_grad, w_qkv, tokens, inv, gain, grads], out_shape, rows, part, True, False, 4,
+        "input_line",
+    )
 
 
 def rope_tables(length):
@@ -165,7 +476,7 @@
 
 
 def attend_back_kernel(
-    scale, block, q_ref, k_ref, v_ref, d_ref, cos_ref, sin_ref, srow_ref, scol_ref,
+    scale, block, q_ref, k_ref, v_ref, d_ref, cos_ref, sin_ref, srow_ref, scol_ref, _,
     dq_ref, dk_ref, dv_ref, dk_sum, dv_sum
 ):
     rows = q_ref.shape[0]
@@ -196,7 +507,7 @@
     dv_ref[...] = dv_sum[...].astype(BF)
 
 
-def attend_back(queries, keys, values, grads, cosine, sine, span_row, span_col):
+def attend_back(queries, keys, values, grads, cosine, sine, span_row, span_col, earlier):
     rows, width = queries.shape
     heads = width // HD
     head = pl.BlockSpec((rows, HD), lambda h: (0, h))
@@ -205,7 +516,8 @@
         functools.partial(attend_back_kernel, 1.0 / math.sqrt(HD), min(256, rows)),
         grid=(heads,),
         in_specs=[head] * 4
-        + [whole((rows, HD)), whole((rows, HD)), whole((1, rows)), whole((rows, 1))],
+        + [whole((rows, HD)), whole((rows, HD)), whole((1, rows)), whole((rows, 1))]
+        + [pl.BlockSpec(memory_space=pl.ANY)],
         out_specs=[head] * 3,
         out_shape=[
             jax.ShapeDtypeStruct((rows, width), F32),
@@ -219,14 +531,50 @@
             transcendentals=rows * rows * heads,
         ),
         name="attend_back",
-    )(queries, keys, values, grads, cosine, sine, span_row, span_col)
+    )(queries, keys, values, grads, cosine, sine, span_row, span_col, earlier)
+
+
+def prepare_kernel(n, x_ref, own_ref, *refs):
+    pieces, (xt_ref, y_ref, yt_ref) = refs[: n - 1], refs[n - 1 :]
+    part = own_ref.shape[1]
+    me = lax.axis_index("col")
+    for s in range(n):
+        cols = slice(s * part, (s + 1) * part)
+        xt_ref[cols, :] = x_ref[:, cols].T
+    for k, piece in enumerate((own_ref, *pieces)):
+        cols = pl.ds(pl.multiple_of(lax.rem(me - k + n, n) * part, part), part)
+        y_ref[:, cols] = piece[...]
+        yt_ref[cols, :] = piece[...].T
+
+
+def prepare(x, own, pieces):
+    rows, width = x.shape
+    part = own.shape[1]
+    n = width // part
+    step = min(256, rows)
+    wide = pl.BlockSpec((step, width), lambda i: (i, 0))
+    tall = pl.BlockSpec((width, step), lambda i: (0, i))
+    block = pl.BlockSpec((step, part), lambda i: (i, 0))
+    out = lambda a, b: jax.ShapeDtypeStruct((a, b), BF)
+    return pl.pallas_call(
+        functools.partial(prepare_kernel, n),
+        grid=(rows // step,),
+        in_specs=[wide] + [block] * n,
+        out_specs=[tall, wide, tall],
+        out_shape=[out(width, rows), out(rows, width), out(width, rows)],
+        compiler_params=pltpu.CompilerParams(vmem_limit_bytes=VMEM_LIMIT),
+        cost_estimate=pl.CostEstimate(
+            flops=0, bytes_accessed=10 * rows * width, transcendentals=0
+        ),
+        name="prepare",
+    )(x, own, *pieces)
 
 
 def moe_kernel(
     first, n_col, closing, x_ref, xt_ref, y_ref, yt_ref, gates_ref, w_ref, *rest
 ):
     if closing:
-        probs_ref, before_ref, router_ref, *rest = rest
+        probs_ref, before_ref, router_ref, first_ref, *rest = rest
     dx_ref, dw_ref, hid_ref, dg_ref, acc, pre, up, grad, d_pre, d_up = rest
     step = pl.program_id(0)
     expert = step + first
@@ -284,7 +632,7 @@
             cols = slice(s * part, (s + 1) * part)
             total = acc[:, cols]
             if closing:
-                total = total + dot_nn(low, router_ref[:, cols])
+                total = total + dot_nn(low, router_ref[:, cols]) + first_ref[s].astype(F32)
             dx_ref[s] = total.astype(BF)
 
 
@@ -413,13 +761,9 @@
     first_half = lax.all_gather(pack_experts(w_gate, w_up, w_down, 0, half), "row", axis=0)
     second_half = lax.all_gather(pack_experts(w_gate, w_up, w_down, half, experts), "row", axis=0)
 
-    below = jnp.broadcast_to(norm_attn.reshape(1, part), (16, part))
-    spread = gather_line(jnp.concatenate([tokens, below], axis=0))
-    token_values = jnp.transpose(spread[:, :rows], (1, 0, 2)).reshape(rows, width).astype(F32)
-    attn_gain = spread[:, rows].reshape(1, width).astype(F32)
-    inv_first = lax.rsqrt(jnp.mean(token_values * token_values, axis=1, keepdims=True) + EPSILON)
-    normed_attn = (token_values * inv_first * attn_gain).astype(BF)
-    grad_blocks = gather_line(after(cotangent, spread))
+    attn_gain = norm_attn.reshape(1, part)
+    normed_attn, inv_first = norm_line(tokens, attn_gain, width)
+    grad_pieces = pieces_line(cotangent + zero_of(normed_attn))
     qkv = dot_nn(normed_attn, full_qkv)
     query_raw, key_raw = qkv[:, :part], qkv[:, part : 2 * part]
 
@@ -436,20 +780,9 @@
         qkv, query_inv, key_inv, query_gain, key_gain, cosine, sine, span_row, span_col
     )
 
-    attn_parts = dot_nt(mixed, full_out)
-    attn = scatter_line(
-        lambda s: lax.dynamic_slice_in_dim(attn_parts, s * part, part, 1)
-    )
-    local_tokens = tokens.astype(F32)
-    hidden_state = local_tokens + after(attn, grad_blocks)
-    moe_gain = norm_moe.astype(F32).reshape(1, part)
-    hidden_square = sum_small(jnp.sum(hidden_state * hidden_state, axis=1)[None])
-    inv_second = lax.rsqrt(hidden_square[0][:, None] / width + EPSILON)
-    flat = lambda blocks: jnp.transpose(blocks, (1, 0, 2)).reshape(rows, width)
-    turn = lambda blocks: jnp.transpose(blocks, (0, 2, 1)).reshape(width, rows)
-    moe_blocks = gather_line((hidden_state * inv_second * moe_gain).astype(BF))
-    normed_moe, normed_moe_t = flat(moe_blocks), turn(moe_blocks)
-    grad_full, grad_full_t = flat(grad_blocks), turn(grad_blocks)
+    moe_gain = norm_moe.reshape(1, part)
+    normed_moe, hidden_state, inv_second = attn_line(mixed, full_out, tokens, moe_gain, width)
+    normed_moe_t, grad_full, grad_full_t = prepare(normed_moe, cotangent, grad_pieces)
 
     router_t = gather_small(mats[:, 4 * part : 4 * part + cols].T).reshape(experts, width)
     router_probs = jax.nn.softmax(dot_nt(normed_moe, router_t), axis=1)
@@ -462,27 +795,23 @@
     )
     dx_b, dw_b, hid_b, dg_b = moe_half(
         half, normed_moe, normed_moe_t, grad_full, grad_full_t, gate_table, second_half,
-        (router_probs, dg_a, router_t),
+        (router_probs, dg_a, router_t, dx_a),
     )
     summed_a = lax.psum_scatter(dw_a, "row", scatter_dimension=0)
     summed_b = lax.psum_scatter(dw_b, "row", scatter_dimension=0)
-
-    pick = lambda blocks, s: lax.dynamic_index_in_dim(blocks, s, 0, keepdims=False).astype(F32)
-    dx_b = after(dx_b, summed_a)
-    moe_in_grad = scatter_line(lambda s: pick(dx_a, s) + pick(dx_b, s))
-    moe_stat = sum_small(jnp.sum(moe_in_grad * moe_gain * hidden_state, axis=1)[None])[0][:, None]
-    d_moe_gain = jnp.sum(moe_in_grad * hidden_state * inv_second, axis=0)
-    hidden_grad = (
-        cotangent.astype(F32)
-        + inv_second * moe_gain * moe_in_grad
-        - inv_second**3 * hidden_state * moe_stat / width
-    )
-    attn_grad = flat(gather_line(hidden_grad.astype(BF)))
+    moe_parts = down(hid_a, hid_b, first_half, second_half)
+
+    attn_grad, hidden_grad, d_moe_gain = moe_line(
+        dx_b, hidden_state, inv_second, moe_gain, cotangent, moe_parts, width
+    )
+    parted = zero_of(attn_grad)
+    pick = lambda s: lax.dynamic_index_in_dim(moe_parts, s, 0, keepdims=False) + parted
+    own_part, other_parts = scatter_line(pick)
     mixed_grad = dot_nn(attn_grad, full_out).astype(BF)
     d_out_w = dot_tn(attn_grad, mixed)
 
     query_turned, key_turned, value_grad = attend_back(
-        queries, keys, values, after(mixed_grad, summed_b), cosine, sine, span_row, span_col
+        queries, keys, values, mixed_grad, cosine, sine, span_row, span_col, summed_a
     )
     query_scaled = query_turned * query_gain.astype(F32)
     key_scaled = key_turned * key_gain.astype(F32)
@@ -500,7 +829,9 @@
         key_inv * key_scaled - key_inv**3 * key_raw * stats[1][:, None] / width
     ).astype(BF)
     qkv_grad = jnp.concatenate([query_raw_grad, key_raw_grad, value_grad], axis=1)
-    attn_in_terms = dot_nt(qkv_grad, full_qkv)
+    d_tokens, d_attn_gain = input_line(
+        qkv_grad, full_qkv, tokens, inv_first, attn_gain, hidden_grad, width
+    )
     d_qkv_w = dot_tn(normed_attn, qkv_grad)
 
     gate_grad = jnp.where(routed, sum_small(dg_b.T).T, 0.0)
@@ -509,38 +840,23 @@
     ).astype(BF)
     d_router_w = dot_tn(normed_moe, lax.dynamic_slice_in_dim(logit_low, me * cols, cols, 1))
 
-    d_out_mats = jnp.concatenate(
-        [d_out_w.astype(BF), d_router_w.astype(BF), jnp.zeros((width, -cols % 128), BF)], axis=1
-    )
-    summed_out = lax.psum_scatter(
-        after(row_major(d_out_mats), summed_b), "row", scatter_dimension=0, tiled=True
+    spare = jnp.broadcast_to(summed_b[0, 0, 0, 0], (width, -cols % 128))
+    d_mats = jnp.concatenate(
+        [d_qkv_w.astype(BF), d_out_w.astype(BF), d_router_w.astype(BF), spare], axis=1
+    )
+    summed = lax.psum_scatter(
+        row_major(d_mats), "row", scatter_dimension=0, tiled=True
     ).astype(F32)
-    summed_qkv = lax.psum_scatter(
-        after(row_major(d_qkv_w.astype(BF)), summed_out), "row", scatter_dimension=0, tiled=True
-    ).astype(F32)
-
-    attn_in_grad = scatter_line(
-        lambda s: lax.dynamic_slice_in_dim(attn_in_terms, s * part, part, 1)
-    )
-    local_gain = norm_attn.astype(F32).reshape(1, part)
-    attn_stat = sum_small(jnp.sum(attn_in_grad * local_gain * local_tokens, axis=1)[None])
-    d_attn_gain = jnp.sum(attn_in_grad * local_tokens * inv_first, axis=0)
-    d_tokens = (
-        hidden_grad
-        + inv_first * local_gain * attn_in_grad
-        - inv_first**3 * local_tokens * attn_stat[0][:, None] / width
-    )
-
-    moe_parts = down(hid_a, hid_b, first_half, second_half)
-    output = (hidden_state + scatter_line(lambda s: pick(moe_parts, s))).astype(BF)
-
-    gains = lax.psum(jnp.stack([d_attn_gain, d_query_gain, d_key_gain, d_moe_gain]), "row")
+    others = functools.reduce(lambda a, b: a + b.astype(F32), other_parts, zero_of(d_tokens))
+    output = (hidden_state + own_part + others).astype(BF)
+
+    gains = lax.psum(jnp.stack([d_attn_gain[0], d_query_gain, d_key_gain, d_moe_gain[0]]), "row")
     expert_grads = jnp.concatenate([summed_a, summed_b], axis=0)
     unpack = lambda i: jnp.transpose(expert_grads[:, i], (1, 0, 2)).astype(F32)
-    cut = lambda i: summed_qkv[:, i * part : (i + 1) * part]
+    cut = lambda i: summed[:, i * part : (i + 1) * part]
     return (
         output, d_tokens, gains[0], gains[1], gains[2], gains[3],
-        cut(0), cut(1), cut(2), summed_out[:, :part], summed_out[:, part : part + cols],
+        cut(0), cut(1), cut(2), cut(3), summed[:, 4 * part : 4 * part + cols],
         unpack(0), unpack(1), unpack(2),
     )
 

time: 1260 us -> 1080 us (0.86)
  Pallas kernels: 326 us -> 811 us
  waiting for transfers between devices: 466 us -> 66.3 us
  starting transfers between devices: 187 us -> 24.2 us
  other arithmetic: 101 us -> 31.9 us
  local copies, waits for them, and re-layouts: 97.3 us -> 77 us
  matrix products: 49.6 us -> 33.7 us
    pallas_call x0 -> x5, Pallas kernels: none -> 484 us  [the longest x4 475 us: along_line(): pl.pallas_call(functools.partial(line_kernel, n, make, len(operands), len...]
    ppermute x48 -> x6, waiting for transfers between devices: 337 us -> 0.02 us  [shift(): return lax.ppermute(values, 'col', [(i, (i + k) % n) for i in range(n)])]
    ppermute x48 -> x6, starting transfers between devices: 152 us -> 6.38 us  [shift(): return lax.ppermute(values, 'col', [(i, (i + k) % n) for i in range(n)])]
    ppermute x3, waiting for transfers between devices: 45.9 us -> 0.01 us  [gather_small(): piece = lax.ppermute(values, 'col', [(i, (i + k) % n) for i in range(n)])]
    convert_element_type x20 -> x1, other arithmetic: 42 us -> 4.55 us  [shards(): output = (hidden_state + own_part + others).astype(BF)]
    reduce_scatter x1, waiting for transfers between devices: 24.2 us -> 0.01 us  [shards(): summed_a = lax.psum_scatter(dw_a, 'row', scatter_dimension=0)]
    broadcast_in_dim x10 -> x0, other arithmetic: 16.1 us -> none  [the longest x9 15.8 us: gather_line(): out = lax.dynamic_update_index_in_dim(out, piece, lax.rem(me - r + n, n), 0)]
    ppermute x18 -> x9, starting transfers between devices: 28.7 us -> 13.1 us  [sum_small(): lax.ppermute(values, 'col', [(i, (i + k) % n) for i in range(n)])]
  transfers between devices with their start and end apart: 76 -> 24, of which waited for: 42 -> 2; matrix products, arithmetic and copies ran while one was open for 18% -> 9% of each run, Pallas kernels for 26% -> 76%
where the time goes in v2:
time: 1080 us; the launch traced here: 1070 us
  Pallas kernels  811 us (75%)
  local copies, waits for them, and re-layouts  77 us (7%)
  waiting for transfers between devices  66.3 us (6%)
  matrix products  33.7 us (3%)
  other arithmetic  31.9 us (3%)
  starting transfers between devices  24.2 us (2%)
  between operations  16.9 us (2%)
  blocking collectives  12.5 us (1%)
    pallas_call x4, Pallas kernels, along_line(): pl.pallas_call(functools.partial(line_kernel, n, make, len(operands), len...  475 us
    pallas_call x2, Pallas kernels, moe_half(): pl.pallas_call(functools.partial(moe_kernel, first, n_col, closing is not...  261 us
    ppermute x9, waiting for transfers between devices, sum_small(): lax.ppermute(values, 'col', [(i, (i + k) % n) for i in range(n)])  66.2 us
    pallas_call x1, Pallas kernels, down(): pl.pallas_call(functools.partial(down_kernel, n_col), grid=(2 * half,), i...  27 us
    pallas_call x1, Pallas kernels, attend_back(): pl.pallas_call(functools.partial(attend_back_kernel, 1.0 / math.sqrt(HD),...  21.7 us
  transfers between devices with their start and end apart: 24, of which 2 were waited for; matrix products, arithmetic and copies ran while one was open for 9% of the time, Pallas kernels for 76%

profile of v2, /device:TPU:0, one launch (start us, length us, event | category | flops | bytes accessed | tf_op | source)
XLA Modules:
  0.0 1073.2 jit_solution(7787816164089773423)
XLA Ops:
  8.2 3.2 concatenate.18
  14.4 2.0 pad_maximum_fusion
  17.1 2.1 pad_maximum_fusion.1
  20.5 84.2 %norm_line.1 = (bf16[1024,2048]{1,0:T(8,128)(2,1)}, f32[1024,1]{1,0:T(8,128)}) custom-call(bf16[1024,512]{1,0:T(8,128)(2,1)} %refs_2_.3, bf16[1,512]{1,0:T(2,128)(2,1)} %reshape.132.refs_1_.refs_4_), custom_call_target="tpu_custom_call" | custom-call | flops 1000000 | bytes 524288 | tf_op jit(solution)/shard_map/norm_line/pallas_call | solution.py:265
  106.5 2.3 broadcast_add_fusion
  108.8 1.8 collective-permute-start.5
  114.4 2.0 fusion.15
  117.7 10.0 fusion.19.q_ref.k_ref.v_ref
  128.1 2.6 collective-permute-start.1
  130.8 2.7 collective-permute-start.2
  134.6 64.4 %collective-permute-done.1 = f32[2,1024]{1,0:T(2,128)S(1)} collective-permute-done((f32[2,1024]{1,0:T(2,128)S(1)}, f32[2,1024]{1,0:T(2,128)S(1)}, u32[]{:S(2)}, u32[]{:S(2)}) %collective-permute-start.1) | collective-permute-done | bytes 8224 | tf_op jit(solution)/shard_map/ppermute | solution.py:68
  201.9 1.9 bitcast_dynamic-update-slice_fusion
  203.7 3.0 slice.129.refs_1_
  206.8 3.4 collective-permute-start.7
  213.1 16.8 %attend.1 = (bf16[1024,512]{1,0:T(8,128)(2,1)}, bf16[1024,512]{1,0:T(8,128)(2,1)}, bf16[1024,512]{1,0:T(8,128)(2,1)}, bf16[1024,512]{1,0:T(8,128)(2,1)}) custom-call(f32[1024,1536]{1,0:T(8,128)} %copy-done, f32[1024,1536]{1,0:T(8,128)} %copy-done, f32[1024,1536]{1,0:T(8,128)} %copy-done, f32[1024,1]{1,0:T(8,128)} %copy.116.iq_ref, f32[1024,1]{1,0:T(8,128)} %copy.117.ik_ref, ...), custom_call_target="tpu_custom_call" | custom-call | flops 2147483648 | bytes 10485760 | tf_op jit(solution)/shard_map/attend/pallas_call | solution.py:459
  229.9 136.6 %attn_line.1 = (bf16[1024,2048]{1,0:T(8,128)(2,1)}, f32[1024,512]{1,0:T(8,128)}, f32[1024,1]{1,0:T(8,128)}) custom-call(bf16[1024,512]{1,0:T(8,128)(2,1)} %get-tuple-element.43.refs_0_, bf16[2048,512]{1,0:T(8,128)(2,1)} %slice.129.refs_1_, bf16[1024,512]{1,0:T(8,128)(2,1)} %refs_2_.3, bf16[1,512]{1,0:T(2,128)(2,1)} %reshape.135.refs_3_), custom_call_target="tpu_custom_call" | custom-call | flops 1000000 | bytes 524288 | tf_op jit(solution)/shard_map/attn_line/pallas_call | solution.py:265
  367.5 8.8 prepare.1
  376.2 1.9 bitcast_dynamic-update-slice_fusion.2
  379.4 1.9 bitcast_dynamic-update-slice_fusion.1
  381.3 2.0 copy.119
  383.3 3.4 fusion.29
  388.6 127.7 %experts.2 = (bf16[4,1024,512]{2,1,0:T(8,128)(2,1)}, bf16[8,8,3,256,256]{4,3,2,1,0:T(8,128)(2,1)}, bf16[8,1024,256]{2,1,0:T(8,128)(2,1)}, f32[1024,16]{1,0:T(8,128)}) custom-call(bf16[1024,2048]{1,0:T(8,128)(2,1)} %get-tuple-element.45.x_ref, bf16[2048,1024]{1,0:T(8,128)(2,1)} %get-tuple-element.46.xt_ref, bf16[1024,2048]{1,0:T(8,128)(2,1)} %get-tuple-element.47.y_ref, ...), custom_call_target="tpu_custom_call" | custom-call | flops 68719476736 | bytes 75497472 | tf_op jit(solution)/shard_map/experts/pallas_call | solution.py:656
  516.4 133.3 %experts.3 = (bf16[4,1024,512]{2,1,0:T(8,128)(2,1)}, bf16[8,8,3,256,256]{4,3,2,1,0:T(8,128)(2,1)}, bf16[8,1024,256]{2,1,0:T(8,128)(2,1)}, f32[1024,16]{1,0:T(8,128)}) custom-call(bf16[1024,2048]{1,0:T(8,128)(2,1)} %get-tuple-element.45.x_ref, bf16[2048,1024]{1,0:T(8,128)(2,1)} %get-tuple-element.46.xt_ref, bf16[1024,2048]{1,0:T(8,128)(2,1)} %get-tuple-element.47.y_ref, ...), custom_call_target="tpu_custom_call" | custom-call | flops 68719476736 | bytes 75497472 | tf_op jit(solution)/shard_map/experts/pallas_call | solution.py:656
  650.5 2.8 collective-permute-start.17
  653.3 27.0 %down.1.refs_5_ = bf16[4,1024,512]{2,1,0:T(8,128)(2,1)} custom-call(bf16[8,1024,256]{2,1,0:T(8,128)(2,1)} %get-tuple-element.49.hid_a, bf16[8,1024,256]{2,1,0:T(8,128)(2,1)} %get-tuple-element.52.hid_b, bf16[8,8,3,256,256]{4,3,2,1,0:T(8,128)(2,1)} %bitcast.144, bf16[8,8,3,256,256]{4,3,2,1,0:T(8,128)(2,1)} %bitcast.146), custom_call_target="tpu_custom_call" | custom-call | flops 17179869184 | bytes 29360128 | tf_op jit(solution)/shard_map/down/pallas_call | solution.py:715
  680.3 134.6 %moe_line.1 = (bf16[1024,2048]{1,0:T(8,128)(2,1)}, f32[1024,512]{1,0:T(8,128)}, f32[1,512]{1,0:T(1,128)}) custom-call(bf16[4,1024,512]{2,1,0:T(8,128)(2,1)} %get-tuple-element.53.refs_0_, f32[1024,512]{1,0:T(8,128)} %get-tuple-element.44.refs_1_, f32[1024,1]{1,0:T(8,128)} %get-tuple-element.54.refs_2_, bf16[1,512]{1,0:T(2,128)(2,1)} %reshape.135.refs_3_, ...), custom_call_target="tpu_custom_call" | custom-call | flops 1000000 | bytes 524288 | tf_op jit(solution)/shard_map/moe_line/pallas_call | solution.py:265
  814.9 6.3 convolution_convert_fusion.3.d_ref
  821.2 3.8 convolution_convert_fusion.1
  825.0 2.5 multiply_reduce_fusion.6
  827.5 21.7 %attend_back.1 = (f32[1024,512]{1,0:T(8,128)}, f32[1024,512]{1,0:T(8,128)}, bf16[1024,512]{1,0:T(8,128)(2,1)}) custom-call(bf16[1024,512]{1,0:T(8,128)(2,1)} %get-tuple-element.56.q_ref, bf16[1024,512]{1,0:T(8,128)(2,1)} %get-tuple-element.57.k_ref, bf16[1024,512]{1,0:T(8,128)(2,1)} %get-tuple-element.58.v_ref, ...), custom_call_target="tpu_custom_call" | custom-call | flops 5368709120 | bytes 10485760 | tf_op jit(solution)/shard_map/attend_back/pallas_call | solution.py:515
  849.2 4.2 multiply_reduce_fusion.1
  854.5 2.0 collective-permute-start.11
  860.1 1.8 collective-permute-done.9
  862.0 3.6 subtract_convert_fusion.1
  866.4 9.3 convolution_convert_fusion
  877.2 13.2 %concatenate.22 = bf16[2048,2176]{1,0:T(8,128)(2,1)} concatenate(bf16[2048,1536]{1,0:T(8,128)(2,1)} %convolution_convert_fusion, bf16[2048,512]{1,0:T(8,128)(2,1)S(1)} %copy-done.9, bf16[2048,4]{1,0:T(8,128)(2,1)} %copy.133, bf16[2048,124]{1,0:T(8,128)(2,1)} %broadcast_in_dim.66), dimensions={1} | concatenate | bytes 17825792 | tf_op jit(solution)/shard_map/concatenate | solution.py:844
  890.5 6.2 slice.124.refs_1_
  898.5 1.9 add_bitcast_fusion.2
  900.4 2.0 collective-permute-start.14
  902.4 2.0 collective-permute-start.13
  905.2 4.4 copy.137
  909.7 4.4 copy.135
  914.1 4.4 copy.136
  918.6 1.8 pad_maximum_fusion.2.refs_0_
  920.3 120.0 %input_line.1 = (f32[1024,512]{1,0:T(8,128)}, f32[1,512]{1,0:T(1,128)}) custom-call(bf16[1024,1536]{1,0:T(8,128)(2,1)} %pad_maximum_fusion.2.refs_0_, bf16[2048,1536]{1,0:T(8,128)(2,1)} %slice.124.refs_1_, bf16[1024,512]{1,0:T(8,128)(2,1)} %refs_2_.3, f32[1024,1]{1,0:T(8,128)} %get-tuple-element.63.refs_3_, bf16[1,512]{1,0:T(2,128)(2,1)} %reshape.132.refs_1_.refs_4_, ...), custom_call_target="tpu_custom_call" | custom-call | flops 1000000 | bytes 524288 | tf_op jit(solution)/shard_map/input_line/pallas_call | solution.py:265
  1042.8 12.5 %psum.7 = f32[4,512]{1,0:T(4,128)S(1)} all-reduce(f32[4,512]{1,0:T(4,128)S(1)} %pad_maximum_fusion.8), channel_id=1, replica_groups=mesh['row'=8,'col'=4] {'row'}, use_global_device_ids=true, to_apply=%region_11.12 | all-reduce | flops 2048 | bytes 16384 | tf_op jit(solution)/shard_map/psum | solution.py:853
  1056.0 4.6 fusion.6
  1062.2 2.6 fusion.25
  (167 shorter events, 38.8 us)
Async XLA Ops:
  7.2 4.3 copy-start.11
  7.2 110.5 %all-gather.6.cloned.1.call-start = ((), (), s32[]{:S(2)}) async-start(), calls=%async_computation.3 | async-start | bytes 10027008 | tf_op jit(solution)/shard_map/all_gather | solution.py:758
  11.5 377.2 %all-gather.8.cloned.1.call-start = ((), (), s32[]{:S(2)}) async-start(), calls=%async_computation.7 | async-start | bytes 28311552 | tf_op jit(solution)/shard_map/all_gather | solution.py:761
  16.4 500.0 %all-gather.10.cloned.1.call-start = ((), (), s32[]{:S(2)}) async-start(), calls=%async_computation.8 | async-start | bytes 28311552 | tf_op jit(solution)/shard_map/all_gather | solution.py:762
  19.2 92.0 %copy-start.31 = (bf16[512]{0:T(512)(128)(2,1)S(1)}, bf16[512]{0:T(512)(128)(2,1)}, u32[]{:S(2)}) copy-start(bf16[512]{0:T(512)(128)(2,1)} %param.20) | copy-start | bytes 3076
  19.2 92.6 %copy-start.25 = (bf16[512]{0:T(512)(128)(2,1)S(1)}, bf16[512]{0:T(512)(128)(2,1)}, u32[]{:S(2)}) copy-start(bf16[512]{0:T(512)(128)(2,1)} %param.18) | copy-start | bytes 3076
  19.2 93.2 %copy-start.27 = (bf16[512]{0:T(512)(128)(2,1)S(1)}, bf16[512]{0:T(512)(128)(2,1)}, u32[]{:S(2)}) copy-start(bf16[512]{0:T(512)(128)(2,1)} %param.19) | copy-start | bytes 3076
  19.2 93.7 %copy-start.24 = (s32[1024,8]{0,1:T(8,128)S(1)}, s32[1024,8]{0,1:T(8,128)}, u32[]{:S(2)}) copy-start(s32[1024,8]{0,1:T(8,128)} %param.29) | copy-start | bytes 98308
  19.2 94.1 %copy-start.32 = (s32[1,2]{1,0:T(1,128)S(1)}, s32[1,2]{1,0:T(1,128)}, u32[]{:S(2)}) copy-start(s32[1,2]{1,0:T(1,128)} %param.30) | copy-start | bytes 28
  19.3 808.3 %reduce-scatter.4.cloned.1.call-start = ((), (), s32[]{:S(2)}) async-start(), calls=%async_computation.4 | async-start | bytes 28311552 | tf_op jit(solution)/shard_map/reduce_scatter | solution.py:800
  108.8 257.8 %collective-permute-start.5 = (bf16[1024,512]{1,0:T(8,128)(2,1)}, bf16[1024,512]{1,0:T(8,128)(2,1)}, u32[]{:S(2)}, u32[]{:S(2)}) collective-permute-start(bf16[1024,512]{1,0:T(8,128)(2,1)} %broadcast_add_fusion), channel_id=1, source_target_pairs={{0,3},{1,0},{2,1},{3,2},{4,7},{5,4},{6,5},{7,6},{8,11},{9,8},{10,9... | collective-permute-start | bytes 3145736 | tf_op jit(solution)/shard_map/ppermute | solution.py:45
  110.6 256.9 %collective-permute-start.4 = (bf16[1024,512]{1,0:T(8,128)(2,1)}, bf16[1024,512]{1,0:T(8,128)(2,1)}, u32[]{:S(2)}, u32[]{:S(2)}) collective-permute-start(bf16[1024,512]{1,0:T(8,128)(2,1)} %broadcast_add_fusion), channel_id=1, source_target_pairs={{0,2},{1,3},{2,0},{3,1},{4,6},{5,7},{6,4},{7,5},{8,10},{9,11},{10,... | collective-permute-start | bytes 3145736 | tf_op jit(solution)/shard_map/ppermute | solution.py:45
  110.6 256.9 %collective-permute-start.3 = (bf16[1024,512]{1,0:T(8,128)(2,1)}, bf16[1024,512]{1,0:T(8,128)(2,1)}, u32[]{:S(2)}, u32[]{:S(2)}) collective-permute-start(bf16[1024,512]{1,0:T(8,128)(2,1)} %broadcast_add_fusion), channel_id=1, source_target_pairs={{0,1},{1,2},{2,3},{3,0},{4,5},{5,6},{6,7},{7,4},{8,9},{9,10},{10,1... | collective-permute-start | bytes 3145736 | tf_op jit(solution)/shard_map/ppermute | solution.py:45
  113.3 274.0 %copy-start.15 = (pred[1024,16]{1,0:T(8,128)(4,1)}, pred[1024,16]{1,0:T(8,128)(4,1)S(1)}, u32[]{:S(2)}) copy-start(pred[1024,16]{1,0:T(8,128)(4,1)S(1)} %copy.122) | copy-start | bytes 49156
  113.4 14.4 %copy-start.23 = (s32[1024]{0:T(1024)}, s32[1024]{0:T(1024)S(1)}, u32[]{:S(2)}) copy-start(s32[1024]{0:T(1024)S(1)} %fusion.16) | copy-start | bytes 12292
  127.8 74.1 %copy-start = (f32[1024,1536]{1,0:T(8,128)}, f32[1024,1536]{1,0:T(8,128)S(1)}, u32[]{:S(2)}) copy-start(f32[1024,1536]{1,0:T(8,128)S(1)} %fusion.19.q_ref.k_ref.v_ref) | copy-start | bytes 18874372
  128.1 70.8 %collective-permute-start.1 = (f32[2,1024]{1,0:T(2,128)S(1)}, f32[2,1024]{1,0:T(2,128)S(1)}, u32[]{:S(2)}, u32[]{:S(2)}) collective-permute-start(f32[2,1024]{1,0:T(2,128)S(1)} %pad_maximum_fusion.6), channel_id=1, source_target_pairs={{0,2},{1,3},{2,0},{3,1},{4,6},{5,7},{6,4},{7,5},{8,10},{9,11},{10,... | collective-permute-start | bytes 24584 | tf_op jit(solution)/shard_map/ppermute | solution.py:68
  130.8 76.0 %collective-permute-start.2 = (f32[2,1024]{1,0:T(2,128)S(1)}, f32[2,1024]{1,0:T(2,128)S(1)}, u32[]{:S(2)}, u32[]{:S(2)}) collective-permute-start(f32[2,1024]{1,0:T(2,128)S(1)} %pad_maximum_fusion.6), channel_id=1, source_target_pairs={{0,3},{1,0},{2,1},{3,2},{4,7},{5,4},{6,5},{7,6},{8,11},{9,8},{10,9... | collective-permute-start | bytes 24584 | tf_op jit(solution)/shard_map/ppermute | solution.py:68
  198.9 11.2 %collective-permute-start = (f32[2,1024]{1,0:T(2,128)S(1)}, f32[2,1024]{1,0:T(2,128)S(1)}, u32[]{:S(2)}, u32[]{:S(2)}) collective-permute-start(f32[2,1024]{1,0:T(2,128)S(1)} %pad_maximum_fusion.6), channel_id=1, source_target_pairs={{0,1},{1,2},{2,3},{3,0},{4,5},{5,6},{6,7},{7,4},{8,9},{9,10},{10,1... | collective-permute-start | bytes 24584 | tf_op jit(solution)/shard_map/ppermute | solution.py:68
  206.8 172.6 %collective-permute-start.7 = (bf16[4,2048]{0,1:T(8,128)(2,1)S(1)}, bf16[4,2048]{0,1:T(8,128)(2,1)}, u32[]{:S(2)}, u32[]{:S(2)}) collective-permute-start(bf16[4,2048]{0,1:T(8,128)(2,1)S(1)} %slice_bitcast_fusion), channel_id=1, source_target_pairs={{0,2},{1,3},{2,0},{3,1},{4,6},{5,7},{6,4},{7,5},{8,10},{9,11},{10,... | collective-permute-start | bytes 49160 | tf_op jit(solution)/shard_map/ppermute | solution.py:78
  210.2 166.1 %collective-permute-start.6 = (bf16[4,2048]{0,1:T(8,128)(2,1)S(1)}, bf16[4,2048]{0,1:T(8,128)(2,1)}, u32[]{:S(2)}, u32[]{:S(2)}) collective-permute-start(bf16[4,2048]{0,1:T(8,128)(2,1)S(1)} %slice_bitcast_fusion), channel_id=1, source_target_pairs={{0,1},{1,2},{2,3},{3,0},{4,5},{5,6},{6,7},{7,4},{8,9},{9,10},{10,1... | collective-permute-start | bytes 49160 | tf_op jit(solution)/shard_map/ppermute | solution.py:78
  366.6 11.6 %collective-permute-start.8 = (bf16[4,2048]{0,1:T(8,128)(2,1)S(1)}, bf16[4,2048]{0,1:T(8,128)(2,1)}, u32[]{:S(2)}, u32[]{:S(2)}) collective-permute-start(bf16[4,2048]{0,1:T(8,128)(2,1)S(1)} %slice_bitcast_fusion), channel_id=1, source_target_pairs={{0,3},{1,0},{2,1},{3,2},{4,7},{5,4},{6,5},{7,6},{8,11},{9,8},{10,9... | collective-permute-start | bytes 49160 | tf_op jit(solution)/shard_map/ppermute | solution.py:78
  516.4 342.6 %reduce-scatter.6.cloned.1.call-start = ((), (), s32[]{:S(2)}) async-start(), calls=%async_computation.5 | async-start | bytes 28311552 | tf_op jit(solution)/shard_map/reduce_scatter | solution.py:801
  649.8 410.7 %reduce-scatter.8.cloned.1.call-start = ((), (), s32[]{:S(2)}) async-start(), calls=%async_computation.6 | async-start | bytes 10027008 | tf_op jit(solution)/shard_map/reduce_scatter | solution.py:847
  650.4 174.6 %collective-permute-start.16 = (f32[16,1024]{0,1:T(8,128)}, f32[16,1024]{0,1:T(8,128)}, u32[]{:S(2)}, u32[]{:S(2)}) collective-permute-start(f32[16,1024]{0,1:T(8,128)} %bitcast.46), channel_id=1, source_target_pairs={{0,2},{1,3},{2,0},{3,1},{4,6},{5,7},{6,4},{7,5},{8,10},{9,11},{10,... | collective-permute-start | bytes 196616 | tf_op jit(solution)/shard_map/ppermute | solution.py:68
  650.5 174.5 %collective-permute-start.17 = (f32[16,1024]{0,1:T(8,128)}, f32[16,1024]{0,1:T(8,128)}, u32[]{:S(2)}, u32[]{:S(2)}) collective-permute-start(f32[16,1024]{0,1:T(8,128)} %bitcast.46), channel_id=1, source_target_pairs={{0,3},{1,0},{2,1},{3,2},{4,7},{5,4},{6,5},{7,6},{8,11},{9,8},{10,9... | collective-permute-start | bytes 196616 | tf_op jit(solution)/shard_map/ppermute | solution.py:68
  653.3 171.7 %collective-permute-start.15 = (f32[16,1024]{0,1:T(8,128)}, f32[16,1024]{0,1:T(8,128)}, u32[]{:S(2)}, u32[]{:S(2)}) collective-permute-start(f32[16,1024]{0,1:T(8,128)} %bitcast.46), channel_id=1, source_target_pairs={{0,1},{1,2},{2,3},{3,0},{4,5},{5,6},{6,7},{7,4},{8,9},{9,10},{10,1... | collective-permute-start | bytes 196616 | tf_op jit(solution)/shard_map/ppermute | solution.py:68
  814.9 6.3 copy-start.17
  814.9 6.3 copy-start.34
  849.2 7.8 copy-start.1
  849.2 7.8 copy-start.10
  853.5 6.7 collective-permute-start.10
  854.5 5.7 collective-permute-start.11
  856.5 5.4 collective-permute-start.9
  857.0 5.0 copy-start.3
  862.0 4.4 copy-start.33
  865.6 10.1 copy-start.5
  866.4 10.8 %copy-start.9 = (bf16[2048,512]{1,0:T(8,128)(2,1)S(1)}, bf16[2048,512]{1,0:T(8,128)(2,1)}, u32[]{:S(2)}) copy-start(bf16[2048,512]{1,0:T(8,128)(2,1)} %convolution_convert_fusion.1) | copy-start | bytes 6291460
  890.4 8.0 copy-start.2
  898.5 5.9 copy-start.7
  898.5 5.9 copy-start.8
  900.4 155.6 %collective-permute-start.12 = (bf16[1024,512]{1,0:T(8,128)(2,1)}, bf16[1024,512]{1,0:T(8,128)(2,1)}, u32[]{:S(2)}, u32[]{:S(2)}) collective-permute-start(bf16[1024,512]{1,0:T(8,128)(2,1)} %get-tuple-element.157), channel_id=1, source_target_pairs={{0,2},{1,3},{2,0},{3,1},{4,6},{5,7},{6,4},{7,5},{8,10},{9,11},{10,... | collective-permute-start | bytes 3145736 | tf_op jit(solution)/shard_map/ppermute | solution.py:45
  900.4 155.6 %collective-permute-start.14 = (bf16[1024,512]{1,0:T(8,128)(2,1)}, bf16[1024,512]{1,0:T(8,128)(2,1)}, u32[]{:S(2)}, u32[]{:S(2)}) collective-permute-start(bf16[1024,512]{1,0:T(8,128)(2,1)} %get-tuple-element.158), channel_id=1, source_target_pairs={{0,1},{1,2},{2,3},{3,0},{4,5},{5,6},{6,7},{7,4},{8,9},{9,10},{10,1... | collective-permute-start | bytes 3145736 | tf_op jit(solution)/shard_map/ppermute | solution.py:45
  902.4 153.5 %collective-permute-start.13 = (bf16[1024,512]{1,0:T(8,128)(2,1)}, bf16[1024,512]{1,0:T(8,128)(2,1)}, u32[]{:S(2)}, u32[]{:S(2)}) collective-permute-start(bf16[1024,512]{1,0:T(8,128)(2,1)} %get-tuple-element.159), channel_id=1, source_target_pairs={{0,3},{1,0},{2,1},{3,2},{4,7},{5,4},{6,5},{7,6},{8,11},{9,8},{10,9... | collective-permute-start | bytes 3145736 | tf_op jit(solution)/shard_map/ppermute | solution.py:45
  914.1 4.4 copy-start.6
  914.1 4.4 copy-start.19
  920.3 121.8 %copy-start.29 = (f32[1,512]{1,0:T(1,128)S(1)}, f32[1,512]{1,0:T(1,128)}, u32[]{:S(2)}) copy-start(f32[1,512]{1,0:T(1,128)} %get-tuple-element.67) | copy-start | bytes 6148
  1060.5 4.3 copy-start.14
  (11 other events, 22.4 us)
Sparse Core Ops, SparseCore 0:
  11.6 59.1 all-gather.5
  72.7 125.1 all-gather.7
  199.8 125.1 all-gather.9
  516.5 155.1 reduce-scatter.3
  675.1 156.2 reduce-scatter.5
  890.6 72.8 reduce-scatter.7

commit v3 on v2

--- a/solution.py
+++ b/solution.py
@@ -51,19 +51,9 @@
     return [far[k] for k in range(1, n)]
 
 
-def scatter_line(part):
+def sum_small(values, more=0.0):
     n = lax.axis_size("col")
-    me = lax.axis_index("col")
-    others = [
-        shift(part(lax.rem(me + k, n)).astype(BF), k) for k in (*range(2, n), 1)
-    ]
-    total = part(me).astype(F32)
-    return total, others
-
-
-def sum_small(values):
-    n = lax.axis_size("col")
-    total = values
+    total = values + more
     for k in range(1, n):
         total = total + lax.ppermute(values, "col", [(i, (i + k) % n) for i in range(n)])
     return total
@@ -167,14 +157,14 @@
                 term(at(c), me) + sums[0, me, at(c)].astype(F32) + sums[1, me, at(c)].astype(F32)
             )
         stat = jnp.broadcast_to(first(at(c), total), (CHUNK, 128))
-        stat_out[c] = stat.T[:8]
+        stat_out[c] = jnp.concatenate([stat] * (128 // CHUNK), axis=0).T[:8]
 
     def apply(c):
         row = stat_out[c]
         for k in range(1, n):
             stat_copy(k, c).wait_recv()
             row = row + stat_in[k, c]
-        stat = jnp.broadcast_to(row[:1], (128, CHUNK)).T[:, :1]
+        stat = jnp.broadcast_to(row[:1], (128, 128)).T[:CHUNK, :1]
         block = second(at(c), stat)
         if out is not None:
             part = out.shape[1] // n
@@ -247,7 +237,7 @@
     lax.fori_loop(0, chunks, drain, 0)
 
 
-def along_line(make, operands, out_shape, rows, part, sums, gathers, number, name, others=()):
+def along_line(make, operands, out_shape, rows, part, sums, gathers, number, name):
     n = lax.axis_size("col")
     chunks = rows // CHUNK
     vmem = pl.BlockSpec(memory_space=pltpu.VMEM)
@@ -264,7 +254,7 @@
         scratch += [pltpu.SemaphoreType.DMA((2, 2, n, chunks))]
     return pl.pallas_call(
         functools.partial(line_kernel, n, make, len(operands), len(out_shape)),
-        in_specs=[vmem] * (len(operands) - len(others)) + list(others),
+        in_specs=[vmem] * len(operands),
         out_specs=[vmem] * len(out_shape),
         out_shape=out_shape,
         scratch_shapes=scratch,
@@ -333,11 +323,11 @@
     )
 
 
-def moe_line(terms, hidden, inv, gain, grads, earlier, width):
+def moe_line(terms, hidden, inv, gain, grads, width):
     rows, part = hidden.shape
 
     def make(ins, outs):
-        t_ref, hidden_ref, inv_ref, gain_ref, y_ref, _ = ins
+        t_ref, hidden_ref, inv_ref, gain_ref, y_ref = ins
         out_ref, grad_ref, d_gain_ref = outs
         d_gain_ref[...] = jnp.zeros_like(d_gain_ref)
 
@@ -367,8 +357,7 @@
         jax.ShapeDtypeStruct((1, part), F32),
     ]
     return along_line(
-        make, [terms, hidden, inv, gain, grads, earlier], out_shape, rows, part, True, True, 3,
-        "moe_line", [pl.BlockSpec(memory_space=pl.ANY)],
+        make, [terms, hidden, inv, gain, grads], out_shape, rows, part, True, True, 3, "moe_line"
     )
 
 
@@ -535,7 +524,7 @@
 
 
 def prepare_kernel(n, x_ref, own_ref, *refs):
-    pieces, (xt_ref, y_ref, yt_ref) = refs[: n - 1], refs[n - 1 :]
+    pieces, (_, xt_ref, y_ref, yt_ref) = refs[: n - 1], refs[n - 1 :]
     part = own_ref.shape[1]
     me = lax.axis_index("col")
     for s in range(n):
@@ -547,7 +536,7 @@
         yt_ref[cols, :] = piece[...].T
 
 
-def prepare(x, own, pieces):
+def prepare(x, own, pieces, earlier):
     rows, width = x.shape
     part = own.shape[1]
     n = width // part
@@ -559,7 +548,7 @@
     return pl.pallas_call(
         functools.partial(prepare_kernel, n),
         grid=(rows // step,),
-        in_specs=[wide] + [block] * n,
+        in_specs=[wide] + [block] * n + [pl.BlockSpec(memory_space=pl.ANY)],
         out_specs=[tall, wide, tall],
         out_shape=[out(width, rows), out(rows, width), out(width, rows)],
         compiler_params=pltpu.CompilerParams(vmem_limit_bytes=VMEM_LIMIT),
@@ -567,20 +556,126 @@
             flops=0, bytes_accessed=10 * rows * width, transcendentals=0
         ),
         name="prepare",
-    )(x, own, *pieces)
-
-
-def moe_kernel(
-    first, n_col, closing, x_ref, xt_ref, y_ref, yt_ref, gates_ref, w_ref, *rest
+    )(x, own, *pieces, earlier)
+
+
+def gate_of(gates_ref, at, span, expert):
+    experts = gates_ref.shape[1]
+    mine = lax.broadcasted_iota(jnp.int32, (span, experts), 1) == expert
+    return mine, jnp.sum(jnp.where(mine, gates_ref[at, :], 0.0), axis=1, keepdims=True)
+
+
+def forward_kernel(first, n_col, closing, x_ref, gates_ref, w_ref, *rest):
+    if closing:
+        first_ref, *rest = rest
+    out_ref, pre_ref, up_ref, acc, hid = rest
+    step = pl.program_id(0)
+    rows, width = x_ref.shape
+    units = w_ref.shape[-1]
+
+    @pl.when(step == 0)
+    def _():
+        acc[...] = jnp.zeros_like(acc)
+
+    w_gate = w_ref[:, 0, 0].reshape(width, units)
+    w_up = w_ref[:, 0, 1].reshape(width, units)
+    span = min(256, rows)
+    for start in range(0, rows, span):
+        at = slice(start, start + span)
+        g, u = dot_nn(x_ref[at, :], w_gate), dot_nn(x_ref[at, :], w_up)
+        _, gate = gate_of(gates_ref, at, span, step + first)
+        hid[at, :] = (gate * (g / (1.0 + jnp.exp(-g)) * u)).astype(BF)
+        pre_ref[0, at, :] = g.astype(BF)
+        up_ref[0, at, :] = u.astype(BF)
+
+    w_down = w_ref[:, 0, 2].reshape(width, units)
+    part = width // n_col
+    for s in range(n_col):
+        cols = slice(s * part, (s + 1) * part)
+        acc[:, cols] += dot_nt(hid[...], w_down[cols, :])
+
+    @pl.when(step == pl.num_programs(0) - 1)
+    def _():
+        for s in range(n_col):
+            total = acc[:, s * part : (s + 1) * part]
+            if closing:
+                total = total + first_ref[s].astype(F32)
+            out_ref[s] = total.astype(BF)
+
+
+def once(shape):
+    return pl.BlockSpec(shape, lambda e: (0,) * len(shape), pipeline_mode=pl.Buffered(1))
+
+
+def each(shape):
+    return pl.BlockSpec((1, *shape), lambda e: (e,) + (0,) * len(shape))
+
+
+def moe_forward(first, x, gates, weights, before):
+    rows, width = x.shape
+    n_row, here, _, depth, units = weights.shape
+    n_col = lax.axis_size("col")
+    block = pl.BlockSpec((n_row, 1, 3, depth, units), lambda e: (0, e, 0, 0, 0))
+    blocks = (n_col, rows, width // n_col)
+    more = [] if before is None else [before]
+    hidden = jax.ShapeDtypeStruct((here, rows, units), BF)
+    return pl.pallas_call(
+        functools.partial(forward_kernel, first, n_col, before is not None),
+        grid=(here,),
+        in_specs=[once((rows, width)), once(gates.shape), block] + [once(a.shape) for a in more],
+        out_specs=[once(blocks), each((rows, units)), each((rows, units))],
+        out_shape=[jax.ShapeDtypeStruct(blocks, BF), hidden, hidden],
+        scratch_shapes=[pltpu.VMEM((rows, width), F32)]
+        + [pltpu.VMEM((rows, units), BF)],
+        compiler_params=pltpu.CompilerParams(vmem_limit_bytes=VMEM_LIMIT),
+        cost_estimate=pl.CostEstimate(
+            flops=6 * here * rows * width * units,
+            bytes_accessed=6 * here * n_row * depth * units + 8 * rows * width,
+            transcendentals=here * rows * units,
+        ),
+        name="experts_forward",
+    )(x, gates, weights, *more)
+
+
+def backward_kernel(
+    first, n_col, closing, xt_ref, y_ref, yt_ref, gates_ref, w_ref, pre_ref, up_ref, *rest
 ):
     if closing:
         probs_ref, before_ref, router_ref, first_ref, *rest = rest
-    dx_ref, dw_ref, hid_ref, dg_ref, acc, pre, up, grad, d_pre, d_up = rest
+        dx_ref, dw_ref, dg_ref, acc, hid, d_pre, d_up = rest
+    else:
+        parts_ref, dx_ref, dw_ref, dg_ref, got_ref, acc, hid, d_pre, d_up, sems = rest
     step = pl.program_id(0)
-    expert = step + first
-    rows, width = x_ref.shape
+    rows, width = y_ref.shape
+    me = lax.axis_index("col")
+
+    def part_copy(k):
+        other = lax.rem(me + k, n_col)
+        return pltpu.make_async_remote_copy(
+            src_ref=parts_ref.at[other], dst_ref=got_ref.at[k - 1], send_sem=sems.at[0, k - 1],
+            recv_sem=sems.at[1, k - 1], device_id={"col": other},
+            device_id_type=pl.DeviceIdType.MESH,
+        )
+
+    if not closing:
+        @pl.when(step == 0)
+        def _():
+            barrier = pltpu.get_barrier_semaphore()
+            for k in range(1, n_col):
+                pl.semaphore_signal(
+                    barrier, inc=1, device_id={"col": lax.rem(me + k, n_col)},
+                    device_id_type=pl.DeviceIdType.MESH,
+                )
+            pl.semaphore_wait(barrier, n_col - 1)
+            for k in range(1, n_col):
+                part_copy(k).start()
+
+        @pl.when(step == pl.num_programs(0) - 1)
+        def _():
+            for k in range(1, n_col):
+                part_copy(k).wait()
+
     n_row, _, _, depth, units = w_ref.shape
-    experts = gates_ref.shape[1]
 
     @pl.when(step == 0)
     def _():
@@ -590,33 +685,26 @@
     w_gate = w_ref[:, 0, 0].reshape(width, units)
     w_up = w_ref[:, 0, 1].reshape(width, units)
     w_down = w_ref[:, 0, 2].reshape(width, units)
-    pre[...] = dot_nn(x_ref[...], w_gate)
-    up[...] = dot_nn(x_ref[...], w_up)
-    grad[...] = dot_nn(y_ref[...], w_down)
-
-    span = 32
-
-    def activate(i, carry):
-        at = pl.ds(pl.multiple_of(i * span, span), span)
-        g, u, dh = pre[at, :], up[at, :], grad[at, :]
-        mine = lax.broadcasted_iota(jnp.int32, (span, experts), 1) == expert
-        gate = jnp.sum(jnp.where(mine, gates_ref[at, :], 0.0), axis=1, keepdims=True)
+    span = min(256, rows)
+
+    for start in range(0, rows, span):
+        at = slice(start, start + span)
+        dh = dot_nn(y_ref[at, :], w_down)
+        g, u = pre_ref[0, at, :].astype(F32), up_ref[0, at, :].astype(F32)
+        mine, gate = gate_of(gates_ref, at, span, step + first)
         s = 1.0 / (1.0 + jnp.exp(-g))
         silu = g * s
         both = silu * u
-        hid_ref[0, at, :] = (gate * both).astype(BF)
+        hid[at, :] = (gate * both).astype(BF)
         d_gate = jnp.sum(dh * both, axis=1, keepdims=True)
         dg_ref[at, :] += jnp.where(mine, d_gate, 0.0)
         act = dh * gate
         d_pre[at, :] = (act * u * (s * (1.0 + g * (1.0 - s)))).astype(BF)
         d_up[at, :] = (act * silu).astype(BF)
-        return carry
-
-    lax.fori_loop(0, rows // span, activate, 0)
 
     dw_ref[:, 0, 0] = dot_nn(xt_ref[...], d_pre[...]).astype(BF).reshape(n_row, depth, units)
     dw_ref[:, 0, 1] = dot_nn(xt_ref[...], d_up[...]).astype(BF).reshape(n_row, depth, units)
-    dw_ref[:, 0, 2] = dot_nn(yt_ref[...], hid_ref[0]).astype(BF).reshape(n_row, depth, units)
+    dw_ref[:, 0, 2] = dot_nn(yt_ref[...], hid[...]).astype(BF).reshape(n_row, depth, units)
     part = width // n_col
     for s in range(n_col):
         cols = slice(s * part, (s + 1) * part)
@@ -636,102 +724,46 @@
             dx_ref[s] = total.astype(BF)
 
 
-def moe_half(first, x, xt, y, yt, gates, weights, closing):
-    rows, width = x.shape
+def moe_backward(first, xt, y, yt, gates, weights, pre, up, parts, closing):
+    rows, width = y.shape
     n_row, here, _, depth, units = weights.shape
-    experts = gates.shape[1]
     n_col = lax.axis_size("col")
-    once = lambda shape: pl.BlockSpec(
-        shape, lambda e: (0,) * len(shape), pipeline_mode=pl.Buffered(1)
-    )
     block = pl.BlockSpec((n_row, 1, 3, depth, units), lambda e: (0, e, 0, 0, 0))
-    operands = [x, xt, y, yt, gates, weights]
-    in_specs = [
-        once((rows, width)), once((width, rows)), once((rows, width)), once((width, rows)),
-        once((rows, experts)), block,
-    ]
-    if closing is not None:
-        operands += list(closing)
-        in_specs += [once(a.shape) for a in closing]
+    blocks = (n_col, rows, width // n_col)
+    any_place = pl.BlockSpec(memory_space=pl.ANY)
+    more = [parts] if closing is None else list(closing)
+    more_specs = [any_place] if closing is None else [once(a.shape) for a in more]
+    got, got_specs, sems, extra = [], [], [], {}
+    if closing is None:
+        got = [jax.ShapeDtypeStruct((n_col - 1, rows, width // n_col), BF)]
+        got_specs = [any_place]
+        sems = [pltpu.SemaphoreType.DMA((2, n_col - 1))]
+        extra = {"collective_id": 5, "has_side_effects": True}
     return pl.pallas_call(
-        functools.partial(moe_kernel, first, n_col, closing is not None),
+        functools.partial(backward_kernel, first, n_col, closing is not None),
         grid=(here,),
-        in_specs=in_specs,
-        out_specs=[
-            once((n_col, rows, width // n_col)), block,
-            pl.BlockSpec((1, rows, units), lambda e: (e, 0, 0)), once((rows, experts)),
-        ],
+        in_specs=[
+            once((width, rows)), once((rows, width)), once((width, rows)), once(gates.shape),
+            block, each((rows, units)), each((rows, units)),
+        ]
+        + more_specs,
+        out_specs=[once(blocks), block, once(gates.shape)] + got_specs,
         out_shape=[
-            jax.ShapeDtypeStruct((n_col, rows, width // n_col), BF),
-            jax.ShapeDtypeStruct(weights.shape, BF),
-            jax.ShapeDtypeStruct((here, rows, units), BF),
-            jax.ShapeDtypeStruct((rows, experts), F32),
-        ],
+            jax.ShapeDtypeStruct(blocks, BF), jax.ShapeDtypeStruct(weights.shape, BF),
+            jax.ShapeDtypeStruct(gates.shape, F32),
+        ]
+        + got,
         scratch_shapes=[pltpu.VMEM((rows, width), F32)]
-        + [pltpu.VMEM((rows, units), F32)] * 3
-        + [pltpu.VMEM((rows, units), BF)] * 2,
-        compiler_params=pltpu.CompilerParams(vmem_limit_bytes=VMEM_LIMIT),
+        + [pltpu.VMEM((rows, units), BF)] * 3
+        + sems,
+        compiler_params=pltpu.CompilerParams(vmem_limit_bytes=VMEM_LIMIT, **extra),
         cost_estimate=pl.CostEstimate(
-            flops=16 * here * rows * width * units,
+            flops=12 * here * rows * width * units,
             bytes_accessed=12 * here * n_row * depth * units + 12 * rows * width,
             transcendentals=here * rows * units,
         ),
-        name="experts",
-    )(*operands)
-
-
-def down_kernel(n_col, hid_a, hid_b, w_a, w_b, out_ref, acc):
-    step = pl.program_id(0)
-    half = pl.num_programs(0) // 2
-    rows, width = acc.shape
-    part = width // n_col
-
-    @pl.when(step == 0)
-    def _():
-        acc[...] = jnp.zeros_like(acc)
-
-    def add(hid, weight):
-        w_down = weight[:, 0, 0].reshape(width, weight.shape[-1])
-        for s in range(n_col):
-            cols = slice(s * part, (s + 1) * part)
-            acc[:, cols] += dot_nt(hid[0], w_down[cols, :])
-
-    pl.when(step < half)(lambda: add(hid_a, w_a))
-    pl.when(step >= half)(lambda: add(hid_b, w_b))
-
-    @pl.when(step == 2 * half - 1)
-    def _():
-        for s in range(n_col):
-            out_ref[s] = acc[:, s * part : (s + 1) * part].astype(BF)
-
-
-def down(hid_a, hid_b, weights_a, weights_b):
-    half, rows, units = hid_a.shape
-    n_row, _, _, depth, _ = weights_a.shape
-    width = n_row * depth
-    n_col = lax.axis_size("col")
-    low = lambda e: jnp.minimum(e, half - 1)
-    high = lambda e: jnp.maximum(e - half, 0)
-    return pl.pallas_call(
-        functools.partial(down_kernel, n_col),
-        grid=(2 * half,),
-        in_specs=[
-            pl.BlockSpec((1, rows, units), lambda e: (low(e), 0, 0)),
-            pl.BlockSpec((1, rows, units), lambda e: (high(e), 0, 0)),
-            pl.BlockSpec((n_row, 1, 1, depth, units), lambda e: (0, low(e), 2, 0, 0)),
-            pl.BlockSpec((n_row, 1, 1, depth, units), lambda e: (0, high(e), 2, 0, 0)),
-        ],
-        out_specs=pl.BlockSpec((n_col, rows, width // n_col), lambda e: (0, 0, 0)),
-        out_shape=jax.ShapeDtypeStruct((n_col, rows, width // n_col), BF),
-        scratch_shapes=[pltpu.VMEM((rows, width), F32)],
-        compiler_params=pltpu.CompilerParams(vmem_limit_bytes=VMEM_LIMIT),
-        cost_estimate=pl.CostEstimate(
-            flops=4 * half * rows * width * units,
-            bytes_accessed=4 * half * (width + rows) * units + 2 * rows * width,
-            transcendentals=0,
-        ),
-        name="down",
-    )(hid_a, hid_b, weights_a, weights_b)
+        name="experts_backward",
+    )(xt, y, yt, gates, weights, pre, up, *more)
 
 
 def pack_experts(w_gate, w_up, w_down, first, last):
@@ -763,7 +795,6 @@
 
     attn_gain = norm_attn.reshape(1, part)
     normed_attn, inv_first = norm_line(tokens, attn_gain, width)
-    grad_pieces = pieces_line(cotangent + zero_of(normed_attn))
     qkv = dot_nn(normed_attn, full_qkv)
     query_raw, key_raw = qkv[:, :part], qkv[:, part : 2 * part]
 
@@ -782,7 +813,7 @@
 
     moe_gain = norm_moe.reshape(1, part)
     normed_moe, hidden_state, inv_second = attn_line(mixed, full_out, tokens, moe_gain, width)
-    normed_moe_t, grad_full, grad_full_t = prepare(normed_moe, cotangent, grad_pieces)
+    grad_pieces = pieces_line(cotangent + zero_of(normed_moe))
 
     router_t = gather_small(mats[:, 4 * part : 4 * part + cols].T).reshape(experts, width)
     router_probs = jax.nn.softmax(dot_nt(normed_moe, router_t), axis=1)
@@ -790,23 +821,24 @@
     routed = jnp.any(routes[:, :, None] == expert_ids[None, None, :], axis=1)
     gate_table = jnp.where(routed, router_probs, 0.0)
 
-    dx_a, dw_a, hid_a, dg_a = moe_half(
-        0, normed_moe, normed_moe_t, grad_full, grad_full_t, gate_table, first_half, None
-    )
-    dx_b, dw_b, hid_b, dg_b = moe_half(
-        half, normed_moe, normed_moe_t, grad_full, grad_full_t, gate_table, second_half,
-        (router_probs, dg_a, router_t, dx_a),
+    part_a, pre_a, up_a = moe_forward(0, normed_moe, gate_table, first_half, None)
+    moe_parts, pre_b, up_b = moe_forward(half, normed_moe, gate_table, second_half, part_a)
+    normed_moe_t, grad_full, grad_full_t = prepare(normed_moe, cotangent, grad_pieces, up_b)
+    dx_a, dw_a, dg_a, other_parts = moe_backward(
+        0, normed_moe_t, grad_full, grad_full_t, gate_table, first_half, pre_a, up_a, moe_parts,
+        None,
+    )
+    own_part = lax.dynamic_index_in_dim(moe_parts, me, 0, keepdims=False).astype(F32)
+    output = (hidden_state + own_part + jnp.sum(other_parts.astype(F32), axis=0)).astype(BF)
+    dx_b, dw_b, dg_b = moe_backward(
+        half, normed_moe_t, grad_full, grad_full_t, gate_table, second_half, pre_b, up_b,
+        None, (router_probs, dg_a, router_t, dx_a),
     )
     summed_a = lax.psum_scatter(dw_a, "row", scatter_dimension=0)
     summed_b = lax.psum_scatter(dw_b, "row", scatter_dimension=0)
-    moe_parts = down(hid_a, hid_b, first_half, second_half)
-
     attn_grad, hidden_grad, d_moe_gain = moe_line(
-        dx_b, hidden_state, inv_second, moe_gain, cotangent, moe_parts, width
-    )
-    parted = zero_of(attn_grad)
-    pick = lambda s: lax.dynamic_index_in_dim(moe_parts, s, 0, keepdims=False) + parted
-    own_part, other_parts = scatter_line(pick)
+        dx_b, hidden_state, inv_second, moe_gain, cotangent, width
+    )
     mixed_grad = dot_nn(attn_grad, full_out).astype(BF)
     d_out_w = dot_tn(attn_grad, mixed)
 
@@ -834,24 +866,21 @@
     )
     d_qkv_w = dot_tn(normed_attn, qkv_grad)
 
-    gate_grad = jnp.where(routed, sum_small(dg_b.T).T, 0.0)
+    gate_grad = jnp.where(routed, sum_small(dg_b.T, zero_of(attn_grad)).T, 0.0)
     logit_low = (
         router_probs * (gate_grad - jnp.sum(router_probs * gate_grad, axis=1, keepdims=True))
     ).astype(BF)
     d_router_w = dot_tn(normed_moe, lax.dynamic_slice_in_dim(logit_low, me * cols, cols, 1))
 
-    spare = jnp.broadcast_to(summed_b[0, 0, 0, 0], (width, -cols % 128))
+    spare = jnp.zeros((width, -cols % 128), BF)
     d_mats = jnp.concatenate(
         [d_qkv_w.astype(BF), d_out_w.astype(BF), d_router_w.astype(BF), spare], axis=1
     )
     summed = lax.psum_scatter(
         row_major(d_mats), "row", scatter_dimension=0, tiled=True
     ).astype(F32)
-    others = functools.reduce(lambda a, b: a + b.astype(F32), other_parts, zero_of(d_tokens))
-    output = (hidden_state + own_part + others).astype(BF)
-
     gains = lax.psum(jnp.stack([d_attn_gain[0], d_query_gain, d_key_gain, d_moe_gain[0]]), "row")
-    expert_grads = jnp.concatenate([summed_a, summed_b], axis=0)
+    expert_grads = jnp.concatenate([summed_a, summed_b], axis=0) + zero_of(d_tokens)
     unpack = lambda i: jnp.transpose(expert_grads[:, i], (1, 0, 2)).astype(F32)
     cut = lambda i: summed[:, i * part : (i + 1) * part]
     return (

time: 1080 us -> 994 us (0.920)
  Pallas kernels: 811 us -> 758 us
  waiting for transfers between devices: 66.3 us -> 14.7 us
  starting transfers between devices: 24.2 us -> 39.9 us
    pallas_call x3 -> x4, Pallas kernels: 288 us -> 232 us  [the longest x2 162 us: moe_backward(): pl.pallas_call(functools.partial(backward_kernel, first, n_col, closing i...]
    ppermute x9, waiting for transfers between devices: 66.2 us -> 14.6 us  [sum_small(): lax.ppermute(values, 'col', [(i, (i + k) % n) for i in range(n)])]
    ppermute x9, starting transfers between devices: 13.1 us -> 32.6 us  [sum_small(): lax.ppermute(values, 'col', [(i, (i + k) % n) for i in range(n)])]
  transfers between devices with their start and end apart: 24 -> 21, of which waited for: 2 -> 4; matrix products, arithmetic and copies ran while one was open for 9% -> 13% of each run, Pallas kernels for 76% -> 67%
where the time goes in v3:
time: 994 us; the launch traced here: 985 us
  Pallas kernels  758 us (76%)
  local copies, waits for them, and re-layouts  75.8 us (8%)
  starting transfers between devices  39.9 us (4%)
  matrix products  34 us (3%)
  other arithmetic  32.9 us (3%)
  between operations  17 us (2%)
  waiting for transfers between devices  14.7 us (1%)
  blocking collectives  12.5 us (1%)
    pallas_call x4, Pallas kernels, along_line(): pl.pallas_call(functools.partial(line_kernel, n, make, len(operands), len...  480 us
    pallas_call x2, Pallas kernels, moe_backward(): pl.pallas_call(functools.partial(backward_kernel, first, n_col, closing i...  162 us
    pallas_call x2, Pallas kernels, moe_forward(): pl.pallas_call(functools.partial(forward_kernel, first, n_col, before is...  70.5 us
    ppermute x9, starting transfers between devices, sum_small(): lax.ppermute(values, 'col', [(i, (i + k) % n) for i in range(n)])  32.6 us
    unnamed x78, local copies, waits for them, and re-layouts  21.6 us
    pallas_call x1, Pallas kernels, attend_back(): pl.pallas_call(functools.partial(attend_back_kernel, 1.0 / math.sqrt(HD),...  21.2 us
  transfers between devices with their start and end apart: 21, of which 4 were waited for; matrix products, arithmetic and copies ran while one was open for 13% of the time, Pallas kernels for 67%

profile of v3, /device:TPU:0, one launch (start us, length us, event | category | flops | bytes accessed | tf_op | source)
XLA Modules:
  0.0 985.2 jit_solution(5189040618512800060)
XLA Ops:
  8.2 3.2 concatenate.18
  14.4 2.0 pad_maximum_fusion.1
  17.1 2.0 pad_maximum_fusion
  23.7 84.1 %norm_line.1 = (bf16[1024,2048]{1,0:T(8,128)(2,1)}, f32[1024,1]{1,0:T(8,128)}) custom-call(bf16[1024,512]{1,0:T(8,128)(2,1)} %refs_2_.3, bf16[1,512]{1,0:T(2,128)(2,1)} %reshape.122.refs_1_.refs_4_), custom_call_target="tpu_custom_call" | custom-call | flops 1000000 | bytes 524288 | tf_op jit(solution)/shard_map/norm_line/pallas_call | solution.py:255
  107.9 2.0 fusion.10
  112.3 2.4 collective-permute-start.4
  114.7 10.0 %fusion.14.q_ref.k_ref.v_ref = f32[1024,1536]{1,0:T(8,128)S(1)} fusion(bf16[1024,2048]{1,0:T(8,128)(2,1)} %get-tuple-element.47, bf16[2048,2176]{1,0:T(8,128)(2,1)} %all-gather.6.cloned.1.call-done), kind=kOutput, calls=%fused_computation.72 | convolution fusion | flops 6442450944 | bytes 16777216 | tf_op jit(solution)/shard_map/dot_general | solution.py:24
  125.1 2.0 collective-permute-start
  127.1 2.4 collective-permute-start.2
  131.3 2.0 bitcast_dynamic-update-slice_fusion
  133.3 3.0 slice.125.refs_1_
  138.5 9.9 %collective-permute-done.1 = f32[2,1024]{1,0:T(2,128)S(1)} collective-permute-done((f32[2,1024]{1,0:T(2,128)S(1)}, f32[2,1024]{1,0:T(2,128)S(1)}, u32[]{:S(2)}, u32[]{:S(2)}) %collective-permute-start.1) | collective-permute-done | bytes 8224 | tf_op jit(solution)/shard_map/ppermute | solution.py:58
  151.0 16.7 %attend.1 = (bf16[1024,512]{1,0:T(8,128)(2,1)}, bf16[1024,512]{1,0:T(8,128)(2,1)}, bf16[1024,512]{1,0:T(8,128)(2,1)}, bf16[1024,512]{1,0:T(8,128)(2,1)}) custom-call(f32[1024,1536]{1,0:T(8,128)} %copy-done, f32[1024,1536]{1,0:T(8,128)} %copy-done, f32[1024,1536]{1,0:T(8,128)} %copy-done, f32[1024,1]{1,0:T(8,128)} %copy.116.iq_ref, f32[1024,1]{1,0:T(8,128)} %copy.117.ik_ref, ...), custom_call_target="tpu_custom_call" | custom-call | flops 2147483648 | bytes 10485760 | tf_op jit(solution)/shard_map/attend/pallas_call | solution.py:448
  167.7 143.8 %attn_line.1 = (bf16[1024,2048]{1,0:T(8,128)(2,1)}, f32[1024,512]{1,0:T(8,128)}, f32[1024,1]{1,0:T(8,128)}) custom-call(bf16[1024,512]{1,0:T(8,128)(2,1)} %get-tuple-element.48.refs_0_, bf16[2048,512]{1,0:T(8,128)(2,1)} %slice.125.refs_1_, bf16[1024,512]{1,0:T(8,128)(2,1)} %refs_2_.3, bf16[1,512]{1,0:T(2,128)(2,1)} %reshape.125.refs_3_), custom_call_target="tpu_custom_call" | custom-call | flops 1000000 | bytes 524288 | tf_op jit(solution)/shard_map/attn_line/pallas_call | solution.py:255
  313.4 2.3 broadcast_add_fusion
  315.6 1.8 collective-permute-start.7
  317.4 2.0 collective-permute-start.8
  319.4 1.9 bitcast_dynamic-update-slice_fusion.2
  321.3 1.9 bitcast_dynamic-update-slice_fusion.1
  323.2 2.2 copy.119
  326.7 3.4 fusion.24
  332.0 34.4 %experts_forward.2 = (bf16[4,1024,512]{2,1,0:T(8,128)(2,1)}, bf16[8,1024,256]{2,1,0:T(8,128)(2,1)}, bf16[8,1024,256]{2,1,0:T(8,128)(2,1)}) custom-call(bf16[1024,2048]{1,0:T(8,128)(2,1)} %get-tuple-element.50.x_ref, f32[1024,16]{1,0:T(8,128)} %get-tuple-element.160.gates_ref, bf16[8,8,3,256,256]{4,3,2,1,0:T(8,128)(2,1)} %bitcast.135), custom_call_target="tpu_custom_call" | custom-call | flops 25769803776 | bytes 41943040 | tf_op jit(solution)/shard_map/experts_forward/pallas_call | solution.py:622
  366.4 36.1 %experts_forward.3 = (bf16[4,1024,512]{2,1,0:T(8,128)(2,1)}, bf16[8,1024,256]{2,1,0:T(8,128)(2,1)}, bf16[8,1024,256]{2,1,0:T(8,128)(2,1)}) custom-call(bf16[1024,2048]{1,0:T(8,128)(2,1)} %get-tuple-element.50.x_ref, f32[1024,16]{1,0:T(8,128)} %get-tuple-element.160.gates_ref, bf16[8,8,3,256,256]{4,3,2,1,0:T(8,128)(2,1)} %bitcast.137, ...), custom_call_target="tpu_custom_call" | custom-call | flops 25769803776 | bytes 41943040 | tf_op jit(solution)/shard_map/experts_forward/pallas_call | solution.py:622
  402.6 8.9 prepare.1
  411.4 90.7 %experts_backward.2 = (bf16[4,1024,512]{2,1,0:T(8,128)(2,1)}, bf16[8,8,3,256,256]{4,3,2,1,0:T(8,128)(2,1)}, f32[1024,16]{1,0:T(8,128)}, bf16[3,1024,512]{2,1,0:T(8,128)(2,1)}) custom-call(bf16[2048,1024]{1,0:T(8,128)(2,1)} %get-tuple-element.54.xt_ref, bf16[1024,2048]{1,0:T(8,128)(2,1)} %get-tuple-element.55.y_ref, ...), custom_call_target="tpu_custom_call" | custom-call | flops 51539607552 | bytes 75497472 | tf_op jit(solution)/shard_map/experts_backward/pallas_call | solution.py:742
  502.2 70.9 %experts_backward.3 = (bf16[4,1024,512]{2,1,0:T(8,128)(2,1)}, bf16[8,8,3,256,256]{4,3,2,1,0:T(8,128)(2,1)}, f32[1024,16]{1,0:T(8,128)}) custom-call(bf16[2048,1024]{1,0:T(8,128)(2,1)} %get-tuple-element.54.xt_ref, bf16[1024,2048]{1,0:T(8,128)(2,1)} %get-tuple-element.55.y_ref, bf16[2048,1024]{1,0:T(8,128)(2,1)} %get-tuple-element.56.yt_ref, ...), custom_call_target="tpu_custom_call" | custom-call | flops 51539607552 | bytes 75497472 | tf_op jit(solution)/shard_map/experts_backward/pallas_call | solution.py:742
  573.8 23.1 %collective-permute-start.12 = (f32[16,1024]{0,1:T(8,128)}, f32[16,1024]{0,1:T(8,128)}, u32[]{:S(2)}, u32[]{:S(2)}) collective-permute-start(f32[16,1024]{0,1:T(8,128)} %bitcast.41), channel_id=1, source_target_pairs={{0,1},{1,2},{2,3},{3,0},{4,5},{5,6},{6,7},{7,4},{8,9},{9,10},{10,1... | collective-permute-start | bytes 196616 | tf_op jit(solution)/shard_map/ppermute | solution.py:58
  599.4 162.5 %moe_line.1 = (bf16[1024,2048]{1,0:T(8,128)(2,1)}, f32[1024,512]{1,0:T(8,128)}, f32[1,512]{1,0:T(1,128)}) custom-call(bf16[4,1024,512]{2,1,0:T(8,128)(2,1)} %get-tuple-element.66.refs_0_, f32[1024,512]{1,0:T(8,128)} %get-tuple-element.49.refs_1_, f32[1024,1]{1,0:T(8,128)} %get-tuple-element.67.refs_2_, bf16[1,512]{1,0:T(2,128)(2,1)} %reshape.125.refs_3_, ...), custom_call_target="tpu_custom_call" | custom-call | flops 1000000 | bytes 524288 | tf_op jit(solution)/shard_map/moe_line/pallas_call | solution.py:255
  761.9 6.4 convolution_convert_fusion.3.d_ref
  768.4 3.8 convolution_convert_fusion.1
  773.4 2.5 multiply_reduce_fusion.6
  775.9 21.2 %attend_back.1 = (f32[1024,512]{1,0:T(8,128)}, f32[1024,512]{1,0:T(8,128)}, bf16[1024,512]{1,0:T(8,128)(2,1)}) custom-call(bf16[1024,512]{1,0:T(8,128)(2,1)} %get-tuple-element.60.q_ref, bf16[1024,512]{1,0:T(8,128)(2,1)} %get-tuple-element.61.k_ref, bf16[1024,512]{1,0:T(8,128)(2,1)} %get-tuple-element.62.v_ref, ...), custom_call_target="tpu_custom_call" | custom-call | flops 5368709120 | bytes 10485760 | tf_op jit(solution)/shard_map/attend_back/pallas_call | solution.py:504
  797.2 4.2 multiply_reduce_fusion.1
  801.5 1.9 collective-permute-start.11
  806.0 3.2 collective-permute-done.9
  809.3 3.7 subtract_convert_fusion.1
  813.9 9.4 convolution_convert_fusion
  824.1 13.2 %concatenate.22 = bf16[2048,2176]{1,0:T(8,128)(2,1)} concatenate(bf16[2048,1536]{1,0:T(8,128)(2,1)} %convolution_convert_fusion, bf16[2048,512]{1,0:T(8,128)(2,1)S(1)} %copy-done.8, bf16[2048,4]{1,0:T(8,128)(2,1)} %copy.133, bf16[2048,124]{1,0:T(8,128)(2,1)} %broadcast_in_dim.66), dimensions={1} | concatenate | bytes 17825792 | tf_op jit(solution)/shard_map/concatenate | solution.py:876
  837.4 6.1 slice.120.refs_1_
  845.1 3.0 fusion.1
  848.0 1.8 pad_maximum_fusion.2.refs_0_
  849.8 89.1 %input_line.1 = (f32[1024,512]{1,0:T(8,128)}, f32[1,512]{1,0:T(1,128)}) custom-call(bf16[1024,1536]{1,0:T(8,128)(2,1)} %pad_maximum_fusion.2.refs_0_, bf16[2048,1536]{1,0:T(8,128)(2,1)} %slice.120.refs_1_, bf16[1024,512]{1,0:T(8,128)(2,1)} %refs_2_.3, f32[1024,1]{1,0:T(8,128)} %get-tuple-element.73.refs_3_, bf16[1,512]{1,0:T(2,128)(2,1)} %reshape.122.refs_1_.refs_4_, ...), custom_call_target="tpu_custom_call" | custom-call | flops 1000000 | bytes 524288 | tf_op jit(solution)/shard_map/input_line/pallas_call | solution.py:255
  940.8 3.8 maximum_add_fusion
  946.2 4.4 copy.135
  950.7 4.4 copy.136
  955.1 4.4 copy.137
  959.6 12.5 %psum.7 = f32[4,512]{1,0:T(4,128)S(1)} all-reduce(f32[4,512]{1,0:T(4,128)S(1)} %pad_maximum_fusion.7), channel_id=1, replica_groups=mesh['row'=8,'col'=4] {'row'}, use_global_device_ids=true, to_apply=%region_12.13 | all-reduce | flops 2048 | bytes 16384 | tf_op jit(solution)/shard_map/psum | solution.py:882
  974.2 2.6 fusion.20
  (162 shorter events, 38.8 us)
Async XLA Ops:
  7.2 4.3 copy-start.9
  7.2 104.0 %all-gather.6.cloned.1.call-start = ((), (), s32[]{:S(2)}) async-start(), calls=%async_computation.3 | async-start | bytes 10027008 | tf_op jit(solution)/shard_map/all_gather | solution.py:790
  11.5 320.6 %all-gather.10.cloned.1.call-start = ((), (), s32[]{:S(2)}) async-start(), calls=%async_computation.8 | async-start | bytes 28311552 | tf_op jit(solution)/shard_map/all_gather | solution.py:793
  11.7 2.1 copy-start.11
  16.4 350.0 %all-gather.8.cloned.1.call-start = ((), (), s32[]{:S(2)}) async-start(), calls=%async_computation.7 | async-start | bytes 28311552 | tf_op jit(solution)/shard_map/all_gather | solution.py:794
  19.2 2.4 copy-start.24
  19.2 3.0 copy-start.26
  19.2 3.6 copy-start.31
  19.2 4.1 copy-start.23
  19.2 756.7 %reduce-scatter.4.cloned.1.call-start = ((), (), s32[]{:S(2)}) async-start(), calls=%async_computation.4 | async-start | bytes 28311552 | tf_op jit(solution)/shard_map/reduce_scatter | solution.py:837
  20.5 91.7 %copy-start.22 = (s32[1024]{0:T(1024)}, s32[1024]{0:T(1024)S(1)}, u32[]{:S(2)}) copy-start(s32[1024]{0:T(1024)S(1)} %fusion.11) | copy-start | bytes 12292
  23.7 307.0 %copy-start.14 = (pred[1024,16]{1,0:T(8,128)(4,1)}, pred[1024,16]{1,0:T(8,128)(4,1)S(1)}, u32[]{:S(2)}) copy-start(pred[1024,16]{1,0:T(8,128)(4,1)S(1)} %copy.122) | copy-start | bytes 49156
  112.2 205.2 %collective-permute-start.3 = (bf16[4,2048]{0,1:T(8,128)(2,1)S(1)}, bf16[4,2048]{0,1:T(8,128)(2,1)}, u32[]{:S(2)}, u32[]{:S(2)}) collective-permute-start(bf16[4,2048]{0,1:T(8,128)(2,1)S(1)} %slice_bitcast_fusion.3), channel_id=1, source_target_pairs={{0,1},{1,2},{2,3},{3,0},{4,5},{5,6},{6,7},{7,4},{8,9},{9,10},{10,1... | collective-permute-start | bytes 49160 | tf_op jit(solution)/shard_map/ppermute | solution.py:68
  112.3 209.0 %collective-permute-start.4 = (bf16[4,2048]{0,1:T(8,128)(2,1)S(1)}, bf16[4,2048]{0,1:T(8,128)(2,1)}, u32[]{:S(2)}, u32[]{:S(2)}) collective-permute-start(bf16[4,2048]{0,1:T(8,128)(2,1)S(1)} %slice_bitcast_fusion.3), channel_id=1, source_target_pairs={{0,2},{1,3},{2,0},{3,1},{4,6},{5,7},{6,4},{7,5},{8,10},{9,11},{10,... | collective-permute-start | bytes 49160 | tf_op jit(solution)/shard_map/ppermute | solution.py:68
  124.7 6.5 copy-start
  125.1 12.6 %collective-permute-start = (f32[2,1024]{1,0:T(2,128)S(1)}, f32[2,1024]{1,0:T(2,128)S(1)}, u32[]{:S(2)}, u32[]{:S(2)}) collective-permute-start(f32[2,1024]{1,0:T(2,128)S(1)} %pad_maximum_fusion.5), channel_id=1, source_target_pairs={{0,1},{1,2},{2,3},{3,0},{4,5},{5,6},{6,7},{7,4},{8,9},{9,10},{10,1... | collective-permute-start | bytes 24584 | tf_op jit(solution)/shard_map/ppermute | solution.py:58
  127.1 21.2 %collective-permute-start.1 = (f32[2,1024]{1,0:T(2,128)S(1)}, f32[2,1024]{1,0:T(2,128)S(1)}, u32[]{:S(2)}, u32[]{:S(2)}) collective-permute-start(f32[2,1024]{1,0:T(2,128)S(1)} %pad_maximum_fusion.5), channel_id=1, source_target_pairs={{0,2},{1,3},{2,0},{3,1},{4,6},{5,7},{6,4},{7,5},{8,10},{9,11},{10,... | collective-permute-start | bytes 24584 | tf_op jit(solution)/shard_map/ppermute | solution.py:58
  127.1 21.2 %collective-permute-start.2 = (f32[2,1024]{1,0:T(2,128)S(1)}, f32[2,1024]{1,0:T(2,128)S(1)}, u32[]{:S(2)}, u32[]{:S(2)}) collective-permute-start(f32[2,1024]{1,0:T(2,128)S(1)} %pad_maximum_fusion.5), channel_id=1, source_target_pairs={{0,3},{1,0},{2,1},{3,2},{4,7},{5,4},{6,5},{7,6},{8,11},{9,8},{10,9... | collective-permute-start | bytes 24584 | tf_op jit(solution)/shard_map/ppermute | solution.py:58
  137.7 187.7 %collective-permute-start.5 = (bf16[4,2048]{0,1:T(8,128)(2,1)S(1)}, bf16[4,2048]{0,1:T(8,128)(2,1)}, u32[]{:S(2)}, u32[]{:S(2)}) collective-permute-start(bf16[4,2048]{0,1:T(8,128)(2,1)S(1)} %slice_bitcast_fusion.3), channel_id=1, source_target_pairs={{0,3},{1,0},{2,1},{3,2},{4,7},{5,4},{6,5},{7,6},{8,11},{9,8},{10,9... | collective-permute-start | bytes 49160 | tf_op jit(solution)/shard_map/ppermute | solution.py:68
  315.6 86.9 %collective-permute-start.6 = (bf16[1024,512]{1,0:T(8,128)(2,1)}, bf16[1024,512]{1,0:T(8,128)(2,1)}, u32[]{:S(2)}, u32[]{:S(2)}) collective-permute-start(bf16[1024,512]{1,0:T(8,128)(2,1)} %broadcast_add_fusion), channel_id=1, source_target_pairs={{0,1},{1,2},{2,3},{3,0},{4,5},{5,6},{6,7},{7,4},{8,9},{9,10},{10,1... | collective-permute-start | bytes 3145736 | tf_op jit(solution)/shard_map/ppermute | solution.py:45
  315.6 86.9 %collective-permute-start.7 = (bf16[1024,512]{1,0:T(8,128)(2,1)}, bf16[1024,512]{1,0:T(8,128)(2,1)}, u32[]{:S(2)}, u32[]{:S(2)}) collective-permute-start(bf16[1024,512]{1,0:T(8,128)(2,1)} %broadcast_add_fusion), channel_id=1, source_target_pairs={{0,2},{1,3},{2,0},{3,1},{4,6},{5,7},{6,4},{7,5},{8,10},{9,11},{10,... | collective-permute-start | bytes 3145736 | tf_op jit(solution)/shard_map/ppermute | solution.py:45
  317.4 85.1 %collective-permute-start.8 = (bf16[1024,512]{1,0:T(8,128)(2,1)}, bf16[1024,512]{1,0:T(8,128)(2,1)}, u32[]{:S(2)}, u32[]{:S(2)}) collective-permute-start(bf16[1024,512]{1,0:T(8,128)(2,1)} %broadcast_add_fusion), channel_id=1, source_target_pairs={{0,3},{1,0},{2,1},{3,2},{4,7},{5,4},{6,5},{7,6},{8,11},{9,8},{10,9... | collective-permute-start | bytes 3145736 | tf_op jit(solution)/shard_map/ppermute | solution.py:45
  326.7 4.0 copy-start.19
  502.1 438.7 %reduce-scatter.8.cloned.1.call-start = ((), (), s32[]{:S(2)}) async-start(), calls=%async_computation.6 | async-start | bytes 28311552 | tf_op jit(solution)/shard_map/reduce_scatter | solution.py:838
  573.2 399.5 %reduce-scatter.6.cloned.1.call-start = ((), (), s32[]{:S(2)}) async-start(), calls=%async_computation.5 | async-start | bytes 10027008 | tf_op jit(solution)/shard_map/reduce_scatter | solution.py:879
  573.8 199.5 %collective-permute-start.12 = (f32[16,1024]{0,1:T(8,128)}, f32[16,1024]{0,1:T(8,128)}, u32[]{:S(2)}, u32[]{:S(2)}) collective-permute-start(f32[16,1024]{0,1:T(8,128)} %bitcast.41), channel_id=1, source_target_pairs={{0,1},{1,2},{2,3},{3,0},{4,5},{5,6},{6,7},{7,4},{8,9},{9,10},{10,1... | collective-permute-start | bytes 196616 | tf_op jit(solution)/shard_map/ppermute | solution.py:58
  597.0 176.4 %collective-permute-start.13 = (f32[16,1024]{0,1:T(8,128)}, f32[16,1024]{0,1:T(8,128)}, u32[]{:S(2)}, u32[]{:S(2)}) collective-permute-start(f32[16,1024]{0,1:T(8,128)} %bitcast.41), channel_id=1, source_target_pairs={{0,2},{1,3},{2,0},{3,1},{4,6},{5,7},{6,4},{7,5},{8,10},{9,11},{10,... | collective-permute-start | bytes 196616 | tf_op jit(solution)/shard_map/ppermute | solution.py:58
  598.0 175.4 %collective-permute-start.14 = (f32[16,1024]{0,1:T(8,128)}, f32[16,1024]{0,1:T(8,128)}, u32[]{:S(2)}, u32[]{:S(2)}) collective-permute-start(f32[16,1024]{0,1:T(8,128)} %bitcast.41), channel_id=1, source_target_pairs={{0,3},{1,0},{2,1},{3,2},{4,7},{5,4},{6,5},{7,6},{8,11},{9,8},{10,9... | collective-permute-start | bytes 196616 | tf_op jit(solution)/shard_map/ppermute | solution.py:58
  761.9 6.5 copy-start.16
  761.9 6.5 copy-start.34
  768.4 5.0 copy-start.4
  768.4 5.0 copy-start.15
  797.2 6.8 copy-start.1
  797.2 6.8 copy-start.13
  801.4 4.6 collective-permute-start.10
  801.5 4.5 collective-permute-start.11
  803.4 5.8 collective-permute-start.9
  804.0 5.3 copy-start.3
  809.3 3.7 copy-start.17
  809.3 4.6 copy-start.33
  813.0 10.3 %copy-start.5 = (bf16[1024,512]{1,0:T(8,128)(2,1)}, bf16[1024,512]{1,0:T(8,128)(2,1)S(1)}, u32[]{:S(2)}) copy-start(bf16[1024,512]{1,0:T(8,128)(2,1)S(1)} %get-tuple-element.166) | copy-start | bytes 3145732
  813.9 10.3 %copy-start.8 = (bf16[2048,512]{1,0:T(8,128)(2,1)S(1)}, bf16[2048,512]{1,0:T(8,128)(2,1)}, u32[]{:S(2)}) copy-start(bf16[2048,512]{1,0:T(8,128)(2,1)} %convolution_convert_fusion.1) | copy-start | bytes 6291460
  837.4 6.1 copy-start.7
  845.1 3.0 copy-start.6
  845.1 3.0 copy-start.18
  955.1 4.5 copy-start.28
  955.1 4.5 copy-start.29
  959.6 17.2 %copy-start.12 = (f32[1024,512]{1,0:T(8,128)S(1)}, f32[1024,512]{1,0:T(8,128)}, u32[]{:S(2)}) copy-start(f32[1024,512]{1,0:T(8,128)} %get-tuple-element.217) | copy-start | bytes 6291460
  (8 other events, 7.9 us)
Sparse Core Ops, SparseCore 0:
  11.6 59.1 all-gather.5
  73.3 125.1 all-gather.9
  200.4 125.1 all-gather.7
  502.2 176.5 reduce-scatter.3
  682.3 156.3 reduce-scatter.7
  842.1 74.1 reduce-scatter.5

commit v4 on v3

--- a/solution.py
+++ b/solution.py
@@ -184,7 +184,7 @@
                 gather_copy(way, s, c, me + step).start()
 
     lag = 0 if term is None else n - 1
-    last = lag + 1 + (0 if out is None else n)
+    last = lag + (1 if out is None else n)
 
     def body(t, carry):
         def stage(delay, action):
@@ -192,8 +192,8 @@
             pl.when(jnp.logical_and(c >= 0, c < chunks))(lambda: action(c))
 
         if out is not None:
-            for r in range(n - 1, -1, -1):
-                stage(lag + 2 + r, lambda c: pass_on(c, r))
+            for r in range(n - 1, 0, -1):
+                stage(lag + 1 + r, lambda c: pass_on(c, r))
         if term is not None:
             on_turn(t, hops[0], ready)
             for hop, later in zip(hops, hops[1:]):
@@ -201,19 +201,21 @@
                 on_turn(t, later, ready)
                 on_turn(t, hop, send)
             on_turn(t, hops[-1], add)
+        stage(lag + 1, apply)
         stage(lag, finish)
         if term is not None:
             on_turn(t, hops[-1], send)
-        stage(lag + 1, apply)
 
         def tell(c):
             for k in range(1, n):
                 stat_copy(k, c).start()
 
         stage(lag, tell)
+        if out is not None:
+            stage(lag + 1, lambda c: pass_on(c, 0))
         return carry
 
-    lax.fori_loop(0, chunks + last + 1, body, 0)
+    lax.fori_loop(0, chunks + last, body, 0)
 
     def drain(c, carry):
         for k in range(1, n):
@@ -642,38 +644,36 @@
 ):
     if closing:
         probs_ref, before_ref, router_ref, first_ref, *rest = rest
-        dx_ref, dw_ref, dg_ref, acc, hid, d_pre, d_up = rest
-    else:
-        parts_ref, dx_ref, dw_ref, dg_ref, got_ref, acc, hid, d_pre, d_up, sems = rest
+    parts_ref, dx_ref, dw_ref, dg_ref, got_ref, acc, hid, d_pre, d_up, sems = rest
     step = pl.program_id(0)
     rows, width = y_ref.shape
     me = lax.axis_index("col")
 
     def part_copy(k):
         other = lax.rem(me + k, n_col)
+        count = rows // 2
         return pltpu.make_async_remote_copy(
-            src_ref=parts_ref.at[other], dst_ref=got_ref.at[k - 1], send_sem=sems.at[0, k - 1],
+            src_ref=parts_ref.at[other, pl.ds(count if closing else 0, count)], dst_ref=got_ref.at[k - 1], send_sem=sems.at[0, k - 1],
             recv_sem=sems.at[1, k - 1], device_id={"col": other},
             device_id_type=pl.DeviceIdType.MESH,
         )
 
-    if not closing:
-        @pl.when(step == 0)
-        def _():
-            barrier = pltpu.get_barrier_semaphore()
-            for k in range(1, n_col):
-                pl.semaphore_signal(
-                    barrier, inc=1, device_id={"col": lax.rem(me + k, n_col)},
-                    device_id_type=pl.DeviceIdType.MESH,
-                )
-            pl.semaphore_wait(barrier, n_col - 1)
-            for k in range(1, n_col):
-                part_copy(k).start()
-
-        @pl.when(step == pl.num_programs(0) - 1)
-        def _():
-            for k in range(1, n_col):
-                part_copy(k).wait()
+    @pl.when(step == 0)
+    def _():
+        barrier = pltpu.get_barrier_semaphore()
+        for k in range(1, n_col):
+            pl.semaphore_signal(
+                barrier, inc=1, device_id={"col": lax.rem(me + k, n_col)},
+                device_id_type=pl.DeviceIdType.MESH,
+            )
+        pl.semaphore_wait(barrier, n_col - 1)
+        for k in range(1, n_col):
+            part_copy(k).start()
+
+    @pl.when(step == pl.num_programs(0) - 1)
+    def _():
+        for k in range(1, n_col):
+            part_copy(k).wait()
 
     n_row, _, _, depth, units = w_ref.shape
 
@@ -731,14 +731,12 @@
     block = pl.BlockSpec((n_row, 1, 3, depth, units), lambda e: (0, e, 0, 0, 0))
     blocks = (n_col, rows, width // n_col)
     any_place = pl.BlockSpec(memory_space=pl.ANY)
-    more = [parts] if closing is None else list(closing)
-    more_specs = [any_place] if closing is None else [once(a.shape) for a in more]
-    got, got_specs, sems, extra = [], [], [], {}
-    if closing is None:
-        got = [jax.ShapeDtypeStruct((n_col - 1, rows, width // n_col), BF)]
-        got_specs = [any_place]
-        sems = [pltpu.SemaphoreType.DMA((2, n_col - 1))]
-        extra = {"collective_id": 5, "has_side_effects": True}
+    more = list(closing or ())
+    more_specs = [once(a.shape) for a in more] + [any_place]
+    more.append(parts)
+    got = [jax.ShapeDtypeStruct((n_col - 1, rows // 2, width // n_col), BF)]
+    sems = [pltpu.SemaphoreType.DMA((2, n_col - 1))]
+    extra = {"collective_id": 5 if closing is None else 6, "has_side_effects": True}
     return pl.pallas_call(
         functools.partial(backward_kernel, first, n_col, closing is not None),
         grid=(here,),
@@ -747,7 +745,7 @@
             block, each((rows, units)), each((rows, units)),
         ]
         + more_specs,
-        out_specs=[once(blocks), block, once(gates.shape)] + got_specs,
+        out_specs=[once(blocks), block, once(gates.shape), any_place],
         out_shape=[
             jax.ShapeDtypeStruct(blocks, BF), jax.ShapeDtypeStruct(weights.shape, BF),
             jax.ShapeDtypeStruct(gates.shape, F32),
@@ -824,15 +822,13 @@
     part_a, pre_a, up_a = moe_forward(0, normed_moe, gate_table, first_half, None)
     moe_parts, pre_b, up_b = moe_forward(half, normed_moe, gate_table, second_half, part_a)
     normed_moe_t, grad_full, grad_full_t = prepare(normed_moe, cotangent, grad_pieces, up_b)
-    dx_a, dw_a, dg_a, other_parts = moe_backward(
+    dx_a, dw_a, dg_a, parts_a = moe_backward(
         0, normed_moe_t, grad_full, grad_full_t, gate_table, first_half, pre_a, up_a, moe_parts,
         None,
     )
-    own_part = lax.dynamic_index_in_dim(moe_parts, me, 0, keepdims=False).astype(F32)
-    output = (hidden_state + own_part + jnp.sum(other_parts.astype(F32), axis=0)).astype(BF)
-    dx_b, dw_b, dg_b = moe_backward(
+    dx_b, dw_b, dg_b, parts_b = moe_backward(
         half, normed_moe_t, grad_full, grad_full_t, gate_table, second_half, pre_b, up_b,
-        None, (router_probs, dg_a, router_t, dx_a),
+        moe_parts, (router_probs, dg_a, router_t, dx_a),
     )
     summed_a = lax.psum_scatter(dw_a, "row", scatter_dimension=0)
     summed_b = lax.psum_scatter(dw_b, "row", scatter_dimension=0)
@@ -866,7 +862,7 @@
     )
     d_qkv_w = dot_tn(normed_attn, qkv_grad)
 
-    gate_grad = jnp.where(routed, sum_small(dg_b.T, zero_of(attn_grad)).T, 0.0)
+    gate_grad = jnp.where(routed, sum_small(dg_b.T + zero_of(attn_grad), zero_of(query_turned)).T, 0.0)
     logit_low = (
         router_probs * (gate_grad - jnp.sum(router_probs * gate_grad, axis=1, keepdims=True))
     ).astype(BF)
@@ -879,6 +875,10 @@
     summed = lax.psum_scatter(
         row_major(d_mats), "row", scatter_dimension=0, tiled=True
     ).astype(F32)
+    own_part = lax.dynamic_index_in_dim(moe_parts, me, 0, keepdims=False).astype(F32)
+    other_parts = jnp.concatenate([parts_a, parts_b], axis=1) + zero_of(d_tokens)
+    output = (hidden_state + own_part + jnp.sum(other_parts.astype(F32), axis=0)).astype(BF)
+
     gains = lax.psum(jnp.stack([d_attn_gain[0], d_query_gain, d_key_gain, d_moe_gain[0]]), "row")
     expert_grads = jnp.concatenate([summed_a, summed_b], axis=0) + zero_of(d_tokens)
     unpack = lambda i: jnp.transpose(expert_grads[:, i], (1, 0, 2)).astype(F32)

time: 994 us -> 923 us (0.929)
  Pallas kernels: 758 us -> 694 us
  starting transfers between devices: 39.9 us -> 22.4 us
    pallas_call x4, Pallas kernels: 480 us -> 432 us  [along_line(): pl.pallas_call(functools.partial(line_kernel, n, make, len(operands), len...]
    ppermute x9, starting transfers between devices: 32.6 us -> 12.4 us  [sum_small(): lax.ppermute(values, 'col', [(i, (i + k) % n) for i in range(n)])]
    pallas_call x2, Pallas kernels: 162 us -> 145 us  [moe_backward(): pl.pallas_call(functools.partial(backward_kernel, first, n_col, closing i...]
    unnamed x78 -> x72, local copies, waits for them, and re-layouts: 21.6 us -> 20.4 us
  transfers between devices with their start and end apart: 21 -> 21, of which waited for: 4 -> 1; matrix products, arithmetic and copies ran while one was open for 13% -> 15% of each run, Pallas kernels for 67% -> 68%
where the time goes in v4:
time: 923 us; the launch traced here: 905 us
  Pallas kernels  694 us (75%)
  local copies, waits for them, and re-layouts  75.7 us (8%)
  matrix products  37.3 us (4%)
  other arithmetic  35.7 us (4%)
  starting transfers between devices  22.4 us (2%)
  between operations  17.6 us (2%)
  blocking collectives  12.2 us (1%)
  waiting for transfers between devices  9.52 us (1%)
    pallas_call x4, Pallas kernels, along_line(): pl.pallas_call(functools.partial(line_kernel, n, make, len(operands), len...  432 us
    pallas_call x2, Pallas kernels, moe_backward(): pl.pallas_call(functools.partial(backward_kernel, first, n_col, closing i...  145 us
    pallas_call x2, Pallas kernels, moe_forward(): pl.pallas_call(functools.partial(forward_kernel, first, n_col, before is...  70.4 us
    pallas_call x1, Pallas kernels, attend_back(): pl.pallas_call(functools.partial(attend_back_kernel, 1.0 / math.sqrt(HD),...  21.4 us
    unnamed x72, local copies, waits for them, and re-layouts  20.4 us
    dot_general x3, matrix products, dot_tn(): lax.dot_general(a, b, (((0,), (0,)), ((), ())), preferred_element_type=F32)  19 us
  transfers between devices with their start and end apart: 21, of which 1 were waited for; matrix products, arithmetic and copies ran while one was open for 15% of the time, Pallas kernels for 68%

profile of v4, /device:TPU:0, one launch (start us, length us, event | category | flops | bytes accessed | tf_op | source)
XLA Modules:
  0.0 904.9 jit_solution(8156104294266487350)
XLA Ops:
  8.2 3.2 concatenate.21
  14.4 2.0 pad_maximum_fusion.1
  17.1 2.1 pad_maximum_fusion
  23.8 84.4 %norm_line.1 = (bf16[1024,2048]{1,0:T(8,128)(2,1)}, f32[1024,1]{1,0:T(8,128)}) custom-call(bf16[1024,512]{1,0:T(8,128)(2,1)} %refs_2_.3, bf16[1,512]{1,0:T(2,128)(2,1)} %reshape.128.refs_1_.refs_4_), custom_call_target="tpu_custom_call" | custom-call | flops 1000000 | bytes 524288 | tf_op jit(solution)/shard_map/norm_line/pallas_call | solution.py:257
  108.2 2.0 fusion.10
  111.5 10.0 %fusion.14.q_ref.k_ref.v_ref = f32[1024,1536]{1,0:T(8,128)S(1)} fusion(bf16[1024,2048]{1,0:T(8,128)(2,1)} %get-tuple-element.48, bf16[2048,2176]{1,0:T(8,128)(2,1)} %all-gather.6.cloned.1.call-done), kind=kOutput, calls=%fused_computation.74 | convolution fusion | flops 6442450944 | bytes 16777216 | tf_op jit(solution)/shard_map/dot_general | solution.py:24
  121.9 1.8 collective-permute-start.2
  125.5 3.1 collective-permute-start.3
  130.9 1.9 bitcast_dynamic-update-slice_fusion
  132.7 3.0 slice.130.refs_1_
  135.8 2.2 collective-permute-start.5
  137.9 9.4 %collective-permute-done.1 = f32[2,1024]{1,0:T(2,128)S(1)} collective-permute-done((f32[2,1024]{1,0:T(2,128)S(1)}, f32[2,1024]{1,0:T(2,128)S(1)}, u32[]{:S(2)}, u32[]{:S(2)}) %collective-permute-start.1) | collective-permute-done | bytes 8224 | tf_op jit(solution)/shard_map/ppermute | solution.py:58
  150.0 16.7 %attend.1 = (bf16[1024,512]{1,0:T(8,128)(2,1)}, bf16[1024,512]{1,0:T(8,128)(2,1)}, bf16[1024,512]{1,0:T(8,128)(2,1)}, bf16[1024,512]{1,0:T(8,128)(2,1)}) custom-call(f32[1024,1536]{1,0:T(8,128)} %copy-done, f32[1024,1536]{1,0:T(8,128)} %copy-done, f32[1024,1536]{1,0:T(8,128)} %copy-done, f32[1024,1]{1,0:T(8,128)} %copy.116.iq_ref, f32[1024,1]{1,0:T(8,128)} %copy.117.ik_ref, ...), custom_call_target="tpu_custom_call" | custom-call | flops 2147483648 | bytes 10485760 | tf_op jit(solution)/shard_map/attend/pallas_call | solution.py:450
  166.7 148.7 %attn_line.1 = (bf16[1024,2048]{1,0:T(8,128)(2,1)}, f32[1024,512]{1,0:T(8,128)}, f32[1024,1]{1,0:T(8,128)}) custom-call(bf16[1024,512]{1,0:T(8,128)(2,1)} %get-tuple-element.49.refs_0_, bf16[2048,512]{1,0:T(8,128)(2,1)} %slice.130.refs_1_, bf16[1024,512]{1,0:T(8,128)(2,1)} %refs_2_.3, bf16[1,512]{1,0:T(2,128)(2,1)} %reshape.131.refs_3_), custom_call_target="tpu_custom_call" | custom-call | flops 1000000 | bytes 524288 | tf_op jit(solution)/shard_map/attn_line/pallas_call | solution.py:257
  317.2 2.3 broadcast_add_fusion
  319.5 3.8 collective-permute-start.8
  323.3 2.0 bitcast_dynamic-update-slice_fusion.2
  325.3 1.9 bitcast_dynamic-update-slice_fusion.1
  327.2 2.0 copy.119
  330.5 3.4 fusion.24
  335.8 34.4 %experts_forward.2 = (bf16[4,1024,512]{2,1,0:T(8,128)(2,1)}, bf16[8,1024,256]{2,1,0:T(8,128)(2,1)}, bf16[8,1024,256]{2,1,0:T(8,128)(2,1)}) custom-call(bf16[1024,2048]{1,0:T(8,128)(2,1)} %get-tuple-element.51.x_ref, f32[1024,16]{1,0:T(8,128)} %get-tuple-element.162.gates_ref, bf16[8,8,3,256,256]{4,3,2,1,0:T(8,128)(2,1)} %bitcast.138), custom_call_target="tpu_custom_call" | custom-call | flops 25769803776 | bytes 41943040 | tf_op jit(solution)/shard_map/experts_forward/pallas_call | solution.py:624
  370.2 36.0 %experts_forward.3 = (bf16[4,1024,512]{2,1,0:T(8,128)(2,1)}, bf16[8,1024,256]{2,1,0:T(8,128)(2,1)}, bf16[8,1024,256]{2,1,0:T(8,128)(2,1)}) custom-call(bf16[1024,2048]{1,0:T(8,128)(2,1)} %get-tuple-element.51.x_ref, f32[1024,16]{1,0:T(8,128)} %get-tuple-element.162.gates_ref, bf16[8,8,3,256,256]{4,3,2,1,0:T(8,128)(2,1)} %bitcast.140, ...), custom_call_target="tpu_custom_call" | custom-call | flops 25769803776 | bytes 41943040 | tf_op jit(solution)/shard_map/experts_forward/pallas_call | solution.py:624
  406.2 8.9 prepare.1
  415.1 70.8 %experts_backward.2 = (bf16[4,1024,512]{2,1,0:T(8,128)(2,1)}, bf16[8,8,3,256,256]{4,3,2,1,0:T(8,128)(2,1)}, f32[1024,16]{1,0:T(8,128)}, bf16[3,512,512]{2,1,0:T(8,128)(2,1)}) custom-call(bf16[2048,1024]{1,0:T(8,128)(2,1)} %get-tuple-element.55.xt_ref, bf16[1024,2048]{1,0:T(8,128)(2,1)} %get-tuple-element.56.y_ref, ...), custom_call_target="tpu_custom_call" | custom-call | flops 51539607552 | bytes 75497472 | tf_op jit(solution)/shard_map/experts_backward/pallas_call | solution.py:740
  486.0 73.9 %experts_backward.3 = (bf16[4,1024,512]{2,1,0:T(8,128)(2,1)}, bf16[8,8,3,256,256]{4,3,2,1,0:T(8,128)(2,1)}, f32[1024,16]{1,0:T(8,128)}, bf16[3,512,512]{2,1,0:T(8,128)(2,1)}) custom-call(bf16[2048,1024]{1,0:T(8,128)(2,1)} %get-tuple-element.55.xt_ref, bf16[1024,2048]{1,0:T(8,128)(2,1)} %get-tuple-element.56.y_ref, ...), custom_call_target="tpu_custom_call" | custom-call | flops 51539607552 | bytes 75497472 | tf_op jit(solution)/shard_map/experts_backward/pallas_call | solution.py:740
  560.6 131.3 %moe_line.1 = (bf16[1024,2048]{1,0:T(8,128)(2,1)}, f32[1024,512]{1,0:T(8,128)}, f32[1,512]{1,0:T(1,128)}) custom-call(bf16[4,1024,512]{2,1,0:T(8,128)(2,1)} %get-tuple-element.68.refs_0_, f32[1024,512]{1,0:T(8,128)} %get-tuple-element.50.refs_1_, f32[1024,1]{1,0:T(8,128)} %get-tuple-element.69.refs_2_, bf16[1,512]{1,0:T(2,128)(2,1)} %reshape.131.refs_3_, ...), custom_call_target="tpu_custom_call" | custom-call | flops 1000000 | bytes 524288 | tf_op jit(solution)/shard_map/moe_line/pallas_call | solution.py:257
  694.6 4.2 collective-permute-start.14
  699.6 6.3 convolution_convert_fusion.1
  705.9 4.9 convolution_convert_fusion.3.d_ref
  710.8 21.4 %attend_back.1 = (f32[1024,512]{1,0:T(8,128)}, f32[1024,512]{1,0:T(8,128)}, bf16[1024,512]{1,0:T(8,128)(2,1)}) custom-call(bf16[1024,512]{1,0:T(8,128)(2,1)} %get-tuple-element.65.q_ref, bf16[1024,512]{1,0:T(8,128)(2,1)} %get-tuple-element.66.k_ref, bf16[1024,512]{1,0:T(8,128)(2,1)} %get-tuple-element.67.v_ref, ...), custom_call_target="tpu_custom_call" | custom-call | flops 5368709120 | bytes 10485760 | tf_op jit(solution)/shard_map/attend_back/pallas_call | solution.py:506
  732.2 4.6 multiply_reduce_fusion.1
  736.8 3.3 collective-permute-start.11
  744.6 3.2 convolution_convert_fusion.2
  748.9 3.8 subtract_convert_fusion.1
  753.5 9.4 %convolution_convert_fusion = bf16[2048,1536]{1,0:T(8,128)(2,1)} fusion(bf16[1024,2048]{1,0:T(8,128)(2,1)S(1)} %copy-done.30, bf16[1024,512]{1,0:T(8,128)(2,1)S(1)} %copy-done.14, bf16[1024,512]{1,0:T(8,128)(2,1)S(1)} %get-tuple-element.168, bf16[1024,512]{1,0:T(8,128)(2,1)S(1)} %get-tuple-element.167), kind=kOutput, calls=%fused_computation | convolution fusion | flops 6455033856 | bytes 13631488 | tf_op jit(solution)/shard_map/dot_general | solution.py:32
  763.8 13.4 %concatenate.26 = bf16[2048,2176]{1,0:T(8,128)(2,1)} concatenate(bf16[2048,1536]{1,0:T(8,128)(2,1)} %convolution_convert_fusion, bf16[2048,512]{1,0:T(8,128)(2,1)S(1)} %copy-done.6, bf16[2048,4]{1,0:T(8,128)(2,1)} %copy.133, bf16[2048,124]{1,0:T(8,128)(2,1)} %broadcast_in_dim.66), dimensions={1} | concatenate | bytes 17825792 | tf_op jit(solution)/shard_map/concatenate | solution.py:872
  777.3 5.9 slice.125.refs_1_
  783.2 1.8 pad_maximum_fusion.2.refs_0_
  784.9 68.1 %input_line.1 = (f32[1024,512]{1,0:T(8,128)}, f32[1,512]{1,0:T(1,128)}) custom-call(bf16[1024,1536]{1,0:T(8,128)(2,1)} %pad_maximum_fusion.2.refs_0_, bf16[2048,1536]{1,0:T(8,128)(2,1)} %slice.125.refs_1_, bf16[1024,512]{1,0:T(8,128)(2,1)} %refs_2_.3, f32[1024,1]{1,0:T(8,128)} %get-tuple-element.75.refs_3_, bf16[1,512]{1,0:T(2,128)(2,1)} %reshape.128.refs_1_.refs_4_, ...), custom_call_target="tpu_custom_call" | custom-call | flops 1000000 | bytes 524288 | tf_op jit(solution)/shard_map/input_line/pallas_call | solution.py:257
  854.9 3.8 maximum_add_fusion
  858.8 1.6 convert_bitcast_fusion
  860.4 4.4 copy.135
  864.9 4.4 copy.136
  869.3 4.4 copy.137
  873.8 12.2 %psum.7 = f32[4,512]{1,0:T(4,128)S(1)} all-reduce(f32[4,512]{1,0:T(4,128)S(1)} %pad_maximum_fusion.7), channel_id=1, replica_groups=mesh['row'=8,'col'=4] {'row'}, use_global_device_ids=true, to_apply=%region_12.13 | all-reduce | flops 2048 | bytes 16384 | tf_op jit(solution)/shard_map/psum | solution.py:882
  886.0 2.8 convert_reduce_fusion
  889.4 2.8 fusion.1
  893.9 2.6 fusion.20
  (158 shorter events, 36.6 us)
Async XLA Ops:
  7.2 4.3 copy-start.7
  7.2 104.3 %all-gather.6.cloned.1.call-start = ((), (), s32[]{:S(2)}) async-start(), calls=%async_computation.3 | async-start | bytes 10027008 | tf_op jit(solution)/shard_map/all_gather | solution.py:788
  11.5 324.4 %all-gather.10.cloned.1.call-start = ((), (), s32[]{:S(2)}) async-start(), calls=%async_computation.8 | async-start | bytes 28311552 | tf_op jit(solution)/shard_map/all_gather | solution.py:791
  11.5 1.6 copy-start.8
  11.7 2.1 copy-start.9
  16.4 353.8 %all-gather.8.cloned.1.call-start = ((), (), s32[]{:S(2)}) async-start(), calls=%async_computation.7 | async-start | bytes 28311552 | tf_op jit(solution)/shard_map/all_gather | solution.py:792
  19.3 1.3 copy-start.21
  19.3 1.8 copy-start.23
  19.3 2.4 copy-start.29
  19.3 3.6 copy-start.28
  19.3 4.1 copy-start.20
  19.3 691.4 %reduce-scatter.4.cloned.1.call-start = ((), (), s32[]{:S(2)}) async-start(), calls=%async_computation.4 | async-start | bytes 28311552 | tf_op jit(solution)/shard_map/reduce_scatter | solution.py:833
  21.8 99.7 %copy-start.19 = (s32[1024]{0:T(1024)}, s32[1024]{0:T(1024)S(1)}, u32[]{:S(2)}) copy-start(s32[1024]{0:T(1024)S(1)} %fusion.11) | copy-start | bytes 12292
  23.8 310.7 %copy-start.12 = (pred[1024,16]{1,0:T(8,128)(4,1)}, pred[1024,16]{1,0:T(8,128)(4,1)S(1)}, u32[]{:S(2)}) copy-start(pred[1024,16]{1,0:T(8,128)(4,1)S(1)} %copy.122) | copy-start | bytes 49156
  121.5 9.3 %copy-start = (f32[1024,1536]{1,0:T(8,128)}, f32[1024,1536]{1,0:T(8,128)S(1)}, u32[]{:S(2)}) copy-start(f32[1024,1536]{1,0:T(8,128)S(1)} %fusion.14.q_ref.k_ref.v_ref) | copy-start | bytes 18874372
  121.9 13.9 %collective-permute-start.2 = (f32[2,1024]{1,0:T(2,128)S(1)}, f32[2,1024]{1,0:T(2,128)S(1)}, u32[]{:S(2)}, u32[]{:S(2)}) collective-permute-start(f32[2,1024]{1,0:T(2,128)S(1)} %pad_maximum_fusion.5), channel_id=1, source_target_pairs={{0,3},{1,0},{2,1},{3,2},{4,7},{5,4},{6,5},{7,6},{8,11},{9,8},{10,9... | collective-permute-start | bytes 24584 | tf_op jit(solution)/shard_map/ppermute | solution.py:58
  123.7 23.6 %collective-permute-start.1 = (f32[2,1024]{1,0:T(2,128)S(1)}, f32[2,1024]{1,0:T(2,128)S(1)}, u32[]{:S(2)}, u32[]{:S(2)}) collective-permute-start(f32[2,1024]{1,0:T(2,128)S(1)} %pad_maximum_fusion.5), channel_id=1, source_target_pairs={{0,2},{1,3},{2,0},{3,1},{4,6},{5,7},{6,4},{7,5},{8,10},{9,11},{10,... | collective-permute-start | bytes 24584 | tf_op jit(solution)/shard_map/ppermute | solution.py:58
  123.7 23.6 %collective-permute-start = (f32[2,1024]{1,0:T(2,128)S(1)}, f32[2,1024]{1,0:T(2,128)S(1)}, u32[]{:S(2)}, u32[]{:S(2)}) collective-permute-start(f32[2,1024]{1,0:T(2,128)S(1)} %pad_maximum_fusion.5), channel_id=1, source_target_pairs={{0,1},{1,2},{2,3},{3,0},{4,5},{5,6},{6,7},{7,4},{8,9},{9,10},{10,1... | collective-permute-start | bytes 24584 | tf_op jit(solution)/shard_map/ppermute | solution.py:58
  125.5 194.0 %collective-permute-start.3 = (bf16[4,2048]{0,1:T(8,128)(2,1)S(1)}, bf16[4,2048]{0,1:T(8,128)(2,1)}, u32[]{:S(2)}, u32[]{:S(2)}) collective-permute-start(bf16[4,2048]{0,1:T(8,128)(2,1)S(1)} %slice_bitcast_fusion.3), channel_id=1, source_target_pairs={{0,1},{1,2},{2,3},{3,0},{4,5},{5,6},{6,7},{7,4},{8,9},{9,10},{10,1... | collective-permute-start | bytes 49160 | tf_op jit(solution)/shard_map/ppermute | solution.py:68
  128.5 196.8 %collective-permute-start.4 = (bf16[4,2048]{0,1:T(8,128)(2,1)S(1)}, bf16[4,2048]{0,1:T(8,128)(2,1)}, u32[]{:S(2)}, u32[]{:S(2)}) collective-permute-start(bf16[4,2048]{0,1:T(8,128)(2,1)S(1)} %slice_bitcast_fusion.3), channel_id=1, source_target_pairs={{0,2},{1,3},{2,0},{3,1},{4,6},{5,7},{6,4},{7,5},{8,10},{9,11},{10,... | collective-permute-start | bytes 49160 | tf_op jit(solution)/shard_map/ppermute | solution.py:68
  135.8 193.4 %collective-permute-start.5 = (bf16[4,2048]{0,1:T(8,128)(2,1)S(1)}, bf16[4,2048]{0,1:T(8,128)(2,1)}, u32[]{:S(2)}, u32[]{:S(2)}) collective-permute-start(bf16[4,2048]{0,1:T(8,128)(2,1)S(1)} %slice_bitcast_fusion.3), channel_id=1, source_target_pairs={{0,3},{1,0},{2,1},{3,2},{4,7},{5,4},{6,5},{7,6},{8,11},{9,8},{10,9... | collective-permute-start | bytes 49160 | tf_op jit(solution)/shard_map/ppermute | solution.py:68
  319.5 86.7 %collective-permute-start.6 = (bf16[1024,512]{1,0:T(8,128)(2,1)}, bf16[1024,512]{1,0:T(8,128)(2,1)}, u32[]{:S(2)}, u32[]{:S(2)}) collective-permute-start(bf16[1024,512]{1,0:T(8,128)(2,1)} %broadcast_add_fusion), channel_id=1, source_target_pairs={{0,1},{1,2},{2,3},{3,0},{4,5},{5,6},{6,7},{7,4},{8,9},{9,10},{10,1... | collective-permute-start | bytes 3145736 | tf_op jit(solution)/shard_map/ppermute | solution.py:45
  319.5 86.7 %collective-permute-start.7 = (bf16[1024,512]{1,0:T(8,128)(2,1)}, bf16[1024,512]{1,0:T(8,128)(2,1)}, u32[]{:S(2)}, u32[]{:S(2)}) collective-permute-start(bf16[1024,512]{1,0:T(8,128)(2,1)} %broadcast_add_fusion), channel_id=1, source_target_pairs={{0,2},{1,3},{2,0},{3,1},{4,6},{5,7},{6,4},{7,5},{8,10},{9,11},{10,... | collective-permute-start | bytes 3145736 | tf_op jit(solution)/shard_map/ppermute | solution.py:45
  319.5 86.7 %collective-permute-start.8 = (bf16[1024,512]{1,0:T(8,128)(2,1)}, bf16[1024,512]{1,0:T(8,128)(2,1)}, u32[]{:S(2)}, u32[]{:S(2)}) collective-permute-start(bf16[1024,512]{1,0:T(8,128)(2,1)} %broadcast_add_fusion), channel_id=1, source_target_pairs={{0,3},{1,0},{2,1},{3,2},{4,7},{5,4},{6,5},{7,6},{8,11},{9,8},{10,9... | collective-permute-start | bytes 3145736 | tf_op jit(solution)/shard_map/ppermute | solution.py:45
  330.5 4.0 copy-start.16
  485.9 369.0 %reduce-scatter.8.cloned.1.call-start = ((), (), s32[]{:S(2)}) async-start(), calls=%async_computation.6 | async-start | bytes 28311552 | tf_op jit(solution)/shard_map/reduce_scatter | solution.py:834
  560.0 332.3 %reduce-scatter.6.cloned.1.call-start = ((), (), s32[]{:S(2)}) async-start(), calls=%async_computation.5 | async-start | bytes 10027008 | tf_op jit(solution)/shard_map/reduce_scatter | solution.py:875
  560.6 133.1 %copy-start.11 = (f32[1024,16]{1,0:T(8,128)S(1)}, f32[1024,16]{1,0:T(8,128)}, u32[]{:S(2)}) copy-start(f32[1024,16]{1,0:T(8,128)} %get-tuple-element.80) | copy-start | bytes 196612
  694.6 11.3 %copy-start.31 = (bf16[1024,2048]{1,0:T(8,128)(2,1)S(1)}, bf16[1024,2048]{1,0:T(8,128)(2,1)}, u32[]{:S(2)}) copy-start(bf16[1024,2048]{1,0:T(8,128)(2,1)} %get-tuple-element.70) | copy-start | bytes 12582916
  694.6 47.6 %collective-permute-start.14 = (f32[16,1024]{0,1:T(8,128)}, f32[16,1024]{0,1:T(8,128)}, u32[]{:S(2)}, u32[]{:S(2)}) collective-permute-start(f32[16,1024]{0,1:T(8,128)} %add_bitcast_fusion), channel_id=1, source_target_pairs={{0,3},{1,0},{2,1},{3,2},{4,7},{5,4},{6,5},{7,6},{8,11},{9,8},{10,9... | collective-permute-start | bytes 196616 | tf_op jit(solution)/shard_map/ppermute | solution.py:58
  698.8 44.1 %collective-permute-start.13 = (f32[16,1024]{0,1:T(8,128)}, f32[16,1024]{0,1:T(8,128)}, u32[]{:S(2)}, u32[]{:S(2)}) collective-permute-start(f32[16,1024]{0,1:T(8,128)} %add_bitcast_fusion), channel_id=1, source_target_pairs={{0,2},{1,3},{2,0},{3,1},{4,6},{5,7},{6,4},{7,5},{8,10},{9,11},{10,... | collective-permute-start | bytes 196616 | tf_op jit(solution)/shard_map/ppermute | solution.py:58
  698.8 44.1 %collective-permute-start.12 = (f32[16,1024]{0,1:T(8,128)}, f32[16,1024]{0,1:T(8,128)}, u32[]{:S(2)}, u32[]{:S(2)}) collective-permute-start(f32[16,1024]{0,1:T(8,128)} %add_bitcast_fusion), channel_id=1, source_target_pairs={{0,1},{1,2},{2,3},{3,0},{4,5},{5,6},{6,7},{7,4},{8,9},{9,10},{10,1... | collective-permute-start | bytes 196616 | tf_op jit(solution)/shard_map/ppermute | solution.py:58
  732.1 8.8 copy-start.2
  732.1 10.8 %copy-start.3 = (f32[1024,16]{1,0:T(8,128)S(1)}, f32[1024,16]{1,0:T(8,128)}, u32[]{:S(2)}) copy-start(f32[1024,16]{1,0:T(8,128)} %get-tuple-element.163.rest_0_) | copy-start | bytes 196612
  732.2 10.8 %copy-start.13 = (pred[1024,16]{1,0:T(8,128)(4,1)S(1)}, pred[1024,16]{1,0:T(8,128)(4,1)}, u32[]{:S(2)}) copy-start(pred[1024,16]{1,0:T(8,128)(4,1)} %copy-done.12) | copy-start | bytes 49156
  736.8 12.1 %collective-permute-start.11 = (f32[2,1024]{1,0:T(2,128)S(1)}, f32[2,1024]{1,0:T(2,128)S(1)}, u32[]{:S(2)}, u32[]{:S(2)}) collective-permute-start(f32[2,1024]{1,0:T(2,128)S(1)} %pad_maximum_fusion.6), channel_id=1, source_target_pairs={{0,3},{1,0},{2,1},{3,2},{4,7},{5,4},{6,5},{7,6},{8,11},{9,8},{10,9... | collective-permute-start | bytes 24584 | tf_op jit(solution)/shard_map/ppermute | solution.py:58
  740.1 8.8 collective-permute-start.10
  742.2 6.7 collective-permute-start.9
  748.9 3.8 copy-start.14
  748.9 4.5 copy-start.30
  752.7 10.2 %copy-start.4 = (bf16[1024,512]{1,0:T(8,128)(2,1)}, bf16[1024,512]{1,0:T(8,128)(2,1)S(1)}, u32[]{:S(2)}) copy-start(bf16[1024,512]{1,0:T(8,128)(2,1)S(1)} %get-tuple-element.168) | copy-start | bytes 3145732
  753.5 10.3 %copy-start.6 = (bf16[2048,512]{1,0:T(8,128)(2,1)S(1)}, bf16[2048,512]{1,0:T(8,128)(2,1)}, u32[]{:S(2)}) copy-start(bf16[2048,512]{1,0:T(8,128)(2,1)} %convolution_convert_fusion.1) | copy-start | bytes 6291460
  777.2 5.9 copy-start.5
  777.2 5.9 copy-start.15
  869.3 4.5 copy-start.25
  869.3 4.5 copy-start.26
  873.7 15.6 %copy-start.1 = (f32[1024,512]{1,0:T(8,128)S(1)}, f32[1024,512]{1,0:T(8,128)}, u32[]{:S(2)}) copy-start(f32[1024,512]{1,0:T(8,128)} %get-tuple-element.50.refs_1_) | copy-start | bytes 6291460
  892.2 4.3 copy-start.10
  (5 other events, 3.4 us)
Sparse Core Ops, SparseCore 0:
  11.6 59.1 all-gather.5
  73.3 125.1 all-gather.9
  200.4 125.1 all-gather.7
  486.0 155.4 reduce-scatter.3
  645.0 156.2 reduce-scatter.7
  804.8 74.0 reduce-scatter.5

commit v5 on v4

--- a/solution.py
+++ b/solution.py
@@ -372,7 +372,7 @@
         d_gain_ref[...] = jnp.zeros_like(d_gain_ref)
 
         def term(at, s):
-            return dot_nt(q_ref[at, :], w_ref[pl.ds(s * part, part), :])
+            return dot_nt(q_ref[at, :], w_ref[pl.ds(s * part, part), : q_ref.shape[1]])
 
         def first(at, total):
             grad_ref[at, :] = total
@@ -858,7 +858,7 @@
     ).astype(BF)
     qkv_grad = jnp.concatenate([query_raw_grad, key_raw_grad, value_grad], axis=1)
     d_tokens, d_attn_gain = input_line(
-        qkv_grad, full_qkv, tokens, inv_first, attn_gain, hidden_grad, width
+        qkv_grad, mats, tokens, inv_first, attn_gain, hidden_grad, width
     )
     d_qkv_w = dot_tn(normed_attn, qkv_grad)
 

time: 923 us -> 920 us (level)
  transfers between devices with their start and end apart: 21 -> 21, of which waited for: 1 -> 1; matrix products, arithmetic and copies ran while one was open for 15% -> 14% of each run, Pallas kernels for 68% -> 68%
where the time goes in v5:
time: 920 us; the launch traced here: 902 us
  Pallas kernels  695 us (76%)
  local copies, waits for them, and re-layouts  71.3 us (8%)
  matrix products  37.3 us (4%)
  other arithmetic  35.8 us (4%)
  starting transfers between devices  22.4 us (2%)
  between operations  17.6 us (2%)
  blocking collectives  12.8 us (1%)
  waiting for transfers between devices  9.52 us (1%)
    pallas_call x4, Pallas kernels, along_line(): pl.pallas_call(functools.partial(line_kernel, n, make, len(operands), len...  433 us
    pallas_call x2, Pallas kernels, moe_backward(): pl.pallas_call(functools.partial(backward_kernel, first, n_col, closing i...  145 us
    pallas_call x2, Pallas kernels, moe_forward(): pl.pallas_call(functools.partial(forward_kernel, first, n_col, before is...  70.4 us
    unnamed x72, local copies, waits for them, and re-layouts  21.9 us
    pallas_call x1, Pallas kernels, attend_back(): pl.pallas_call(functools.partial(attend_back_kernel, 1.0 / math.sqrt(HD),...  21.4 us
    dot_general x3, matrix products, dot_tn(): lax.dot_general(a, b, (((0,), (0,)), ((), ())), preferred_element_type=F32)  19 us
  transfers between devices with their start and end apart: 21, of which 1 were waited for; matrix products, arithmetic and copies ran while one was open for 14% of the time, Pallas kernels for 68%

profile of v5, /device:TPU:0, one launch (start us, length us, event | category | flops | bytes accessed | tf_op | source)
XLA Modules:
  0.0 902.1 jit_solution(2666451220537860537)
XLA Ops:
  8.2 3.2 concatenate.21
  14.4 2.0 pad_maximum_fusion.1
  17.1 2.1 pad_maximum_fusion
  23.8 84.4 %norm_line.1 = (bf16[1024,2048]{1,0:T(8,128)(2,1)}, f32[1024,1]{1,0:T(8,128)}) custom-call(bf16[1024,512]{1,0:T(8,128)(2,1)} %refs_2_.3, bf16[1,512]{1,0:T(2,128)(2,1)} %reshape.128.refs_1_.refs_4_), custom_call_target="tpu_custom_call" | custom-call | flops 1000000 | bytes 524288 | tf_op jit(solution)/shard_map/norm_line/pallas_call | solution.py:257
  108.2 2.0 fusion.12
  111.5 10.0 %fusion.q_ref.k_ref.v_ref = f32[1024,1536]{1,0:T(8,128)S(1)} fusion(bf16[1024,2048]{1,0:T(8,128)(2,1)} %get-tuple-element.48, bf16[2048,2176]{1,0:T(8,128)(2,1)} %all-gather.6.cloned.1.call-done.refs_1_), kind=kOutput, calls=%fused_computation.1 | convolution fusion | flops 6442450944 | bytes 16777216 | tf_op jit(solution)/shard_map/dot_general | solution.py:24
  121.9 1.8 collective-permute-start.2
  125.5 3.1 collective-permute-start.3
  130.9 1.9 bitcast_dynamic-update-slice_fusion
  132.7 3.0 slice.130.refs_1_
  135.8 2.2 collective-permute-start.5
  137.9 9.4 %collective-permute-done.1 = f32[2,1024]{1,0:T(2,128)S(1)} collective-permute-done((f32[2,1024]{1,0:T(2,128)S(1)}, f32[2,1024]{1,0:T(2,128)S(1)}, u32[]{:S(2)}, u32[]{:S(2)}) %collective-permute-start.1) | collective-permute-done | bytes 8224 | tf_op jit(solution)/shard_map/ppermute | solution.py:58
  150.0 16.7 %attend.1 = (bf16[1024,512]{1,0:T(8,128)(2,1)}, bf16[1024,512]{1,0:T(8,128)(2,1)}, bf16[1024,512]{1,0:T(8,128)(2,1)}, bf16[1024,512]{1,0:T(8,128)(2,1)}) custom-call(f32[1024,1536]{1,0:T(8,128)} %copy-done, f32[1024,1536]{1,0:T(8,128)} %copy-done, f32[1024,1536]{1,0:T(8,128)} %copy-done, f32[1024,1]{1,0:T(8,128)} %copy.116.iq_ref, f32[1024,1]{1,0:T(8,128)} %copy.117.ik_ref, ...), custom_call_target="tpu_custom_call" | custom-call | flops 2147483648 | bytes 10485760 | tf_op jit(solution)/shard_map/attend/pallas_call | solution.py:450
  166.7 148.7 %attn_line.1 = (bf16[1024,2048]{1,0:T(8,128)(2,1)}, f32[1024,512]{1,0:T(8,128)}, f32[1024,1]{1,0:T(8,128)}) custom-call(bf16[1024,512]{1,0:T(8,128)(2,1)} %get-tuple-element.49.refs_0_, bf16[2048,512]{1,0:T(8,128)(2,1)} %slice.130.refs_1_, bf16[1024,512]{1,0:T(8,128)(2,1)} %refs_2_.3, bf16[1,512]{1,0:T(2,128)(2,1)} %reshape.131.refs_3_), custom_call_target="tpu_custom_call" | custom-call | flops 1000000 | bytes 524288 | tf_op jit(solution)/shard_map/attn_line/pallas_call | solution.py:257
  317.2 2.3 broadcast_add_fusion
  319.5 3.8 collective-permute-start.8
  323.3 2.0 bitcast_dynamic-update-slice_fusion.2
  325.3 1.9 bitcast_dynamic-update-slice_fusion.1
  327.2 2.0 copy.119
  330.5 3.4 fusion.24
  335.8 34.4 %experts_forward.2 = (bf16[4,1024,512]{2,1,0:T(8,128)(2,1)}, bf16[8,1024,256]{2,1,0:T(8,128)(2,1)}, bf16[8,1024,256]{2,1,0:T(8,128)(2,1)}) custom-call(bf16[1024,2048]{1,0:T(8,128)(2,1)} %get-tuple-element.51.x_ref, f32[1024,16]{1,0:T(8,128)} %get-tuple-element.162.gates_ref, bf16[8,8,3,256,256]{4,3,2,1,0:T(8,128)(2,1)} %bitcast.138), custom_call_target="tpu_custom_call" | custom-call | flops 25769803776 | bytes 41943040 | tf_op jit(solution)/shard_map/experts_forward/pallas_call | solution.py:624
  370.2 36.0 %experts_forward.3 = (bf16[4,1024,512]{2,1,0:T(8,128)(2,1)}, bf16[8,1024,256]{2,1,0:T(8,128)(2,1)}, bf16[8,1024,256]{2,1,0:T(8,128)(2,1)}) custom-call(bf16[1024,2048]{1,0:T(8,128)(2,1)} %get-tuple-element.51.x_ref, f32[1024,16]{1,0:T(8,128)} %get-tuple-element.162.gates_ref, bf16[8,8,3,256,256]{4,3,2,1,0:T(8,128)(2,1)} %bitcast.140, ...), custom_call_target="tpu_custom_call" | custom-call | flops 25769803776 | bytes 41943040 | tf_op jit(solution)/shard_map/experts_forward/pallas_call | solution.py:624
  406.2 8.9 prepare.1
  415.1 70.8 %experts_backward.2 = (bf16[4,1024,512]{2,1,0:T(8,128)(2,1)}, bf16[8,8,3,256,256]{4,3,2,1,0:T(8,128)(2,1)}, f32[1024,16]{1,0:T(8,128)}, bf16[3,512,512]{2,1,0:T(8,128)(2,1)}) custom-call(bf16[2048,1024]{1,0:T(8,128)(2,1)} %get-tuple-element.55.xt_ref, bf16[1024,2048]{1,0:T(8,128)(2,1)} %get-tuple-element.56.y_ref, ...), custom_call_target="tpu_custom_call" | custom-call | flops 51539607552 | bytes 75497472 | tf_op jit(solution)/shard_map/experts_backward/pallas_call | solution.py:740
  486.0 73.9 %experts_backward.3 = (bf16[4,1024,512]{2,1,0:T(8,128)(2,1)}, bf16[8,8,3,256,256]{4,3,2,1,0:T(8,128)(2,1)}, f32[1024,16]{1,0:T(8,128)}, bf16[3,512,512]{2,1,0:T(8,128)(2,1)}) custom-call(bf16[2048,1024]{1,0:T(8,128)(2,1)} %get-tuple-element.55.xt_ref, bf16[1024,2048]{1,0:T(8,128)(2,1)} %get-tuple-element.56.y_ref, ...), custom_call_target="tpu_custom_call" | custom-call | flops 51539607552 | bytes 75497472 | tf_op jit(solution)/shard_map/experts_backward/pallas_call | solution.py:740
  560.6 131.3 %moe_line.1 = (bf16[1024,2048]{1,0:T(8,128)(2,1)}, f32[1024,512]{1,0:T(8,128)}, f32[1,512]{1,0:T(1,128)}) custom-call(bf16[4,1024,512]{2,1,0:T(8,128)(2,1)} %get-tuple-element.68.refs_0_, f32[1024,512]{1,0:T(8,128)} %get-tuple-element.50.refs_1_, f32[1024,1]{1,0:T(8,128)} %get-tuple-element.69.refs_2_, bf16[1,512]{1,0:T(2,128)(2,1)} %reshape.131.refs_3_, ...), custom_call_target="tpu_custom_call" | custom-call | flops 1000000 | bytes 524288 | tf_op jit(solution)/shard_map/moe_line/pallas_call | solution.py:257
  694.6 4.2 collective-permute-start.14
  699.6 6.3 convolution_convert_fusion.1
  705.9 4.9 convolution_convert_fusion.3.d_ref
  710.8 21.4 %attend_back.1 = (f32[1024,512]{1,0:T(8,128)}, f32[1024,512]{1,0:T(8,128)}, bf16[1024,512]{1,0:T(8,128)(2,1)}) custom-call(bf16[1024,512]{1,0:T(8,128)(2,1)} %get-tuple-element.65.q_ref, bf16[1024,512]{1,0:T(8,128)(2,1)} %get-tuple-element.66.k_ref, bf16[1024,512]{1,0:T(8,128)(2,1)} %get-tuple-element.67.v_ref, ...), custom_call_target="tpu_custom_call" | custom-call | flops 5368709120 | bytes 10485760 | tf_op jit(solution)/shard_map/attend_back/pallas_call | solution.py:506
  732.2 4.6 multiply_reduce_fusion.1
  736.8 3.3 collective-permute-start.11
  742.9 1.6 multiply_reduce_fusion.6
  744.6 3.2 convolution_convert_fusion.2
  748.9 3.8 subtract_convert_fusion.1
  753.5 9.4 %convolution_convert_fusion = bf16[2048,1536]{1,0:T(8,128)(2,1)} fusion(bf16[1024,2048]{1,0:T(8,128)(2,1)S(1)} %copy-done.30, bf16[1024,512]{1,0:T(8,128)(2,1)S(1)} %copy-done.14, bf16[1024,512]{1,0:T(8,128)(2,1)S(1)} %get-tuple-element.168, bf16[1024,512]{1,0:T(8,128)(2,1)S(1)} %get-tuple-element.167), kind=kOutput, calls=%fused_computation | convolution fusion | flops 6455033856 | bytes 13631488 | tf_op jit(solution)/shard_map/dot_general | solution.py:32
  763.8 13.4 %concatenate.26 = bf16[2048,2176]{1,0:T(8,128)(2,1)} concatenate(bf16[2048,1536]{1,0:T(8,128)(2,1)} %convolution_convert_fusion, bf16[2048,512]{1,0:T(8,128)(2,1)S(1)} %copy-done.6, bf16[2048,4]{1,0:T(8,128)(2,1)} %copy.133, bf16[2048,124]{1,0:T(8,128)(2,1)} %broadcast_in_dim.66), dimensions={1} | concatenate | bytes 17825792 | tf_op jit(solution)/shard_map/concatenate | solution.py:872
  778.8 1.8 pad_maximum_fusion.2.refs_0_
  780.5 69.1 %input_line.1 = (f32[1024,512]{1,0:T(8,128)}, f32[1,512]{1,0:T(1,128)}) custom-call(bf16[1024,1536]{1,0:T(8,128)(2,1)} %pad_maximum_fusion.2.refs_0_, bf16[2048,2176]{1,0:T(8,128)(2,1)} %all-gather.6.cloned.1.call-done.refs_1_, bf16[1024,512]{1,0:T(8,128)(2,1)} %refs_2_.3, f32[1024,1]{1,0:T(8,128)} %get-tuple-element.75.refs_3_, ...), custom_call_target="tpu_custom_call" | custom-call | flops 1000000 | bytes 524288 | tf_op jit(solution)/shard_map/input_line/pallas_call | solution.py:257
  851.5 3.9 maximum_add_fusion
  855.4 1.6 convert_bitcast_fusion
  857.0 4.4 copy.135
  861.5 4.4 copy.136
  865.9 4.4 copy.137
  870.4 12.8 %psum.7 = f32[4,512]{1,0:T(4,128)S(1)} all-reduce(f32[4,512]{1,0:T(4,128)S(1)} %pad_maximum_fusion.7), channel_id=1, replica_groups=mesh['row'=8,'col'=4] {'row'}, use_global_device_ids=true, to_apply=%region_12.13 | all-reduce | flops 2048 | bytes 16384 | tf_op jit(solution)/shard_map/psum | solution.py:882
  883.2 2.8 convert_reduce_fusion
  886.6 2.8 fusion.3
  891.2 2.6 fusion.20
  (157 shorter events, 36.5 us)
Async XLA Ops:
  7.2 4.3 copy-start.7
  7.2 104.3 %all-gather.6.cloned.1.call-start = ((), (), s32[]{:S(2)}) async-start(), calls=%async_computation.3 | async-start | bytes 10027008 | tf_op jit(solution)/shard_map/all_gather | solution.py:788
  11.5 324.4 %all-gather.10.cloned.1.call-start = ((), (), s32[]{:S(2)}) async-start(), calls=%async_computation.8 | async-start | bytes 28311552 | tf_op jit(solution)/shard_map/all_gather | solution.py:791
  11.5 1.6 copy-start.8
  11.7 2.1 copy-start.9
  16.4 353.8 %all-gather.8.cloned.1.call-start = ((), (), s32[]{:S(2)}) async-start(), calls=%async_computation.7 | async-start | bytes 28311552 | tf_op jit(solution)/shard_map/all_gather | solution.py:792
  19.3 1.3 copy-start.21
  19.3 1.8 copy-start.23
  19.3 2.4 copy-start.29
  19.3 3.6 copy-start.28
  19.3 4.1 copy-start.20
  19.3 691.4 %reduce-scatter.4.cloned.1.call-start = ((), (), s32[]{:S(2)}) async-start(), calls=%async_computation.4 | async-start | bytes 28311552 | tf_op jit(solution)/shard_map/reduce_scatter | solution.py:833
  21.8 99.7 %copy-start.19 = (s32[1024]{0:T(1024)}, s32[1024]{0:T(1024)S(1)}, u32[]{:S(2)}) copy-start(s32[1024]{0:T(1024)S(1)} %fusion.13) | copy-start | bytes 12292
  23.8 310.7 %copy-start.12 = (pred[1024,16]{1,0:T(8,128)(4,1)}, pred[1024,16]{1,0:T(8,128)(4,1)S(1)}, u32[]{:S(2)}) copy-start(pred[1024,16]{1,0:T(8,128)(4,1)S(1)} %copy.122) | copy-start | bytes 49156
  121.5 9.3 %copy-start = (f32[1024,1536]{1,0:T(8,128)}, f32[1024,1536]{1,0:T(8,128)S(1)}, u32[]{:S(2)}) copy-start(f32[1024,1536]{1,0:T(8,128)S(1)} %fusion.q_ref.k_ref.v_ref) | copy-start | bytes 18874372
  121.9 13.9 %collective-permute-start.2 = (f32[2,1024]{1,0:T(2,128)S(1)}, f32[2,1024]{1,0:T(2,128)S(1)}, u32[]{:S(2)}, u32[]{:S(2)}) collective-permute-start(f32[2,1024]{1,0:T(2,128)S(1)} %pad_maximum_fusion.5), channel_id=1, source_target_pairs={{0,3},{1,0},{2,1},{3,2},{4,7},{5,4},{6,5},{7,6},{8,11},{9,8},{10,9... | collective-permute-start | bytes 24584 | tf_op jit(solution)/shard_map/ppermute | solution.py:58
  123.7 23.6 %collective-permute-start.1 = (f32[2,1024]{1,0:T(2,128)S(1)}, f32[2,1024]{1,0:T(2,128)S(1)}, u32[]{:S(2)}, u32[]{:S(2)}) collective-permute-start(f32[2,1024]{1,0:T(2,128)S(1)} %pad_maximum_fusion.5), channel_id=1, source_target_pairs={{0,2},{1,3},{2,0},{3,1},{4,6},{5,7},{6,4},{7,5},{8,10},{9,11},{10,... | collective-permute-start | bytes 24584 | tf_op jit(solution)/shard_map/ppermute | solution.py:58
  123.7 23.6 %collective-permute-start = (f32[2,1024]{1,0:T(2,128)S(1)}, f32[2,1024]{1,0:T(2,128)S(1)}, u32[]{:S(2)}, u32[]{:S(2)}) collective-permute-start(f32[2,1024]{1,0:T(2,128)S(1)} %pad_maximum_fusion.5), channel_id=1, source_target_pairs={{0,1},{1,2},{2,3},{3,0},{4,5},{5,6},{6,7},{7,4},{8,9},{9,10},{10,1... | collective-permute-start | bytes 24584 | tf_op jit(solution)/shard_map/ppermute | solution.py:58
  125.5 194.0 %collective-permute-start.3 = (bf16[4,2048]{0,1:T(8,128)(2,1)S(1)}, bf16[4,2048]{0,1:T(8,128)(2,1)}, u32[]{:S(2)}, u32[]{:S(2)}) collective-permute-start(bf16[4,2048]{0,1:T(8,128)(2,1)S(1)} %slice_bitcast_fusion.3), channel_id=1, source_target_pairs={{0,1},{1,2},{2,3},{3,0},{4,5},{5,6},{6,7},{7,4},{8,9},{9,10},{10,1... | collective-permute-start | bytes 49160 | tf_op jit(solution)/shard_map/ppermute | solution.py:68
  128.5 196.8 %collective-permute-start.4 = (bf16[4,2048]{0,1:T(8,128)(2,1)S(1)}, bf16[4,2048]{0,1:T(8,128)(2,1)}, u32[]{:S(2)}, u32[]{:S(2)}) collective-permute-start(bf16[4,2048]{0,1:T(8,128)(2,1)S(1)} %slice_bitcast_fusion.3), channel_id=1, source_target_pairs={{0,2},{1,3},{2,0},{3,1},{4,6},{5,7},{6,4},{7,5},{8,10},{9,11},{10,... | collective-permute-start | bytes 49160 | tf_op jit(solution)/shard_map/ppermute | solution.py:68
  135.8 193.4 %collective-permute-start.5 = (bf16[4,2048]{0,1:T(8,128)(2,1)S(1)}, bf16[4,2048]{0,1:T(8,128)(2,1)}, u32[]{:S(2)}, u32[]{:S(2)}) collective-permute-start(bf16[4,2048]{0,1:T(8,128)(2,1)S(1)} %slice_bitcast_fusion.3), channel_id=1, source_target_pairs={{0,3},{1,0},{2,1},{3,2},{4,7},{5,4},{6,5},{7,6},{8,11},{9,8},{10,9... | collective-permute-start | bytes 49160 | tf_op jit(solution)/shard_map/ppermute | solution.py:68
  319.5 86.7 %collective-permute-start.6 = (bf16[1024,512]{1,0:T(8,128)(2,1)}, bf16[1024,512]{1,0:T(8,128)(2,1)}, u32[]{:S(2)}, u32[]{:S(2)}) collective-permute-start(bf16[1024,512]{1,0:T(8,128)(2,1)} %broadcast_add_fusion), channel_id=1, source_target_pairs={{0,1},{1,2},{2,3},{3,0},{4,5},{5,6},{6,7},{7,4},{8,9},{9,10},{10,1... | collective-permute-start | bytes 3145736 | tf_op jit(solution)/shard_map/ppermute | solution.py:45
  319.5 86.7 %collective-permute-start.7 = (bf16[1024,512]{1,0:T(8,128)(2,1)}, bf16[1024,512]{1,0:T(8,128)(2,1)}, u32[]{:S(2)}, u32[]{:S(2)}) collective-permute-start(bf16[1024,512]{1,0:T(8,128)(2,1)} %broadcast_add_fusion), channel_id=1, source_target_pairs={{0,2},{1,3},{2,0},{3,1},{4,6},{5,7},{6,4},{7,5},{8,10},{9,11},{10,... | collective-permute-start | bytes 3145736 | tf_op jit(solution)/shard_map/ppermute | solution.py:45
  319.5 86.7 %collective-permute-start.8 = (bf16[1024,512]{1,0:T(8,128)(2,1)}, bf16[1024,512]{1,0:T(8,128)(2,1)}, u32[]{:S(2)}, u32[]{:S(2)}) collective-permute-start(bf16[1024,512]{1,0:T(8,128)(2,1)} %broadcast_add_fusion), channel_id=1, source_target_pairs={{0,3},{1,0},{2,1},{3,2},{4,7},{5,4},{6,5},{7,6},{8,11},{9,8},{10,9... | collective-permute-start | bytes 3145736 | tf_op jit(solution)/shard_map/ppermute | solution.py:45
  330.5 4.0 copy-start.16
  485.9 365.6 %reduce-scatter.8.cloned.1.call-start = ((), (), s32[]{:S(2)}) async-start(), calls=%async_computation.6 | async-start | bytes 28311552 | tf_op jit(solution)/shard_map/reduce_scatter | solution.py:834
  560.0 329.5 %reduce-scatter.6.cloned.1.call-start = ((), (), s32[]{:S(2)}) async-start(), calls=%async_computation.5 | async-start | bytes 10027008 | tf_op jit(solution)/shard_map/reduce_scatter | solution.py:875
  560.6 133.1 %copy-start.11 = (f32[1024,16]{1,0:T(8,128)S(1)}, f32[1024,16]{1,0:T(8,128)}, u32[]{:S(2)}) copy-start(f32[1024,16]{1,0:T(8,128)} %get-tuple-element.80) | copy-start | bytes 196612
  694.6 11.3 %copy-start.31 = (bf16[1024,2048]{1,0:T(8,128)(2,1)S(1)}, bf16[1024,2048]{1,0:T(8,128)(2,1)}, u32[]{:S(2)}) copy-start(bf16[1024,2048]{1,0:T(8,128)(2,1)} %get-tuple-element.70) | copy-start | bytes 12582916
  694.6 47.6 %collective-permute-start.14 = (f32[16,1024]{0,1:T(8,128)}, f32[16,1024]{0,1:T(8,128)}, u32[]{:S(2)}, u32[]{:S(2)}) collective-permute-start(f32[16,1024]{0,1:T(8,128)} %add_bitcast_fusion), channel_id=1, source_target_pairs={{0,3},{1,0},{2,1},{3,2},{4,7},{5,4},{6,5},{7,6},{8,11},{9,8},{10,9... | collective-permute-start | bytes 196616 | tf_op jit(solution)/shard_map/ppermute | solution.py:58
  698.8 44.1 %collective-permute-start.13 = (f32[16,1024]{0,1:T(8,128)}, f32[16,1024]{0,1:T(8,128)}, u32[]{:S(2)}, u32[]{:S(2)}) collective-permute-start(f32[16,1024]{0,1:T(8,128)} %add_bitcast_fusion), channel_id=1, source_target_pairs={{0,2},{1,3},{2,0},{3,1},{4,6},{5,7},{6,4},{7,5},{8,10},{9,11},{10,... | collective-permute-start | bytes 196616 | tf_op jit(solution)/shard_map/ppermute | solution.py:58
  698.8 44.1 %collective-permute-start.12 = (f32[16,1024]{0,1:T(8,128)}, f32[16,1024]{0,1:T(8,128)}, u32[]{:S(2)}, u32[]{:S(2)}) collective-permute-start(f32[16,1024]{0,1:T(8,128)} %add_bitcast_fusion), channel_id=1, source_target_pairs={{0,1},{1,2},{2,3},{3,0},{4,5},{5,6},{6,7},{7,4},{8,9},{9,10},{10,1... | collective-permute-start | bytes 196616 | tf_op jit(solution)/shard_map/ppermute | solution.py:58
  732.1 8.8 copy-start.2
  732.1 10.8 %copy-start.3 = (f32[1024,16]{1,0:T(8,128)S(1)}, f32[1024,16]{1,0:T(8,128)}, u32[]{:S(2)}) copy-start(f32[1024,16]{1,0:T(8,128)} %get-tuple-element.163.rest_0_) | copy-start | bytes 196612
  732.2 10.8 %copy-start.13 = (pred[1024,16]{1,0:T(8,128)(4,1)S(1)}, pred[1024,16]{1,0:T(8,128)(4,1)}, u32[]{:S(2)}) copy-start(pred[1024,16]{1,0:T(8,128)(4,1)} %copy-done.12) | copy-start | bytes 49156
  736.8 12.1 %collective-permute-start.11 = (f32[2,1024]{1,0:T(2,128)S(1)}, f32[2,1024]{1,0:T(2,128)S(1)}, u32[]{:S(2)}, u32[]{:S(2)}) collective-permute-start(f32[2,1024]{1,0:T(2,128)S(1)} %pad_maximum_fusion.6), channel_id=1, source_target_pairs={{0,3},{1,0},{2,1},{3,2},{4,7},{5,4},{6,5},{7,6},{8,11},{9,8},{10,9... | collective-permute-start | bytes 24584 | tf_op jit(solution)/shard_map/ppermute | solution.py:58
  740.1 8.8 collective-permute-start.10
  742.2 6.7 collective-permute-start.9
  748.9 3.8 copy-start.14
  748.9 4.5 copy-start.30
  752.7 10.2 %copy-start.4 = (bf16[1024,512]{1,0:T(8,128)(2,1)}, bf16[1024,512]{1,0:T(8,128)(2,1)S(1)}, u32[]{:S(2)}) copy-start(bf16[1024,512]{1,0:T(8,128)(2,1)S(1)} %get-tuple-element.168) | copy-start | bytes 3145732
  753.5 10.3 %copy-start.6 = (bf16[2048,512]{1,0:T(8,128)(2,1)S(1)}, bf16[2048,512]{1,0:T(8,128)(2,1)}, u32[]{:S(2)}) copy-start(bf16[2048,512]{1,0:T(8,128)(2,1)} %convolution_convert_fusion.1) | copy-start | bytes 6291460
  777.2 1.2 copy-start.5
  777.2 1.5 copy-start.15
  865.9 4.5 copy-start.25
  865.9 4.5 copy-start.26
  870.4 16.3 %copy-start.1 = (f32[1024,512]{1,0:T(8,128)S(1)}, f32[1024,512]{1,0:T(8,128)}, u32[]{:S(2)}) copy-start(f32[1024,512]{1,0:T(8,128)} %get-tuple-element.50.refs_1_) | copy-start | bytes 6291460
  889.5 4.3 copy-start.10
  (5 other events, 3.4 us)
Sparse Core Ops, SparseCore 0:
  11.6 59.1 all-gather.5
  73.3 125.1 all-gather.9
  200.4 125.1 all-gather.7
  486.0 155.4 reduce-scatter.3
  645.0 156.2 reduce-scatter.7
  804.8 74.3 reduce-scatter.5
